TPU v7x, 32 devices: a whole 2x2x4 slice. The times are simulated.
32 devices in a mesh: dp: 4 (over z), fsdp: 8 (over y, x, core).
Axes of the slice: x: 2, y: 2, z: 4, core: 2. Of those that a mesh axis runs over, the one named last changes fastest.
Arguments:
- tokens: bfloat16 [2, 32, 1024, 1024], P(None, 'fsdp', 'dp'), may hold values from -6 to 6
- cotangent: bfloat16 [2, 32, 1024, 1024], P(None, 'fsdp', 'dp'), may hold values from -6 to 6
- teacher: bfloat16 [2, 32, 1024, 1024], P(None, ('dp', 'fsdp')), may hold values from -6 to 6
- lengths: int32 [2, 32], replicated, may hold values from 1 to 1024, 24576 in all within a row
- dealing: int32 [2, 32], replicated, may hold values from 0 to 3, as said below
- loss_mask: int32 [2, 32, 1024], P(None, ('dp', 'fsdp')), may hold values 0 or 1
- norm_gain: bfloat16 [1024], P(('dp', 'fsdp')), may hold values from 0.5 to 1.5
- norm_bias: bfloat16 [1024], P(('dp', 'fsdp')), may hold values from -2 to 2
- gate_weight: bfloat16 [1024, 3072], P(('dp', 'fsdp')), may hold values from -0.1875 to 0.1875
- reduce_weight: bfloat16 [1024, 512], P(('dp', 'fsdp')), may hold values from -0.1875 to 0.1875
- state_weight: float32 [2, 512, 512], P(None, ('dp', 'fsdp')), may hold values from -0.00390625 to 0.00390625
- decay_rate: float32 [512, 512], P(('dp', 'fsdp')), may hold values from -0.5 to -0.01
- frequency: float32 [512, 512], P(('dp', 'fsdp')), may hold values from -6 to 6
- log_step: float32 [512], P(('dp', 'fsdp')), may hold values from -5.3 to -0.7
- expand_weight: bfloat16 [512, 3072], P(('dp', 'fsdp')), may hold values from -0.25 to 0.25
- out_weight: bfloat16 [3072, 1024], P(('dp', 'fsdp')), may hold values from -0.21875 to 0.21875
Outputs:
- output: bfloat16 [2, 32, 1024, 1024], P(None, 'fsdp', 'dp')
- loss: float32 [], replicated
- tokens_grad: bfloat16 [2, 32, 1024, 1024], P(None, 'fsdp', 'dp')
- gain_grad: float32 [1024], P(('dp', 'fsdp'))
- bias_grad: float32 [1024], P(('dp', 'fsdp'))
- gate_weight_grad: float32 [1024, 3072], P(('dp', 'fsdp'))
- reduce_weight_grad: float32 [1024, 512], P(('dp', 'fsdp'))
- state_weight_grad: float32 [2, 512, 512], P(None, ('dp', 'fsdp'))
- decay_rate_grad: float32 [512, 512], P(('dp', 'fsdp'))
- frequency_grad: float32 [512, 512], P(('dp', 'fsdp'))
- log_step_grad: float32 [512], P(('dp', 'fsdp'))
- expand_weight_grad: float32 [512, 3072], P(('dp', 'fsdp'))
- out_weight_grad: float32 [3072, 1024], P(('dp', 'fsdp'))
Inputs may be any that keep to these rules, and one draw needn't show every extreme that they name: `dealing`: in each micro-batch, the entries of sequences g * 4 to g * 4 + 3 are a permutation of 0 to 3. Each micro-batch's lengths sum to 24576, and the longest is 1024.
All inputs are finite; a program needn't handle non-finite values. No bound on the sum of `loss_mask` on one device may be relied on, other than what follows from the above.
Results may differ from a plain program's by a relative error of at most 0.0063.
Values may be sent and summed in bfloat16 or wider, within the bound.
A program may use at most 320 MiB of HBM per device.

v0:
```python
import jax
import jax.numpy as jnp
from jax import lax
from jax.sharding import PartitionSpec as P

epsilon = 1e-05
highest = lax.Precision.HIGHEST


def matmul(left, right):
    return jnp.dot(left, right, preferred_element_type=jnp.float32)


def rows_inner(left, right):
    return lax.dot_general(
        left, right, (((0,), (0,)), ((), ())), preferred_element_type=jnp.float32
    )


def cols_inner(left, right):
    return lax.dot_general(
        left, right, (((1,), (1,)), ((), ())), preferred_element_type=jnp.float32
    )


def gelu_slope(values):
    return (
        0.5 * (1.0 + lax.erf(values * 0.7071067811865476))
        + values * jnp.exp(-0.5 * values * values) * 0.3989422804014327
    )


def kernel_rows(weight_pair, decay, frequency, log_step, positions):
    step_size = jnp.exp(log_step)
    damping = jnp.exp((step_size[:, None] * decay)[:, :, None] * positions)
    angle = (step_size[:, None] * frequency)[:, :, None] * positions
    waves = weight_pair[0][:, :, None] * jnp.cos(angle) - weight_pair[1][:, :, None] * jnp.sin(
        angle
    )
    return jnp.sum(damping * waves, axis=1)


def fourier_table(length):
    rows_index = jnp.arange(length, dtype=jnp.int32)[:, None]
    cols_index = jnp.arange(length, dtype=jnp.int32)[None, :]
    angle = (rows_index * cols_index % (2 * length)).astype(jnp.float32) * (jnp.pi / length)
    alternate = jnp.where(rows_index % 2 == 0, 1.0, -1.0).astype(jnp.float32)
    sines = jnp.where(cols_index == 0, alternate, -jnp.sin(angle))
    table = jnp.concatenate([jnp.cos(angle), sines], axis=1)
    column = jnp.arange(2 * length, dtype=jnp.int32)
    scaling = jnp.where(column % length == 0, 1.0, 2.0).astype(jnp.float32) / (2.0 * length)
    return (table, scaling)


def transform(table, values):
    return jnp.einsum("tk,th->kh", table, values, precision=highest)


def packed_product(first, second, length):
    first_real, first_imag = (first[:length], first[length:])
    second_real, second_imag = (second[:length], second[length:])
    edge = (jnp.arange(length) == 0)[:, None]
    crossed = first_imag * second_imag
    real_part = first_real * second_real - jnp.where(edge, 0.0, crossed)
    imag_part = jnp.where(edge, crossed, first_real * second_imag + first_imag * second_real)
    return jnp.concatenate([real_part, imag_part], axis=0)


def shards(
    tokens,
    cotangent,
    teacher,
    lengths,
    dealing,
    loss_mask,
    norm_gain,
    norm_bias,
    gate_weight,
    reduce_weight,
    state_weight,
    decay_rate,
    frequency,
    log_step,
    expand_weight,
    out_weight,
):
    dp_count = lax.axis_size("dp")
    group_index = lax.axis_index("fsdp")
    dp_place = lax.axis_index("dp")
    micro_count = tokens.shape[0]
    seq_length = tokens.shape[2] * dp_count
    model_width = tokens.shape[3]
    gate_width = gate_weight.shape[1]
    reduced_width = reduce_weight.shape[1]
    table, scaling = fourier_table(seq_length)
    positions = jnp.arange(seq_length, dtype=jnp.int32)
    float_positions = positions.astype(jnp.float32)
    slot_range = jnp.arange(dp_count, dtype=jnp.int32)
    local_ids = group_index * dp_count + slot_range
    targets = jnp.take(dealing, local_ids, axis=1)
    matches = targets[:, None, :] == slot_range[None, :, None]
    sources = jnp.sum(jnp.where(matches, slot_range[None, None, :], 0), axis=2)
    resident = group_index * dp_count + jnp.take(sources, dp_place, axis=1)
    seq_lengths = jnp.take_along_axis(lengths, resident[:, None], axis=1)
    valid = (positions[None, :] < seq_lengths).astype(jnp.float32)
    keep = loss_mask[:, 0, :].astype(jnp.float32) * valid
    count = lax.psum(jnp.sum(keep), ("dp", "fsdp"))

    def build(weight_pair, decay, freq_values, step_logs):
        return kernel_rows(weight_pair, decay, freq_values, step_logs, float_positions).T

    own_kernel, kernel_back = jax.vjp(build, state_weight, decay_rate, frequency, log_step)
    kernel_spec = lax.all_gather(transform(table, own_kernel), ("dp", "fsdp"), axis=1, tiled=True)
    kernel_total = jnp.zeros((2 * seq_length, reduced_width), jnp.float32)
    gain_total = jnp.zeros((model_width,), jnp.float32)
    bias_total = jnp.zeros((model_width,), jnp.float32)
    gate_total = jnp.zeros((model_width, gate_width), jnp.float32)
    reduce_total = jnp.zeros((model_width, reduced_width), jnp.float32)
    expand_total = jnp.zeros((reduced_width, gate_width), jnp.float32)
    output_total = jnp.zeros((gate_width, model_width), jnp.float32)
    error_total = jnp.zeros((), jnp.float32)
    outputs = []
    returned = []
    for micro in range(micro_count):
        gathered = (
            lax.all_gather(norm_gain, ("dp", "fsdp"), axis=0, tiled=True),
            lax.all_gather(norm_bias, ("dp", "fsdp"), axis=0, tiled=True),
            lax.all_gather(gate_weight, ("dp", "fsdp"), axis=0, tiled=True),
            lax.all_gather(reduce_weight, ("dp", "fsdp"), axis=0, tiled=True),
            lax.all_gather(expand_weight, ("dp", "fsdp"), axis=0, tiled=True),
            lax.all_gather(out_weight, ("dp", "fsdp"), axis=0, tiled=True),
        )
        gain_full, bias_full, w_gate, w_reduce, w_expand, w_out = gathered
        gain_values = gain_full.astype(jnp.float32)
        bias_values = bias_full.astype(jnp.float32)
        order_now = sources[micro]
        sorted_rows = jnp.take(tokens[micro], order_now, axis=0)
        sorted_cot = jnp.take(cotangent[micro], order_now, axis=0)
        seq_rows, seq_cot = (
            lax.all_to_all(sorted_rows, "dp", split_axis=0, concat_axis=1, tiled=True),
            lax.all_to_all(sorted_cot, "dp", split_axis=0, concat_axis=1, tiled=True),
        )
        inputs = seq_rows[0].astype(jnp.float32)
        centre = jnp.mean(inputs, axis=1, keepdims=True)
        centred = inputs - centre
        variance = jnp.mean(centred * centred, axis=1, keepdims=True)
        inverse_std = lax.rsqrt(variance + epsilon)
        unit = centred * inverse_std
        normed = (unit * gain_values + bias_values).astype(jnp.bfloat16)
        pre_gate = matmul(normed, w_gate)
        gate = jax.nn.gelu(pre_gate, approximate=False)
        pre_reduced = matmul(normed, w_reduce)
        reduced = jax.nn.gelu(pre_reduced, approximate=False)
        reduced_spec = transform(table, reduced)
        mixed = jnp.dot(
            table,
            scaling[:, None] * packed_product(reduced_spec, kernel_spec, seq_length),
            precision=highest,
        )
        state_out = mixed.astype(jnp.bfloat16)
        expanded = matmul(state_out, w_expand)
        product = (expanded * gate).astype(jnp.bfloat16)
        branch = matmul(product, w_out)
        valid_now = valid[micro][:, None]
        keep_now = keep[micro][:, None]
        full = inputs + valid_now * branch
        errors = full - teacher[micro, 0].astype(jnp.float32)
        error_total = error_total + jnp.sum(keep_now * errors * errors)
        grad_full = seq_cot[0].astype(jnp.float32) + keep_now * errors * (
            2.0 / (model_width * count)
        )
        grad_branch = (valid_now * grad_full).astype(jnp.bfloat16)
        output_total = output_total + rows_inner(product, grad_branch)
        grad_product = cols_inner(grad_branch, w_out)
        grad_expanded = (grad_product * gate).astype(jnp.bfloat16)
        grad_gate = grad_product * expanded
        expand_total = expand_total + rows_inner(state_out, grad_expanded)
        grad_mixed = cols_inner(grad_expanded, w_expand)
        reversed_spec = transform(table, jnp.flip(grad_mixed, 0))
        grad_reduced = jnp.flip(
            jnp.dot(
                table,
                scaling[:, None] * packed_product(kernel_spec, reversed_spec, seq_length),
                precision=highest,
            ),
            0,
        )
        cross_spec = scaling[:, None] * packed_product(reduced_spec, reversed_spec, seq_length)
        kernel_total = kernel_total + cross_spec
        grad_pre_reduced = (grad_reduced * gelu_slope(pre_reduced)).astype(jnp.bfloat16)
        grad_pre_gate = (grad_gate * gelu_slope(pre_gate)).astype(jnp.bfloat16)
        gate_total = gate_total + rows_inner(normed, grad_pre_gate)
        reduce_total = reduce_total + rows_inner(normed, grad_pre_reduced)
        grad_normed = cols_inner(grad_pre_gate, w_gate) + cols_inner(grad_pre_reduced, w_reduce)
        gain_total = gain_total + jnp.sum(grad_normed * unit, axis=0)
        bias_total = bias_total + jnp.sum(grad_normed, axis=0)
        grad_unit = grad_normed * gain_values
        grad_inputs = grad_full + inverse_std * (
            grad_unit
            - jnp.mean(grad_unit, axis=1, keepdims=True)
            - unit * jnp.mean(grad_unit * unit, axis=1, keepdims=True)
        )
        back_rows, back_grads = (
            lax.all_to_all(
                full.astype(jnp.bfloat16)[None], "dp", split_axis=1, concat_axis=0, tiled=True
            ),
            lax.all_to_all(
                grad_inputs.astype(jnp.bfloat16)[None],
                "dp",
                split_axis=1,
                concat_axis=0,
                tiled=True,
            ),
        )
        outputs.append(jnp.take(back_rows, targets[micro], axis=0))
        returned.append(jnp.take(back_grads, targets[micro], axis=0))
    summed = (
        lax.psum_scatter(gain_total, ("dp", "fsdp"), scatter_dimension=0, tiled=True),
        lax.psum_scatter(bias_total, ("dp", "fsdp"), scatter_dimension=0, tiled=True),
        lax.psum_scatter(gate_total, ("dp", "fsdp"), scatter_dimension=0, tiled=True),
        lax.psum_scatter(reduce_total, ("dp", "fsdp"), scatter_dimension=0, tiled=True),
        lax.psum_scatter(expand_total, ("dp", "fsdp"), scatter_dimension=0, tiled=True),
        lax.psum_scatter(output_total, ("dp", "fsdp"), scatter_dimension=0, tiled=True),
        lax.psum_scatter(kernel_total, ("dp", "fsdp"), scatter_dimension=1, tiled=True),
    )
    kernel_grad = jnp.flip(jnp.dot(table, summed[6], precision=highest), 0)
    pair_grad, decay_grad, frequency_grad, step_grad = kernel_back(kernel_grad)
    error_sum = lax.psum(error_total, ("dp", "fsdp"))
    loss_value = error_sum / (model_width * count)
    return (
        jnp.stack(outputs),
        loss_value,
        jnp.stack(returned),
        summed[0],
        summed[1],
        summed[2],
        summed[3],
        pair_grad,
        decay_grad,
        frequency_grad,
        step_grad,
        summed[4],
        summed[5],
    )


def solution(mesh):
    in_specs = (
        P(None, "fsdp", "dp", None),
        P(None, "fsdp", "dp", None),
        P(None, ("dp", "fsdp"), None, None),
        P(),
        P(),
        P(None, ("dp", "fsdp"), None),
        P(("dp", "fsdp")),
        P(("dp", "fsdp")),
        P(("dp", "fsdp"), None),
        P(("dp", "fsdp"), None),
        P(None, ("dp", "fsdp"), None),
        P(("dp", "fsdp"), None),
        P(("dp", "fsdp"), None),
        P(("dp", "fsdp")),
        P(("dp", "fsdp"), None),
        P(("dp", "fsdp"), None),
    )
    out_specs = (
        P(None, "fsdp", "dp", None),
        P(),
        P(None, "fsdp", "dp", None),
        P(("dp", "fsdp")),
        P(("dp", "fsdp")),
        P(("dp", "fsdp"), None),
        P(("dp", "fsdp"), None),
        P(None, ("dp", "fsdp"), None),
        P(("dp", "fsdp"), None),
        P(("dp", "fsdp"), None),
        P(("dp", "fsdp")),
        P(("dp", "fsdp"), None),
        P(("dp", "fsdp"), None),
    )
    return jax.shard_map(shards, mesh=mesh, in_specs=in_specs, out_specs=out_specs, check_vma=False)
```

profile of v0, /device:TPU:0, one launch (start us, length us, event | category | flops | bytes accessed | tf_op | source)
XLA Modules:
  0.0 1629.8 jit_solution(2541750443456468080)
XLA Ops:
  8.1 15.3 fusion.229
  23.5 16.2 negate_select_fusion.2
  40.5 128.9 %fusion.13 = f32[16,1024]{1,0:T(8,128)S(1)} fusion(f32[16,512]{1,0:T(8,128)S(1)} %get-tuple-element.90, f32[16,512]{1,0:T(8,128)S(1)} %get-tuple-element.116, f32[16,512]{1,0:T(8,128)S(1)} %get-tuple-element.89, f32[1024]{0:T(1024)S(1)} %iota_convert_fusion, f32[16,512]{1,0:T(8,128)S(1)} %get-tuple-element.115), kind=kLoop, calls=%fused_computation.25 | loop fusion | flops 58703872 | bytes 200704 | tf_op jit(solution)/shard_map/jvp()/reduce_sum | solution.py:40
  214.7 53.0 %all-to-all-done.2 = bf16[4,256,1024]{2,1,0:T(8,128)(2,1)S(1)} async-done(((bf16[4,256,1024]{2,1,0:T(8,128)(2,1)}), bf16[4,256,1024]{2,1,0:T(8,128)(2,1)S(1)}, u32[]{:S(2)}, u32[]{:S(2)}) %all-to-all-start.2) | async-done | bytes 2097184 | tf_op jit(solution)/shard_map/all_to_all | solution.py:140
  274.6 79.8 %psum.15 = f32[]{:T(128)} all-reduce(f32[]{:T(128)} %get-tuple-element.46), channel_id=1, replica_groups=mesh['dp'=4,'fsdp'=8] {'dp','fsdp'}, use_global_device_ids=true, to_apply=%region_10.12 | all-reduce | flops 1 | bytes 8 | tf_op jit(solution)/shard_map/psum | solution.py:107
  354.8 38.5 %all-reduce.7 = (bf16[1024]{0:T(1024)(128)(2,1)S(1)}, bf16[1024]{0:T(1024)(128)(2,1)S(1)}) all-reduce(bf16[1024]{0:T(1024)(128)(2,1)S(1)} %dynamic-update-slice.2, bf16[1024]{0:T(1024)(128)(2,1)S(1)} %dynamic-update-slice.1), channel_id=1, replica_groups=mesh['dp'=4,'fsdp'=8] {'dp','fsdp'}, use_global_device_ids=true, to_apply=%add.3 | all-reduce | flops 2048 | bytes 8192
  414.6 24.9 %fusion.105 = f32[2048,512]{1,0:T(8,128)} fusion(f32[1024,512]{1,0:T(8,128)S(1)} %fusion.388, f32[1024,1024]{1,0:T(8,128)S(1)} %copy-done.10, f32[1024,1024]{1,0:T(8,128)S(1)} %copy-done.5), kind=kOutput, calls=%fused_computation.181 | convolution fusion | flops 12920553472 | bytes 14680064 | tf_op jit(solution)/shard_map/tk,th->kh/dot_general | solution.py:56
  442.0 25.3 %fusion.109 = f32[2048,512]{1,0:T(8,128)} fusion(f32[1024,512]{1,0:T(8,128)S(1)} %fusion.390, f32[1024,1024]{1,0:T(8,128)S(1)} %copy-done.10, f32[1024,1024]{1,0:T(8,128)S(1)} %copy-done.5), kind=kOutput, calls=%fused_computation.184 | convolution fusion | flops 12920553472 | bytes 14680064 | tf_op jit(solution)/shard_map/tk,th->kh/dot_general | solution.py:56
  483.1 13.3 fusion.239
  509.3 33.3 %multiply_convert_fusion.3 = (bf16[1024,3072]{1,0:T(8,128)(2,1)}, f32[1024,3072]{1,0:T(8,128)}, f32[1024,3072]{1,0:T(8,128)}) fusion(f32[1024,3072]{1,0:T(8,128)} %fusion.389, bf16[1024,512]{1,0:T(8,128)(2,1)S(1)} %fusion.239, bf16[512,3072]{1,0:T(8,128)(2,1)} %all-gather.10.cloned.1.call-done), kind=kOutput, calls=%fused_computation.69 | convolution fusion | flops 3428843520 | bytes 48234496 | tf_op jit(solution)/shard_map/dot_general | solution.py:11
  567.7 22.6 %multiply_convert_fusion.1 = (bf16[1024,3072]{1,0:T(8,128)(2,1)S(1)}, bf16[1024,3072]{1,0:T(8,128)(2,1)}) fusion(f32[1024,3072]{1,0:T(8,128)} %get-tuple-element.49, f32[1024,3072]{1,0:T(8,128)} %fusion.389, f32[1024,3072]{1,0:T(8,128)} %get-tuple-element.117, bf16[1024,1024]{1,0:T(8,128)(2,1)} %get-tuple-element.83, ...), kind=kOutput, calls=%fused_computation.54 | convolution fusion | flops 6483345408 | bytes 58720256 | tf_op jit(solution)/shard_map/dot_general | solution.py:21
  599.8 13.7 rev.17
  613.5 16.5 %fusion.380 = f32[2048,512]{1,0:T(8,128)S(1)} fusion(f32[1024,512]{1,0:T(8,128)S(1)} %rev.17, f32[1024,1024]{1,0:T(8,128)} %copy-done.9, f32[1024,1024]{1,0:T(8,128)} %copy-done.4), kind=kOutput, calls=%fused_computation.551 | convolution fusion | flops 12886999040 | bytes 14680064 | tf_op jit(solution)/shard_map/tk,th->kh/dot_general | solution.py:56
  636.6 16.7 %fusion.63 = f32[1024,512]{1,0:T(8,128)} fusion(f32[1024,512]{1,0:T(8,128)S(1)} %get-tuple-element.76, f32[1024,512]{1,0:T(8,128)} %get-tuple-element.77, f32[2048]{0:T(1024)S(1)} %copy-done.72, f32[1024,1024]{1,0:T(8,128)S(1)} %copy-done.12, f32[1024,1024]{1,0:T(8,128)S(1)} %copy-done.7), kind=kOutput, calls=%fused_computation.115 | convolution fusion | flops 12889096192 | bytes 14688256 | tf_op jit(solution)/shard_map/dot_general | solution.py:181
  653.3 13.7 rev.18
  669.7 17.6 %fusion.238 = bf16[1024,512]{1,0:T(8,128)(2,1)S(1)} fusion(f32[1024,512]{1,0:T(8,128)} %get-tuple-element.78, f32[1024,512]{1,0:T(8,128)} %get-tuple-element.79, f32[2048]{0:T(1024)S(1)} %copy-done.72, f32[1024,1024]{1,0:T(8,128)} %copy-done.9, f32[1024,1024]{1,0:T(8,128)S(1)} %copy-done.8), kind=kOutput, calls=%fused_computation.355 | convolution fusion | flops 12889620480 | bytes 13639680 | tf_op jit(solution)/shard_map/dot_general | solution.py:155
  706.4 32.4 %multiply_convert_fusion.2 = (bf16[1024,3072]{1,0:T(8,128)(2,1)S(1)}, f32[1024,3072]{1,0:T(8,128)}, f32[1024,3072]{1,0:T(8,128)}) fusion(f32[1024,3072]{1,0:T(8,128)S(1)} %fusion.391, bf16[1024,512]{1,0:T(8,128)(2,1)S(1)} %fusion.238, bf16[512,3072]{1,0:T(8,128)(2,1)S(1)} %copy-done.89), kind=kOutput, calls=%fused_computation.55 | convolution fusion | flops 3428843520 | bytes 48234496 | tf_op jit(solution)/shard_map/dot_general | solution.py:11
  754.0 14.0 fusion.52
  768.0 23.2 %multiply_convert_fusion = (bf16[1024,3072]{1,0:T(8,128)(2,1)}, bf16[1024,3072]{1,0:T(8,128)(2,1)}) fusion(f32[1024,3072]{1,0:T(8,128)} %get-tuple-element.53, f32[1024,3072]{1,0:T(8,128)} %copy-done.95, f32[1024,3072]{1,0:T(8,128)} %get-tuple-element.118, bf16[1024,1024]{1,0:T(8,128)(2,1)S(1)} %get-tuple-element.61, ...), kind=kOutput, calls=%fused_computation.53 | convolution fusion | flops 6483345408 | bytes 58720256 | tf_op jit(solution)/shard_map/dot_general | solution.py:21
  799.7 16.7 %rev.19 = f32[1024,512]{1,0:T(8,128)} reverse(f32[1024,512]{1,0:T(8,128)} %fusion.395), dimensions={0} | reverse | bytes 4194304 | tf_op jit(solution)/shard_map/jit(_flip)/rev | solution.py:179
  816.4 16.2 fusion.379
  844.0 19.3 %fusion.66 = f32[1024,512]{1,0:T(8,128)} fusion(f32[1024,512]{1,0:T(8,128)} %get-tuple-element.74, f32[1024,512]{1,0:T(8,128)} %get-tuple-element.75, f32[2048]{0:T(1024)S(1)} %copy-done.73, f32[1024,1024]{1,0:T(8,128)} %copy-done.9, f32[1024,1024]{1,0:T(8,128)} %copy-done.4), kind=kOutput, calls=%fused_computation.119 | convolution fusion | flops 12889096192 | bytes 14688256 | tf_op jit(solution)/shard_map/dot_general | solution.py:181
  863.2 16.6 %rev.20 = f32[1024,512]{1,0:T(8,128)} reverse(f32[1024,512]{1,0:T(8,128)} %fusion.66), dimensions={0} | reverse | bytes 4194304 | tf_op jit(solution)/shard_map/jit(_flip)/rev | solution.py:180
  976.5 14.2 reduce.26
  1023.9 14.2 convolution_add_fusion.1
  1045.0 14.1 reduce.27
  1084.8 14.1 reduce.28
  1103.4 24.9 %all-to-all-done.5 = bf16[4,2,131072]{2,1,0:T(2,128)(2,1)} async-done(((bf16[4,2,131072]{2,1,0:T(2,128)(2,1)}), bf16[4,2,131072]{2,1,0:T(2,128)(2,1)}, u32[]{:S(2)}, u32[]{:S(2)}) %all-to-all-start.5) | async-done | bytes 2097184 | tf_op jit(solution)/shard_map/all_to_all | solution.py:207
  1134.3 71.4 %all-reduce.6 = (f32[]{:T(128)}, f32[1024]{0:T(1024)S(1)}, f32[1024]{0:T(1024)S(1)}) all-reduce(f32[]{:T(128)S(6)} %add.302, f32[1024]{0:T(1024)S(1)} %add.319, f32[1024]{0:T(1024)S(1)} %add.320), channel_id=1, replica_groups=mesh['dp'=4,'fsdp'=8] {'dp','fsdp'}, use_global_device_ids=true, to_apply=%region_8.10 | all-reduce | flops 2049 | bytes 16392 | tf_op jit(solution)/shard_map/psum | solution.py:228
  1270.6 153.9 %fusion.10 = (f32[16,512]{1,0:T(8,128)S(1)}, f32[16,512]{1,0:T(8,128)S(1)}, f32[16,512]{1,0:T(8,128)S(1)}, f32[16,512]{1,0:T(8,128)S(1)}) fusion(f32[16,1024]{1,0:T(8,128)S(1)} %bitcast.239, f32[16,512]{1,0:T(8,128)S(1)} %copy-done.66, f32[16,512]{1,0:T(8,128)S(1)} %copy-done.70, f32[16,512]{1,0:T(8,128)S(1)} %copy-done.64, f32[1024]{0:T(1024)S(1)} %copy-done.83, ...), kind=kLoop, calls=%fused_computation.22 | loop fusion | flops 192905216 | bytes 331776 | tf_op jit(solution)/shard_map/transpose(jvp())/reduce_sum | solution.py:36
  1426.5 33.2 %reduce-scatter.8.cloned.1.call-done = f32[32,3072]{1,0:T(8,128)} async-done(((f32[1024,3072]{1,0:T(8,128)}), f32[32,3072]{1,0:T(8,128)}) %reduce-scatter.8.cloned.1.call-update) | async-done | bytes 393232 | tf_op jit(solution)/shard_map/reduce_scatter | solution.py:220
  1459.7 162.0 %reduce-scatter.14.cloned.1.call-done = f32[96,1024]{1,0:T(8,128)} async-done(((f32[3072,1024]{1,0:T(8,128)}), f32[96,1024]{1,0:T(8,128)}) %reduce-scatter.14.cloned.1.call-update) | async-done | bytes 393232 | tf_op jit(solution)/shard_map/reduce_scatter | solution.py:223
  (379 shorter events, 440.6 us)
Async XLA Ops:
  7.2 266.1 %copy-start = (s32[2,32]{1,0:T(2,128)S(1)}, s32[2,32]{1,0:T(2,128)}, u32[]{:S(2)}) copy-start(s32[2,32]{1,0:T(2,128)} %param.21) | copy-start | bytes 772
  7.2 402.9 %all-gather.6.cloned.1.call-start = ((), (), s32[]{:S(2)}) async-start(), calls=%async_computation.13 | async-start | bytes 1081344 | tf_op jit(solution)/shard_map/all_gather | solution.py:129
  8.0 459.4 %all-gather.8.cloned.1.call-start = ((), (), s32[]{:S(2)}) async-start(), calls=%async_computation.14 | async-start | bytes 4325376 | tf_op jit(solution)/shard_map/all_gather | solution.py:113
  8.0 469.7 %copy-start.76 = (pred[1024]{0:T(1024)(128)(4,1)}, pred[1024]{0:T(1024)(128)(4,1)S(1)}, u32[]{:S(2)}) copy-start(pred[1024]{0:T(1024)(128)(4,1)S(1)} %iota_compare_fusion.1) | copy-start | bytes 3076
  23.4 146.0 %copy-start.4 = (f32[1024,1024]{1,0:T(8,128)}, f32[1024,1024]{1,0:T(8,128)S(1)}, u32[]{:S(2)}) copy-start(f32[1024,1024]{1,0:T(8,128)S(1)} %fusion.229) | copy-start | bytes 12582916
  39.7 129.7 %copy-start.9 = (f32[1024,1024]{1,0:T(8,128)}, f32[1024,1024]{1,0:T(8,128)S(1)}, u32[]{:S(2)}) copy-start(f32[1024,1024]{1,0:T(8,128)S(1)} %negate_select_fusion.2) | copy-start | bytes 12582916
  174.6 321.9 %all-gather.12.cloned.1.call-start = ((), (), s32[]{:S(2)}) async-start(), calls=%async_computation.16 | async-start | bytes 6488064 | tf_op jit(solution)/shard_map/all_gather | solution.py:128
  175.4 334.0 %all-gather.10.cloned.1.call-start = ((), (), s32[]{:S(2)}) async-start(), calls=%async_computation.15 | async-start | bytes 3244032 | tf_op jit(solution)/shard_map/all_gather | solution.py:130
  196.3 71.4 %all-to-all-start.2 = ((bf16[4,256,1024]{2,1,0:T(8,128)(2,1)}), bf16[4,256,1024]{2,1,0:T(8,128)(2,1)S(1)}, u32[]{:S(2)}, u32[]{:S(2)}) async-start(bf16[4,256,1024]{2,1,0:T(8,128)(2,1)} %get-tuple-element.112), calls=%async_computation.2 | async-start | bytes 4194304 | tf_op jit(solution)/shard_map/all_to_all | solution.py:140
  214.7 139.7 %copy-start.93 = (bf16[32]{0:T(256)(128)(2,1)S(1)}, bf16[32]{0:T(256)(128)(2,1)}, u32[]{:S(2)}) copy-start(bf16[32]{0:T(256)(128)(2,1)} %param.25) | copy-start | bytes 196
  214.7 139.9 %copy-start.94 = (bf16[32]{0:T(256)(128)(2,1)S(1)}, bf16[32]{0:T(256)(128)(2,1)}, u32[]{:S(2)}) copy-start(bf16[32]{0:T(256)(128)(2,1)} %param.24) | copy-start | bytes 196
  267.7 137.5 %copy-start.2 = (bf16[4,256,1024]{2,1,0:T(8,128)(2,1)}, bf16[4,256,1024]{2,1,0:T(8,128)(2,1)S(1)}, u32[]{:S(2)}) copy-start(bf16[4,256,1024]{2,1,0:T(8,128)(2,1)S(1)} %all-to-all-done.2) | copy-start | bytes 6291460
  267.7 128.7 %all-to-all-start = ((bf16[4,256,1024]{2,1,0:T(8,128)(2,1)}), bf16[4,256,1024]{2,1,0:T(8,128)(2,1)}, u32[]{:S(2)}, u32[]{:S(2)}) async-start(bf16[4,256,1024]{2,1,0:T(8,128)(2,1)} %get-tuple-element.114), calls=%async_computation | async-start | bytes 4194304 | tf_op jit(solution)/shard_map/all_to_all | solution.py:140
  272.1 270.5 %all-gather.14.cloned.1.call-start = ((), (), s32[]{:S(2)}) async-start(), calls=%async_computation.17 | async-start | bytes 6488064 | tf_op jit(solution)/shard_map/all_gather | solution.py:131
  394.0 87.3 %copy-start.71 = (f32[2048]{0:T(1024)}, f32[2048]{0:T(1024)S(1)}, u32[]{:S(2)}) copy-start(f32[2048]{0:T(1024)S(1)} %select_multiply_fusion) | copy-start | bytes 24580
  396.5 158.4 %all-to-all-start.4 = ((bf16[4,256,1024]{2,1,0:T(8,128)(2,1)}), bf16[4,256,1024]{2,1,0:T(8,128)(2,1)}, u32[]{:S(2)}, u32[]{:S(2)}) async-start(bf16[4,256,1024]{2,1,0:T(8,128)(2,1)} %get-tuple-element.113), calls=%async_computation.4 | async-start | bytes 4194304 | tf_op jit(solution)/shard_map/all_to_all | solution.py:141
  554.9 199.2 %all-to-all-start.6 = ((bf16[4,256,1024]{2,1,0:T(8,128)(2,1)}), bf16[4,256,1024]{2,1,0:T(8,128)(2,1)}, u32[]{:S(2)}, u32[]{:S(2)}) async-start(bf16[4,256,1024]{2,1,0:T(8,128)(2,1)} %get-tuple-element.111), calls=%async_computation.6 | async-start | bytes 4194304 | tf_op jit(solution)/shard_map/all_to_all | solution.py:141
  560.0 700.4 %reduce-scatter.16.cloned.1.call-start = ((), (), s32[]{:S(2)}) async-start(), calls=%async_computation.22 | async-start | bytes 4325376
  669.3 69.5 %copy-start.39 = (bf16[1024,512]{1,0:T(8,128)(2,1)}, bf16[1024,512]{1,0:T(8,128)(2,1)S(1)}, u32[]{:S(2)}) copy-start(bf16[1024,512]{1,0:T(8,128)(2,1)S(1)} %fusion.116) | copy-start | bytes 3145732
  843.9 582.6 %reduce-scatter.10.cloned.1.call-start = ((), (), s32[]{:S(2)}) async-start(), calls=%async_computation.19 | async-start | bytes 2162688 | tf_op jit(solution)/shard_map/reduce_scatter | solution.py:221
  887.7 538.9 %reduce-scatter.12.cloned.1.call-start = ((), (), s32[]{:S(2)}) async-start(), calls=%async_computation.20 | async-start | bytes 6488064 | tf_op jit(solution)/shard_map/reduce_scatter | solution.py:222
  901.8 557.9 %reduce-scatter.8.cloned.1.call-start = ((), (), s32[]{:S(2)}) async-start(), calls=%async_computation.18 | async-start | bytes 12976128 | tf_op jit(solution)/shard_map/reduce_scatter | solution.py:220
  964.4 53.8 %all-to-all-start.7 = ((bf16[4,2,131072]{2,1,0:T(2,128)(2,1)}), bf16[4,2,131072]{2,1,0:T(2,128)(2,1)S(1)}, u32[]{:S(2)}, u32[]{:S(2)}) async-start(bf16[4,2,131072]{2,1,0:T(2,128)(2,1)} %reshape.503), calls=%async_computation.7 | async-start | bytes 4194304 | tf_op jit(solution)/shard_map/all_to_all | solution.py:207
  1018.2 55.0 %all-to-all-start.3 = ((bf16[4,2,131072]{2,1,0:T(2,128)(2,1)}), bf16[4,2,131072]{2,1,0:T(2,128)(2,1)}, u32[]{:S(2)}, u32[]{:S(2)}) async-start(bf16[4,2,131072]{2,1,0:T(2,128)(2,1)} %reshape.499), calls=%async_computation.3 | async-start | bytes 4194304 | tf_op jit(solution)/shard_map/all_to_all | solution.py:204
  1023.9 597.8 %reduce-scatter.14.cloned.1.call-start = ((), (), s32[]{:S(2)}) async-start(), calls=%async_computation.21 | async-start | bytes 12976128 | tf_op jit(solution)/shard_map/reduce_scatter | solution.py:223
  1073.2 55.1 %all-to-all-start.5 = ((bf16[4,2,131072]{2,1,0:T(2,128)(2,1)}), bf16[4,2,131072]{2,1,0:T(2,128)(2,1)}, u32[]{:S(2)}, u32[]{:S(2)}) async-start(bf16[4,2,131072]{2,1,0:T(2,128)(2,1)} %reshape.505), calls=%async_computation.5 | async-start | bytes 4194304 | tf_op jit(solution)/shard_map/all_to_all | solution.py:207
  1128.3 108.9 %all-to-all-start.1 = ((bf16[4,2,131072]{2,1,0:T(2,128)(2,1)}), bf16[4,2,131072]{2,1,0:T(2,128)(2,1)}, u32[]{:S(2)}, u32[]{:S(2)}) async-start(bf16[4,2,131072]{2,1,0:T(2,128)(2,1)} %reshape.501), calls=%async_computation.1 | async-start | bytes 4194304 | tf_op jit(solution)/shard_map/all_to_all | solution.py:204
  1270.6 154.6 %copy-start.44 = (f32[16,512]{1,0:T(8,128)S(1)}, f32[16,512]{1,0:T(8,128)}, u32[]{:S(2)}) copy-start(f32[16,512]{1,0:T(8,128)} %param.29) | copy-start | bytes 98308
  1270.6 154.6 %copy-start.46 = (f32[16,512]{1,0:T(8,128)S(1)}, f32[16,512]{1,0:T(8,128)}, u32[]{:S(2)}) copy-start(f32[16,512]{1,0:T(8,128)} %param.30) | copy-start | bytes 98308
  1270.6 154.6 %copy-start.85 = (f32[16]{0:T(128)S(1)}, f32[16]{0:T(128)}, u32[]{:S(2)}) copy-start(f32[16]{0:T(128)} %copy-done.84) | copy-start | bytes 196
  1270.6 155.4 %copy-start.88 = (f32[16]{0:T(128)S(1)}, f32[16]{0:T(128)}, u32[]{:S(2)}) copy-start(f32[16]{0:T(128)} %param.31) | copy-start | bytes 196
  1270.6 351.1 %copy-start.1 = (s32[2,32]{1,0:T(2,128)S(1)}, s32[2,32]{1,0:T(2,128)}, u32[]{:S(2)}) copy-start(s32[2,32]{1,0:T(2,128)} %param.21) | copy-start | bytes 772
  (87 other events, 1220.6 us)
Sparse Core Ops, SparseCore 0:
  10.9 56.3 all-gather.5
  174.7 87.4 all-gather.7
  265.1 98.6 all-gather.11
  366.5 64.2 all-gather.9
  433.5 85.5 all-gather.13
  844.1 145.7 reduce-scatter.15
  992.7 139.0 reduce-scatter.9
  1138.9 159.3 reduce-scatter.11
  1305.0 154.6 reduce-scatter.7
  1467.2 154.4 reduce-scatter.13
where the time goes:
time: 1650 us; the launch traced here: 1630 us
  other arithmetic  444 us (27%)
  matrix products  437 us (26%)
  waiting for transfers between devices  296 us (18%)
  local copies, waits for them, and re-layouts  203 us (12%)
  blocking collectives  190 us (12%)
  starting transfers between devices  40.7 us (2%)
  between operations  19.6 us (1%)
    reduce_scatter x1, waiting for transfers between devices, shards(): lax.psum_scatter(output_total, ('dp', 'fsdp'), scatter_dimension=0, tiled...  162 us
    reduce_sum x1, other arithmetic, kernel_rows(): angle = (step_size[:, None] * frequency)[:, :, None] * positions  154 us
    reduce_sum x1, other arithmetic, kernel_rows(): return jnp.sum(damping * waves, axis=1)  129 us
    dot_general x8, matrix products, matmul(): return jnp.dot(left, right, preferred_element_type=jnp.float32)  110 us
    dot_general x8, matrix products, cols_inner(): lax.dot_general(left, right, (((1,), (1,)), ((), ())), preferred_element_...  93.4 us
    dot_general x5, matrix products, transform(): return jnp.einsum('tk,th->kh', table, values, precision=highest)  88 us
    psum x1, blocking collectives, shards(): count = lax.psum(jnp.sum(keep), ('dp', 'fsdp'))  79.8 us
    unnamed x230, local copies, waits for them, and re-layouts  74.6 us
  transfers between devices with their start and end apart: 18, of which 6 were waited for; matrix products, arithmetic and copies ran while one was open for 60% of the time, Pallas kernels for 0%

commit v1 on v0

v1 whole, which is shorter than its diff:
```python
import numpy as np
import jax
import jax.numpy as jnp
from jax import lax
from jax.sharding import PartitionSpec as P

epsilon = 1e-05
highest = lax.Precision.HIGHEST
high = lax.Precision.HIGH
bf16 = jnp.bfloat16
f32 = jnp.float32
both = ("dp", "fsdp")


def matmul(left, right):
    return jnp.dot(left, right, preferred_element_type=f32)


def rows_inner(left, right):
    return lax.dot_general(left, right, (((0,), (0,)), ((), ())), preferred_element_type=f32)


def cols_inner(left, right):
    return lax.dot_general(left, right, (((1,), (1,)), ((), ())), preferred_element_type=f32)


def gelu_and_slope(values):
    phi = 0.5 * (1.0 + lax.erf(values * 0.7071067811865476))
    return (
        values * phi,
        phi + values * jnp.exp(-0.5 * values * values) * 0.3989422804014327,
    )


def fourier_table(chunk):
    freq = np.arange(chunk)[:, None]
    time = np.arange(chunk)[None, :]
    angle = (freq * time % (2 * chunk)) * (np.pi / chunk)
    sines = -np.sin(angle)
    sines[0] = 1.0 - 2.0 * (np.arange(chunk) % 2)
    table = np.concatenate([np.cos(angle), sines], axis=0)
    scaling = np.full((2 * chunk, 1), 1.0 / chunk)
    scaling[0] = scaling[chunk] = 0.5 / chunk
    sign = np.tile(1.0 - 2.0 * (np.arange(chunk) % 2), 2)
    sign[chunk] = 1.0 - 2.0 * (chunk % 2)
    return table.astype(np.float32), (table * scaling).astype(np.float32), sign.astype(np.float32)


def packed_product(first, second, chunk, conjugate):
    a_re, a_im = first[..., :chunk, :, :], first[..., chunk:, :, :]
    b_re, b_im = second[..., :chunk, :, :], second[..., chunk:, :, :]
    edge = (jnp.arange(chunk) == 0)[:, None, None]
    crossed = a_im * b_im
    straight = a_re * b_re
    if conjugate:
        real = straight + jnp.where(edge, 0.0, crossed)
        imag = jnp.where(edge, crossed, a_re * b_im - a_im * b_re)
    else:
        real = straight - jnp.where(edge, 0.0, crossed)
        imag = jnp.where(edge, crossed, a_re * b_im + a_im * b_re)
    return jnp.concatenate([real, imag], axis=-3)


def kernel_factors(decay, frequency, log_step, length):
    fine = 32
    coarse = length // fine
    step_size = jnp.exp(log_step)[:, None]
    real = (step_size * decay)[:, None, :]
    imag = (step_size * frequency)[:, None, :]
    far = (jnp.arange(coarse, dtype=jnp.int32) * fine).astype(f32)[None, :, None]
    near = jnp.arange(fine, dtype=jnp.int32).astype(f32)[None, :, None]
    far_damp, near_damp = jnp.exp(real * far), jnp.exp(real * near)
    return (
        (far_damp * jnp.cos(imag * far), far_damp * jnp.sin(imag * far)),
        (near_damp * jnp.cos(imag * near), near_damp * jnp.sin(imag * near)),
        step_size,
    )


def kernel_forward(weight_pair, factors):
    (far_re, far_im), (near_re, near_im), _ = factors
    w_re, w_im = weight_pair[0][:, None, :], weight_pair[1][:, None, :]
    left = jnp.concatenate([far_re, -far_im], axis=2)
    right = jnp.concatenate(
        [w_re * near_re - w_im * near_im, w_re * near_im + w_im * near_re], axis=2
    )
    rows = jnp.einsum("han,hbn->hab", left, right, precision=highest)
    return rows.reshape(rows.shape[0], -1)


def kernel_backward(grad_rows, weight_pair, decay, frequency, factors):
    (far_re, far_im), (near_re, near_im), step_size = factors
    channels, coarse, states = far_re.shape
    fine = near_re.shape[1]
    tiles = grad_rows.reshape(channels, coarse, fine)
    near_index = jnp.arange(fine, dtype=jnp.int32).astype(f32)
    far_index = (jnp.arange(coarse, dtype=jnp.int32) * fine).astype(f32)[None, :, None]
    stacked = jnp.concatenate([tiles, tiles * near_index], axis=1)
    part = jnp.einsum(
        "hab,hbn->han", stacked, jnp.concatenate([near_re, near_im], axis=2), precision=highest
    )
    u_re, u_im = part[:, :coarse, :states], part[:, :coarse, states:]
    v_re = part[:, coarse:, :states] + far_index * u_re
    v_im = part[:, coarse:, states:] + far_index * u_im
    s_re = jnp.sum(far_re * u_re - far_im * u_im, axis=1)
    s_im = jnp.sum(far_re * u_im + far_im * u_re, axis=1)
    t_re = jnp.sum(far_re * v_re - far_im * v_im, axis=1)
    t_im = jnp.sum(far_re * v_im + far_im * v_re, axis=1)
    w_re, w_im = weight_pair[0], weight_pair[1]
    along_re = step_size * (w_re * t_re - w_im * t_im)
    along_im = -step_size * (w_re * t_im + w_im * t_re)
    return (
        jnp.stack([s_re, -s_im]),
        along_re,
        along_im,
        jnp.sum(decay * along_re + frequency * along_im, axis=1),
    )


def exchange(values):
    return lax.all_to_all(values, "dp", split_axis=0, concat_axis=0, tiled=True)


def scatter_sum(values):
    dp_count, fsdp_count = lax.axis_size("dp"), lax.axis_size("fsdp")
    _, height, width = values.shape
    tiles = values.reshape(dp_count, fsdp_count, height, width).transpose(1, 0, 2, 3)
    part = lax.psum_scatter(
        tiles.reshape(-1, width), "fsdp", scatter_dimension=0, tiled=True
    )
    return lax.psum_scatter(part, "dp", scatter_dimension=0, tiled=True)


def shards(
    tokens,
    cotangent,
    teacher,
    lengths,
    dealing,
    loss_mask,
    norm_gain,
    norm_bias,
    gate_weight,
    reduce_weight,
    state_weight,
    decay_rate,
    frequency,
    log_step,
    expand_weight,
    out_weight,
):
    dp_count = lax.axis_size("dp")
    devices = dp_count * lax.axis_size("fsdp")
    group_index = lax.axis_index("fsdp")
    dp_place = lax.axis_index("dp")
    micro_count, seqs, chunk, model_width = tokens.shape
    rows = seqs * chunk
    seq_length = chunk * dp_count
    gate_width = gate_weight.shape[1]
    reduced_width = reduce_weight.shape[1]
    own_width = reduced_width // dp_count
    table_np, inverse_np, sign_np = fourier_table(chunk)
    table, inverse, sign = jnp.asarray(table_np), jnp.asarray(inverse_np), jnp.asarray(sign_np)

    teach = lax.all_to_all(
        teacher.reshape(micro_count, dp_count, chunk, model_width), "dp", split_axis=1, concat_axis=1, tiled=True
    )
    masked = lax.all_to_all(
        loss_mask.reshape(micro_count, dp_count, chunk), "dp", split_axis=1, concat_axis=1, tiled=True
    )
    local_ids = group_index * seqs + jnp.arange(seqs, dtype=jnp.int32)
    targets = jnp.take(dealing, local_ids, axis=1)
    own_lengths = jnp.take(lengths, local_ids, axis=1)
    positions = dp_place * chunk + jnp.arange(chunk, dtype=jnp.int32)
    valid = (positions[None, None, :] < own_lengths[:, :, None]).astype(f32)
    keep = jnp.stack([jnp.take(masked[m], targets[m], axis=0) for m in range(micro_count)]).astype(f32) * valid
    teach = [jnp.take(teach[m], targets[m], axis=0).reshape(rows, model_width) for m in range(micro_count)]
    count = lax.psum(jnp.sum(keep), both)
    valid = valid.reshape(micro_count, rows, 1)
    keep = keep.reshape(micro_count, rows, 1)

    share = gate_weight.shape[0]
    extra = jnp.concatenate(
        [norm_gain[:, None], norm_bias[:, None], jnp.zeros((share, 126), bf16)], axis=1
    )
    first = lax.all_gather(
        jnp.concatenate([gate_weight, reduce_weight, extra], axis=1), both, axis=0, tiled=True
    )
    w_expand = lax.all_gather(expand_weight, both, axis=0, tiled=True)
    w_out = lax.all_gather(out_weight, both, axis=0, tiled=True)
    w_gate = first[:, :gate_width]
    w_reduce = first[:, gate_width : gate_width + reduced_width]
    gain_values = first[:, gate_width + reduced_width].astype(f32)
    bias_values = first[:, gate_width + reduced_width + 1].astype(f32)

    factors = kernel_factors(decay_rate, frequency, log_step, seq_length)
    own_kernel = kernel_forward(state_weight, factors)
    kernel = lax.all_gather(own_kernel, "fsdp", axis=0, tiled=True)
    segments = jnp.einsum(
        "kt,hct->ckh", table, kernel.reshape(own_width, dp_count, chunk), precision=highest
    )
    previous = jnp.concatenate([jnp.zeros_like(segments[:1]), segments[:-1]], axis=0)
    kernel_spec = (segments + sign[:, None] * previous)[:, :, None, :]

    def spectrum(values):
        flat = values.reshape(dp_count, chunk, seqs * own_width).astype(f32)
        spec = jnp.einsum("kt,ctn->ckn", table, flat, precision=high)
        return spec.reshape(dp_count, 2 * chunk, seqs, own_width)

    def back_to_time(spec):
        flat = spec.reshape(dp_count, 2 * chunk, seqs * own_width)
        return jnp.einsum("kt,ckn->ctn", inverse, flat, precision=high)

    def to_channels(values):
        split = values.reshape(seqs, chunk, dp_count, own_width).transpose(2, 1, 0, 3)
        return exchange(split.astype(bf16).reshape(dp_count, chunk, seqs * own_width))

    def to_rows(values):
        back = exchange(values.astype(bf16))
        return back.reshape(dp_count, chunk, seqs, own_width).transpose(2, 1, 0, 3).reshape(rows, reduced_width)

    error_total = jnp.zeros((), f32)
    outputs, returned, saved = [], [], []
    for m in range(micro_count):
        inputs = tokens[m].reshape(rows, model_width).astype(f32)
        centre = jnp.mean(inputs, axis=1, keepdims=True)
        centred = inputs - centre
        variance = jnp.mean(centred * centred, axis=1, keepdims=True)
        inverse_std = lax.rsqrt(variance + epsilon)
        unit = centred * inverse_std
        normed = (unit * gain_values + bias_values).astype(bf16)
        pre_reduced = matmul(normed, w_reduce)
        reduced, slope_reduced = gelu_and_slope(pre_reduced)
        channel_rows = to_channels(reduced)
        pre_gate = matmul(normed, w_gate)
        gate, slope_gate = gelu_and_slope(pre_gate)
        saved.append((inputs, inverse_std, unit, normed, slope_reduced, channel_rows, gate, slope_gate))

    middle = []
    for m in range(micro_count):
        channel_rows = saved[m][5]
        reduced_spec = spectrum(channel_rows)
        mixed_spec = [
            sum(
                packed_product(kernel_spec[k], reduced_spec[c - k], chunk, False)
                for k in range(c + 1)
            )
            for c in range(dp_count)
        ]
        middle.append((reduced_spec, to_rows(back_to_time(jnp.stack(mixed_spec)))))

    kernel_total = jnp.zeros((dp_count, 2 * chunk, own_width), f32)
    later = []
    out_total, expand_total = 0.0, 0.0
    for m in range(micro_count):
        inputs, inverse_std, unit, normed, slope_reduced, channel_rows, gate, slope_gate = saved[m]
        reduced_spec, state_out = middle[m]
        expanded = matmul(state_out, w_expand)
        product = (expanded * gate).astype(bf16)
        branch = matmul(product, w_out)
        full = inputs + valid[m] * branch
        outputs.append(full.astype(bf16).reshape(seqs, chunk, model_width))
        errors = full - teach[m].astype(f32)
        error_total = error_total + jnp.sum(keep[m] * errors * errors)
        grad_full = cotangent[m].reshape(rows, model_width).astype(f32) + keep[m] * errors * (
            2.0 / (model_width * count)
        )
        grad_branch = (valid[m] * grad_full).astype(bf16)
        grad_product = cols_inner(grad_branch, w_out)
        grad_expanded = (grad_product * gate).astype(bf16)
        grad_pre_gate = (grad_product * expanded * slope_gate).astype(bf16)
        grad_mixed = cols_inner(grad_expanded, w_expand)
        grad_rows = to_channels(grad_mixed)
        out_total = out_total + rows_inner(product, grad_branch)
        expand_total = expand_total + rows_inner(state_out, grad_expanded)
        later.append((grad_full, grad_pre_gate, grad_rows))
    late_sum = scatter_sum(
        jnp.concatenate([out_total.reshape(devices, -1), expand_total.reshape(devices, -1)], axis=1).reshape(
            devices, -1, 1024
        )
    )

    gate_total, reduce_total = 0.0, 0.0
    gain_total, bias_total = 0.0, 0.0
    ends = []
    for m in range(micro_count):
        inputs, inverse_std, unit, normed, slope_reduced, channel_rows, gate, slope_gate = saved[m]
        reduced_spec = middle[m][0]
        grad_full, grad_pre_gate, grad_rows = later[m]
        grad_spec = spectrum(grad_rows)
        back_spec = [
            sum(
                packed_product(kernel_spec[c - k], grad_spec[c], chunk, True)
                for c in range(k, dp_count)
            )
            for k in range(dp_count)
        ]
        grad_reduced = to_rows(back_to_time(jnp.stack(back_spec)))
        cross = [
            sum(
                packed_product(reduced_spec[c - k], grad_spec[c], chunk, True)
                for c in range(k, dp_count)
            )
            for k in range(dp_count)
        ]
        kernel_total = kernel_total + jnp.sum(jnp.stack(cross), axis=2)
        gate_total = gate_total + rows_inner(normed, grad_pre_gate)
        ends.append((grad_full, grad_pre_gate, grad_reduced))
    for m in range(micro_count):
        inputs, inverse_std, unit, normed, slope_reduced, channel_rows, gate, slope_gate = saved[m]
        grad_full, grad_pre_gate, grad_reduced = ends[m]
        grad_pre_reduced = (grad_reduced.astype(f32) * slope_reduced).astype(bf16)
        reduce_total = reduce_total + rows_inner(normed, grad_pre_reduced)
        grad_normed = cols_inner(grad_pre_gate, w_gate) + cols_inner(grad_pre_reduced, w_reduce)
        gain_total = gain_total + jnp.sum(grad_normed * unit, axis=0)
        bias_total = bias_total + jnp.sum(grad_normed, axis=0)
        grad_unit = grad_normed * gain_values
        grad_inputs = grad_full + inverse_std * (
            grad_unit
            - jnp.mean(grad_unit, axis=1, keepdims=True)
            - unit * jnp.mean(grad_unit * unit, axis=1, keepdims=True)
        )
        returned.append(grad_inputs.astype(bf16).reshape(seqs, chunk, model_width))

    following = jnp.concatenate([kernel_total[1:], jnp.zeros_like(kernel_total[:1])], axis=0)
    kernel_grad = jnp.einsum(
        "kt,ckh->hct", inverse, kernel_total + sign[:, None] * following, precision=highest
    ).reshape(reduced_width // dp_count, seq_length)
    kernel_grad = lax.psum_scatter(kernel_grad, "fsdp", scatter_dimension=0, tiled=True)
    pair_grad, decay_grad, frequency_grad, step_grad = kernel_backward(
        kernel_grad, state_weight, decay_rate, frequency, factors
    )
    last_sum = scatter_sum(
        jnp.concatenate([gate_total.reshape(devices, -1), reduce_total.reshape(devices, -1)], axis=1).reshape(
            devices, -1, 1024
        )
    )
    sums = lax.psum(jnp.concatenate([gain_total, bias_total, jnp.full((128,), error_total)]), both)
    place = (dp_place * lax.axis_size("fsdp") + group_index) * share
    loss_value = sums[2 * model_width] / (model_width * count)
    late_flat, last_flat = late_sum.reshape(-1), last_sum.reshape(-1)
    out_size, gate_size = out_weight.size, gate_weight.size
    return (
        jnp.stack(outputs),
        loss_value,
        jnp.stack(returned),
        lax.dynamic_slice(sums, (place,), (share,)),
        lax.dynamic_slice(sums, (model_width + place,), (share,)),
        last_flat[:gate_size].reshape(gate_weight.shape),
        last_flat[gate_size:].reshape(reduce_weight.shape),
        pair_grad,
        decay_grad,
        frequency_grad,
        step_grad,
        late_flat[out_size:].reshape(expand_weight.shape),
        late_flat[:out_size].reshape(out_weight.shape),
    )


def solution(mesh):
    in_specs = (
        P(None, "fsdp", "dp", None),
        P(None, "fsdp", "dp", None),
        P(None, ("dp", "fsdp"), None, None),
        P(),
        P(),
        P(None, ("dp", "fsdp"), None),
        P(("dp", "fsdp")),
        P(("dp", "fsdp")),
        P(("dp", "fsdp"), None),
        P(("dp", "fsdp"), None),
        P(None, ("dp", "fsdp"), None),
        P(("dp", "fsdp"), None),
        P(("dp", "fsdp"), None),
        P(("dp", "fsdp")),
        P(("dp", "fsdp"), None),
        P(("dp", "fsdp"), None),
    )
    out_specs = (
        P(None, "fsdp", "dp", None),
        P(),
        P(None, "fsdp", "dp", None),
        P(("dp", "fsdp")),
        P(("dp", "fsdp")),
        P(("dp", "fsdp"), None),
        P(("dp", "fsdp"), None),
        P(None, ("dp", "fsdp"), None),
        P(("dp", "fsdp"), None),
        P(("dp", "fsdp"), None),
        P(("dp", "fsdp")),
        P(("dp", "fsdp"), None),
        P(("dp", "fsdp"), None),
    )
    return jax.shard_map(shards, mesh=mesh, in_specs=in_specs, out_specs=out_specs, check_vma=False)
```

time: 1650 us -> 973 us (0.59)
  other arithmetic: 444 us -> 119 us
  matrix products: 437 us -> 287 us
  waiting for transfers between devices: 296 us -> 183 us
  local copies, waits for them, and re-layouts: 203 us -> 147 us
  blocking collectives: 190 us -> 159 us
    reduce_sum x6 -> x5, other arithmetic: 298 us -> 8.85 us  [the longest x1 5.25 us: kernel_backward(): t_re = jnp.sum(far_re * v_re - far_im * v_im, axis=1)]
    dot_general x18 -> x20, matrix products: 275 us -> 124 us  [the longest x8 94.8 us: matmul(): return jnp.dot(left, right, preferred_element_type=f32)]
    reduce_scatter x4, waiting for transfers between devices: 195 us -> 123 us  [the longest x2 108 us: scatter_sum(): lax.psum_scatter(tiles.reshape(-1, width), 'fsdp', scatter_dimension=0, t...]
    rev x5 -> x0, local copies, waits for them, and re-layouts: 61.2 us -> none  [the longest x2 30.3 us: shards(): reversed_spec = transform(table, jnp.flip(grad_mixed, 0))]
    unnamed x10 -> x5, other arithmetic: 55.2 us -> 1.35 us
    unnamed x230 -> x250, local copies, waits for them, and re-layouts: 74.6 us -> 21.6 us
    all_to_all x8 -> x10, waiting for transfers between devices: 98.5 us -> 57.8 us  [the longest x8 57.8 us: exchange(): return lax.all_to_all(values, 'dp', split_axis=0, concat_axis=0, tiled=True)]
    unnamed x1 -> x0, blocking collectives: 38.5 us -> none
  transfers between devices with their start and end apart: 18 -> 18, of which waited for: 6 -> 7; matrix products, arithmetic and copies ran while one was open for 60% -> 51% of each run, Pallas kernels for 0% -> 0%
where the time goes in v1:
time: 973 us; the launch traced here: 963 us
  matrix products  287 us (29%)
  waiting for transfers between devices  183 us (19%)
  blocking collectives  159 us (16%)
  local copies, waits for them, and re-layouts  147 us (15%)
  other arithmetic  119 us (12%)
  starting transfers between devices  47 us (5%)
  between operations  20 us (2%)
    psum x1, blocking collectives, shards(): count = lax.psum(jnp.sum(keep), both)  109 us
    reduce_scatter x2, waiting for transfers between devices, scatter_sum(): lax.psum_scatter(tiles.reshape(-1, width), 'fsdp', scatter_dimension=0, t...  108 us
    dot_general x8, matrix products, cols_inner(): lax.dot_general(left, right, (((1,), (1,)), ((), ())), preferred_element_...  96.9 us
    dot_general x8, matrix products, matmul(): return jnp.dot(left, right, preferred_element_type=f32)  94.8 us
    dot_general x8, matrix products, rows_inner(): lax.dot_general(left, right, (((0,), (0,)), ((), ())), preferred_element_...  65.9 us
    all_to_all x8, waiting for transfers between devices, exchange(): return lax.all_to_all(values, 'dp', split_axis=0, concat_axis=0, tiled=True)  57.8 us
    psum x1, blocking collectives, shards(): lax.psum(jnp.concatenate([gain_total, bias_total, jnp.full((128,), error_...  40.5 us
    all_to_all x8, starting transfers between devices, exchange(): return lax.all_to_all(values, 'dp', split_axis=0, concat_axis=0, tiled=True)  35 us
  transfers between devices with their start and end apart: 18, of which 7 were waited for; matrix products, arithmetic and copies ran while one was open for 51% of the time, Pallas kernels for 0%

profile of v1, /device:TPU:0, one launch (start us, length us, event | category | flops | bytes accessed | tf_op | source)
XLA Modules:
  0.0 962.7 jit_solution(8505869496461615605)
XLA Ops:
  33.7 9.0 multiply_subtract_fusion
  44.9 9.9 %all_gather.12 = f32[128,1024]{1,0:T(8,128)S(1)} all-gather(f32[16,1024]{1,0:T(8,128)S(1)} %reshape.3217), channel_id=1, replica_groups=mesh['dp'=4,'fsdp'=8] {'fsdp'}, dimensions={0}, use_global_device_ids=true | all-gather | bytes 589824 | tf_op jit(solution)/shard_map/all_gather | solution.py:198
  68.9 108.9 %psum.14 = f32[]{:T(128)} all-reduce(f32[]{:T(128)} %get-tuple-element.41), channel_id=1, replica_groups=mesh['dp'=4,'fsdp'=8] {'dp','fsdp'}, use_global_device_ids=true, to_apply=%region_5.9 | all-reduce | flops 1 | bytes 8 | tf_op jit(solution)/shard_map/psum | solution.py:178
  231.9 12.3 %fusion.90 = f32[1024,3072]{1,0:T(8,128)} fusion(bf16[1024,1024]{1,0:T(8,128)(2,1)S(1)} %get-tuple-element.196, bf16[1024,3712]{1,0:T(8,128)(2,1)} %all-gather.4.cloned.1.call-done), kind=kOutput, calls=%fused_computation.273 | convolution fusion | flops 6442450944 | bytes 20971520 | tf_op jit(solution)/shard_map/dot_general | solution.py:16
  253.2 13.5 %all-to-all-done = bf16[4,256,512]{1,2,0:T(8,128)(2,1)} async-done(((bf16[4,256,512]{1,2,0:T(8,128)(2,1)}), bf16[4,256,512]{1,2,0:T(8,128)(2,1)}, u32[]{:S(2)}, u32[]{:S(2)}) %all-to-all-start) | async-done | bytes 1048608 | tf_op jit(solution)/shard_map/all_to_all | solution.py:121
  270.7 12.1 %fusion.92 = f32[1024,3072]{1,0:T(8,128)} fusion(bf16[1024,1024]{1,0:T(8,128)(2,1)} %get-tuple-element.195, bf16[1024,3712]{1,0:T(8,128)(2,1)} %all-gather.4.cloned.1.call-done), kind=kOutput, calls=%fused_computation.275 | convolution fusion | flops 6442450944 | bytes 20971520 | tf_op jit(solution)/shard_map/dot_general | solution.py:16
  291.9 20.2 %all-to-all-done.3 = bf16[4,256,512]{1,2,0:T(8,128)(2,1)S(1)} async-done(((bf16[4,256,512]{1,2,0:T(8,128)(2,1)}), bf16[4,256,512]{1,2,0:T(8,128)(2,1)S(1)}, u32[]{:S(2)}, u32[]{:S(2)}) %all-to-all-start.3) | async-done | bytes 1048608 | tf_op jit(solution)/shard_map/all_to_all | solution.py:121
  317.3 16.4 %multiply_convert_fusion.2 = (bf16[1024,3072]{1,0:T(8,128)(2,1)}, f32[1024,3072]{1,0:T(8,128)}, f32[1024,3072]{1,0:T(8,128)}) fusion(f32[1024,3072]{1,0:T(8,128)} %fusion.90, bf16[512,3072]{1,0:T(8,128)(2,1)} %all-gather.6.cloned.1.call-done, bf16[128,8,4,128]{3,2,1,0:T(4,128)(2,1)S(1)} %bitcast.1089), kind=kOutput, calls=%fused_computation.24 | convolution fusion | flops 3240099840 | bytes 48234496 | tf_op jit(solution)/shard_map/dot_general | solution.py:16
  333.7 14.5 %multiply_convert_fusion.4 = (bf16[1024,1024]{1,0:T(8,128)(2,1)}, f32[1024,1024]{1,0:T(8,128)}) fusion(f32[1024]{0:T(1024)S(1)} %bitcast.1192, f32[]{:T(128)S(6)} %div.41, bf16[4,256,1024]{2,1,0:T(8,128)(2,1)} %broadcast_select_fusion, f32[1024]{0:T(1024)S(1)} %bitcast.1189, bf16[1,4,256,1024]{3,2,1,0:T(8,128)(2,1)} %get-tuple-element.211, ...), kind=kOutput, calls=%fused_computation.267 | convolution fusion | flops 6453985280 | bytes 25174020 | tf_op jit(solution)/shard_map/dot_general | solution.py:16
  348.2 25.0 %multiply_convert_fusion = (bf16[1024,3072]{1,0:T(8,128)(2,1)}, bf16[1024,3072]{1,0:T(8,128)(2,1)}) fusion(f32[1024,3072]{1,0:T(8,128)} %get-tuple-element.46, f32[1024,3072]{1,0:T(8,128)} %fusion.90, f32[1024,3072]{1,0:T(8,128)} %get-tuple-element.327, bf16[1024,1024]{1,0:T(8,128)(2,1)} %get-tuple-element.328, ...), kind=kOutput, calls=%fused_computation.22 | convolution fusion | flops 6483345408 | bytes 58720256 | tf_op jit(solution)/shard_map/dot_general | solution.py:24
  388.2 16.3 %multiply_convert_fusion.3 = (bf16[1024,3072]{1,0:T(8,128)(2,1)}, f32[1024,3072]{1,0:T(8,128)}, f32[1024,3072]{1,0:T(8,128)}) fusion(f32[1024,3072]{1,0:T(8,128)} %fusion.92, bf16[512,3072]{1,0:T(8,128)(2,1)} %all-gather.6.cloned.1.call-done, bf16[128,8,4,128]{3,2,1,0:T(4,128)(2,1)S(1)} %bitcast.1091), kind=kOutput, calls=%fused_computation.26 | convolution fusion | flops 3240099840 | bytes 48234496 | tf_op jit(solution)/shard_map/dot_general | solution.py:16
  404.5 13.9 %multiply_convert_fusion.5 = (bf16[1024,1024]{1,0:T(8,128)(2,1)}, f32[1024,1024]{1,0:T(8,128)}) fusion(f32[1024]{0:T(1024)S(1)} %bitcast.1191, f32[]{:T(128)S(6)} %div.41, bf16[4,256,1024]{2,1,0:T(8,128)(2,1)S(1)} %copy-done.18, f32[1024]{0:T(1024)S(1)} %bitcast.1187, bf16[1,4,256,1024]{3,2,1,0:T(8,128)(2,1)} %get-tuple-element.212, ...), kind=kOutput, calls=%fused_computation.268 | convolution fusion | flops 6453985280 | bytes 25174020 | tf_op jit(solution)/shard_map/dot_general | solution.py:16
  418.5 24.9 %multiply_convert_fusion.1 = (bf16[1024,3072]{1,0:T(8,128)(2,1)}, bf16[1024,3072]{1,0:T(8,128)(2,1)}) fusion(f32[1024,3072]{1,0:T(8,128)} %get-tuple-element.44, f32[1024,3072]{1,0:T(8,128)} %fusion.92, f32[1024,3072]{1,0:T(8,128)} %get-tuple-element.332, bf16[1024,1024]{1,0:T(8,128)(2,1)} %get-tuple-element.333, ...), kind=kOutput, calls=%fused_computation.23 | convolution fusion | flops 6483345408 | bytes 58720256 | tf_op jit(solution)/shard_map/dot_general | solution.py:24
  443.4 7.2 convolution_convert_fusion.1
  468.5 15.4 %all-to-all-done.6 = bf16[4,256,512]{1,2,0:T(8,128)(2,1)S(1)} async-done(((bf16[4,256,512]{1,2,0:T(8,128)(2,1)}), bf16[4,256,512]{1,2,0:T(8,128)(2,1)S(1)}, u32[]{:S(2)}, u32[]{:S(2)}) %all-to-all-start.6) | async-done | bytes 1048608 | tf_op jit(solution)/shard_map/all_to_all | solution.py:121
  488.4 12.3 %fusion.326 = f32[1024,3072]{1,0:T(8,128)} fusion(bf16[1024,1024]{1,0:T(8,128)(2,1)} %get-tuple-element.195, bf16[1024,3072]{1,0:T(8,128)(2,1)} %get-tuple-element.50), kind=kOutput, calls=%fused_computation.723 | convolution fusion | flops 6442450944 | bytes 20971520 | tf_op jit(solution)/shard_map/dot_general | solution.py:20
  517.3 14.2 %convolution_add_fusion = f32[1024,3072]{1,0:T(8,128)} fusion(f32[1024,3072]{1,0:T(8,128)} %fusion.326, bf16[1024,1024]{1,0:T(8,128)(2,1)} %copy-done.16, bf16[1024,3072]{1,0:T(8,128)(2,1)} %get-tuple-element.48), kind=kOutput, calls=%fused_computation.144 | convolution fusion | flops 6445596672 | bytes 33554432 | tf_op jit(solution)/shard_map/dot_general | solution.py:20
  531.5 9.9 %reshape.3229 = f32[32,98304]{1,0:T(8,128)} reshape(f32[1024,3072]{1,0:T(8,128)} %convolution_add_fusion) | data formatting | bytes 25165824 | tf_op jit(solution)/shard_map/reshape | solution.py:334
  557.9 10.5 %pad_maximum_fusion.1 = f32[32,114688]{1,0:T(8,128)} fusion(f32[32,16384]{1,0:T(8,128)} %reshape.3230, f32[32,98304]{1,0:T(8,128)} %reshape.3229), kind=kLoop, calls=%fused_computation.9 | loop fusion | flops 3670016 | bytes 29360128 | tf_op jit(solution)/shard_map/concatenate | solution.py:334
  568.5 18.8 %copy.108 = f32[8,4,112,1024]{3,2,1,0:T(8,128)} copy(f32[8,4,112,1024]{3,0,2,1:T(8,128)} %bitcast.1088) | data formatting | bytes 29360128 | tf_op jit(solution)/shard_map/transpose | solution.py:127
  593.3 9.7 %convolution_add_fusion.2 = f32[512,3072]{1,0:T(8,128)} fusion(f32[512,3072]{1,0:T(8,128)S(1)} %fusion.148, bf16[1024,3072]{1,0:T(8,128)(2,1)} %get-tuple-element.47, bf16[128,8,4,128]{3,2,1,0:T(4,128)(2,1)S(1)} %bitcast.1090), kind=kOutput, calls=%fused_computation.146 | convolution fusion | flops 3222798336 | bytes 19922944 | tf_op jit(solution)/shard_map/dot_general | solution.py:20
  603.1 7.6 reshape.3237
  610.7 10.0 %fusion.328 = f32[3072,1024]{1,0:T(8,128)S(1)} fusion(bf16[1024,3072]{1,0:T(8,128)(2,1)} %get-tuple-element.43, bf16[1024,1024]{1,0:T(8,128)(2,1)} %get-tuple-element.333), kind=kOutput, calls=%fused_computation.725 | convolution fusion | flops 6442450944 | bytes 20971520 | tf_op jit(solution)/shard_map/dot_general | solution.py:20
  620.8 9.8 %convolution_add_fusion.1 = f32[3072,1024]{1,0:T(8,128)} fusion(f32[3072,1024]{1,0:T(8,128)S(1)} %fusion.328, bf16[1024,3072]{1,0:T(8,128)(2,1)S(1)} %bitcast.1100, bf16[1024,1024]{1,0:T(8,128)(2,1)S(1)} %copy-done.114), kind=kOutput, calls=%fused_computation.145 | convolution fusion | flops 6445596672 | bytes 33554432 | tf_op jit(solution)/shard_map/dot_general | solution.py:20
  630.6 10.3 %reshape.3236 = f32[32,98304]{1,0:T(8,128)} reshape(f32[3072,1024]{1,0:T(8,128)} %convolution_add_fusion.1) | data formatting | bytes 25165824 | tf_op jit(solution)/shard_map/reshape | solution.py:278
  682.9 8.7 pad_maximum_fusion
  691.6 21.1 %copy.113 = f32[4,8,144,1024]{3,2,0,1:T(8,128)} copy(f32[4,8,144,1024]{3,1,2,0:T(8,128)S(1)} %bitcast.1086) | data formatting | bytes 37748736 | tf_op jit(solution)/shard_map/reshape;reshape | solution.py:127
  713.5 12.1 %fusion.86 = f32[1024,1024]{1,0:T(8,128)} fusion(bf16[1024,3072]{1,0:T(8,128)(2,1)} %get-tuple-element.48, bf16[1024,3712]{1,0:T(8,128)(2,1)} %all-gather.4.cloned.1.call-done), kind=kOutput, calls=%fused_computation.269 | convolution fusion | flops 6442450944 | bytes 16777216 | tf_op jit(solution)/shard_map/dot_general | solution.py:24
  725.6 12.3 %fusion.88 = f32[1024,1024]{1,0:T(8,128)} fusion(bf16[1024,3072]{1,0:T(8,128)(2,1)} %get-tuple-element.50, bf16[1024,3712]{1,0:T(8,128)(2,1)} %all-gather.4.cloned.1.call-done), kind=kOutput, calls=%fused_computation.271 | convolution fusion | flops 6442450944 | bytes 16777216 | tf_op jit(solution)/shard_map/dot_general | solution.py:24
  750.9 108.4 %reduce-scatter.12.cloned.1.call-done = f32[576,1024]{1,0:T(8,128)} async-done(((f32[4608,1024]{1,0:T(8,128)}), f32[576,1024]{1,0:T(8,128)}) %reduce-scatter.12.cloned.1.call-update) | async-done | bytes 2359312 | tf_op jit(solution)/shard_map/reduce_scatter | solution.py:128
  883.1 40.5 %psum.15 = f32[2176]{0:T(1024)S(1)} all-reduce(f32[2176]{0:T(1024)S(1)} %pad_maximum_fusion.5), channel_id=1, replica_groups=mesh['dp'=4,'fsdp'=8] {'dp','fsdp'}, use_global_device_ids=true, to_apply=%region_12.16 | all-reduce | flops 2176 | bytes 17408 | tf_op jit(solution)/shard_map/psum | solution.py:338
  936.0 15.0 %reduce-scatter.14.cloned.1.call-done = f32[144,1024]{1,0:T(8,128)} async-done(((f32[576,1024]{1,0:T(8,128)}), f32[144,1024]{1,0:T(8,128)}) %reduce-scatter.14.cloned.1.call-update) | async-done | bytes 589840 | tf_op jit(solution)/shard_map/reduce_scatter | solution.py:131
  (453 shorter events, 291.7 us)
Async XLA Ops:
  7.2 170.6 %all-gather.4.cloned.1.call-start = ((), (), s32[]{:S(2)}) async-start(), calls=%async_computation.15 | async-start | bytes 7839744 | tf_op jit(solution)/shard_map/all_gather | solution.py:186
  10.5 306.8 %all-gather.6.cloned.1.call-start = ((), (), s32[]{:S(2)}) async-start(), calls=%async_computation.16 | async-start | bytes 3244032 | tf_op jit(solution)/shard_map/all_gather | solution.py:189
  12.5 15.9 %all-to-all-start.4 = ((s32[2,4,256]{2,0,1:T(2,128)}), s32[2,4,256]{2,0,1:T(2,128)S(1)}, u32[]{:S(2)}, u32[]{:S(2)}) async-start(s32[2,4,256]{2,0,1:T(2,128)} %bitcast.186), calls=%async_computation.4 | async-start | bytes 16384 | tf_op jit(solution)/shard_map/all_to_all | solution.py:168
  18.9 314.9 %all-gather.8.cloned.1.call-start = ((), (), s32[]{:S(2)}) async-start(), calls=%async_computation.17 | async-start | bytes 6488064 | tf_op jit(solution)/shard_map/all_gather | solution.py:190
  25.3 153.8 %copy-start.83 = (f32[1,2,4,128]{3,1,2,0:T(2,128)}, f32[1,2,4,128]{3,1,2,0:T(2,128)S(1)}, u32[]{:S(2)}) copy-start(f32[1,2,4,128]{3,1,2,0:T(2,128)S(1)} %copy.124) | copy-start | bytes 12292
  25.3 153.8 %copy-start.85 = (f32[1,2,4,128]{3,1,2,0:T(2,128)}, f32[1,2,4,128]{3,1,2,0:T(2,128)S(1)}, u32[]{:S(2)}) copy-start(f32[1,2,4,128]{3,1,2,0:T(2,128)S(1)} %copy.123) | copy-start | bytes 12292
  25.3 153.8 %copy-start.87 = (f32[1,2,4,128]{3,1,2,0:T(2,128)}, f32[1,2,4,128]{3,1,2,0:T(2,128)S(1)}, u32[]{:S(2)}) copy-start(f32[1,2,4,128]{3,1,2,0:T(2,128)S(1)} %copy.128) | copy-start | bytes 12292
  28.4 164.6 %all-to-all-start.5 = ((bf16[2,4,256,1024]{3,2,0,1:T(8,128)(2,1)}), bf16[2,4,256,1024]{3,2,0,1:T(8,128)(2,1)}, u32[]{:S(2)}, u32[]{:S(2)}) async-start(bf16[2,4,256,1024]{3,2,0,1:T(8,128)(2,1)} %copy.103), calls=%async_computation.5 | async-start | bytes 8388608 | tf_op jit(solution)/shard_map/all_to_all | solution.py:165
  60.9 225.0 %copy-start.41 = (f32[256,128]{0,1:T(8,128)}, f32[256,128]{0,1:T(8,128)S(1)}, u32[]{:S(2)}) copy-start(f32[256,128]{0,1:T(8,128)S(1)} %get-tuple-element.221) | copy-start | bytes 393220
  60.9 225.4 %copy-start.35 = (f32[256,128]{0,1:T(8,128)}, f32[256,128]{0,1:T(8,128)S(1)}, u32[]{:S(2)}) copy-start(f32[256,128]{0,1:T(8,128)S(1)} %get-tuple-element.218) | copy-start | bytes 393220
  60.9 225.4 %copy-start.37 = (f32[256,128]{0,1:T(8,128)}, f32[256,128]{0,1:T(8,128)S(1)}, u32[]{:S(2)}) copy-start(f32[256,128]{0,1:T(8,128)S(1)} %get-tuple-element.219) | copy-start | bytes 393220
  60.9 225.4 %copy-start.39 = (f32[256,128]{0,1:T(8,128)}, f32[256,128]{0,1:T(8,128)S(1)}, u32[]{:S(2)}) copy-start(f32[256,128]{0,1:T(8,128)S(1)} %get-tuple-element.220) | copy-start | bytes 393220
  183.4 48.5 %copy-start.16 = (bf16[1024,1024]{1,0:T(8,128)(2,1)}, bf16[1024,1024]{1,0:T(8,128)(2,1)S(1)}, u32[]{:S(2)}) copy-start(bf16[1024,1024]{1,0:T(8,128)(2,1)S(1)} %get-tuple-element.196) | copy-start | bytes 6291460
  193.0 34.3 %all-to-all-start.2 = ((bf16[4,256,512]{1,2,0:T(8,128)(2,1)}), bf16[4,256,512]{1,2,0:T(8,128)(2,1)}, u32[]{:S(2)}, u32[]{:S(2)}) async-start(bf16[4,256,512]{1,2,0:T(8,128)(2,1)} %bitcast.1106), calls=%async_computation.2 | async-start | bytes 2097152 | tf_op jit(solution)/shard_map/all_to_all | solution.py:121
  197.3 136.4 %copy-start.93 = (f32[1,2,4,128]{3,1,2,0:T(2,128)}, f32[1,2,4,128]{3,1,2,0:T(2,128)S(1)}, u32[]{:S(2)}) copy-start(f32[1,2,4,128]{3,1,2,0:T(2,128)S(1)} %copy.132) | copy-start | bytes 12292
  197.4 207.2 %copy-start.91 = (f32[1,2,4,128]{3,1,2,0:T(2,128)}, f32[1,2,4,128]{3,1,2,0:T(2,128)S(1)}, u32[]{:S(2)}) copy-start(f32[1,2,4,128]{3,1,2,0:T(2,128)S(1)} %copy.130) | copy-start | bytes 12292
  227.4 39.4 %all-to-all-start = ((bf16[4,256,512]{1,2,0:T(8,128)(2,1)}), bf16[4,256,512]{1,2,0:T(8,128)(2,1)}, u32[]{:S(2)}, u32[]{:S(2)}) async-start(bf16[4,256,512]{1,2,0:T(8,128)(2,1)} %bitcast.1105), calls=%async_computation | async-start | bytes 2097152 | tf_op jit(solution)/shard_map/all_to_all | solution.py:121
  266.7 45.4 %all-to-all-start.3 = ((bf16[4,256,512]{1,2,0:T(8,128)(2,1)}), bf16[4,256,512]{1,2,0:T(8,128)(2,1)S(1)}, u32[]{:S(2)}, u32[]{:S(2)}) async-start(bf16[4,256,512]{1,2,0:T(8,128)(2,1)} %fusion.132), calls=%async_computation.3 | async-start | bytes 2097152 | tf_op jit(solution)/shard_map/all_to_all | solution.py:121
  312.1 69.1 %all-to-all-start.1 = ((bf16[4,256,512]{1,2,0:T(8,128)(2,1)}), bf16[4,256,512]{1,2,0:T(8,128)(2,1)}, u32[]{:S(2)}, u32[]{:S(2)}) async-start(bf16[4,256,512]{1,2,0:T(8,128)(2,1)} %fusion.129), calls=%async_computation.1 | async-start | bytes 2097152 | tf_op jit(solution)/shard_map/all_to_all | solution.py:121
  348.2 25.0 %copy-start.12 = (bf16[512,3072]{1,0:T(8,128)(2,1)S(1)}, bf16[512,3072]{1,0:T(8,128)(2,1)}, u32[]{:S(2)}) copy-start(bf16[512,3072]{1,0:T(8,128)(2,1)} %all-gather.6.cloned.1.call-done) | copy-start | bytes 9437188
  381.2 72.2 %all-to-all-start.8 = ((bf16[4,256,512]{1,2,0:T(8,128)(2,1)}), bf16[4,256,512]{1,2,0:T(8,128)(2,1)}, u32[]{:S(2)}, u32[]{:S(2)}) async-start(bf16[4,256,512]{1,2,0:T(8,128)(2,1)} %bitcast.60), calls=%async_computation.8 | async-start | bytes 2097152 | tf_op jit(solution)/shard_map/all_to_all | solution.py:121
  418.5 24.9 %copy-start.13 = (bf16[512,3072]{1,0:T(8,128)(2,1)S(1)}, bf16[512,3072]{1,0:T(8,128)(2,1)}, u32[]{:S(2)}) copy-start(bf16[512,3072]{1,0:T(8,128)(2,1)} %all-gather.6.cloned.1.call-done) | copy-start | bytes 9437188
  453.4 30.4 %all-to-all-start.6 = ((bf16[4,256,512]{1,2,0:T(8,128)(2,1)}), bf16[4,256,512]{1,2,0:T(8,128)(2,1)S(1)}, u32[]{:S(2)}, u32[]{:S(2)}) async-start(bf16[4,256,512]{1,2,0:T(8,128)(2,1)} %bitcast.51), calls=%async_computation.6 | async-start | bytes 2097152 | tf_op jit(solution)/shard_map/all_to_all | solution.py:121
  484.9 28.7 %all-to-all-start.9 = ((bf16[4,256,512]{1,2,0:T(8,128)(2,1)}), bf16[4,256,512]{1,2,0:T(8,128)(2,1)S(1)}, u32[]{:S(2)}, u32[]{:S(2)}) async-start(bf16[4,256,512]{1,2,0:T(8,128)(2,1)} %fusion.138), calls=%async_computation.9 | async-start | bytes 2097152 | tf_op jit(solution)/shard_map/all_to_all | solution.py:121
  513.6 29.4 %all-to-all-start.7 = ((bf16[4,256,512]{1,2,0:T(8,128)(2,1)}), bf16[4,256,512]{1,2,0:T(8,128)(2,1)S(1)}, u32[]{:S(2)}, u32[]{:S(2)}) async-start(bf16[4,256,512]{1,2,0:T(8,128)(2,1)} %fusion.135), calls=%async_computation.7 | async-start | bytes 2097152 | tf_op jit(solution)/shard_map/all_to_all | solution.py:121
  517.1 195.7 %reduce-scatter.8.cloned.1.call-start = ((), (), s32[]{:S(2)}) async-start(), calls=%async_computation.18 | async-start | bytes 16515072 | tf_op jit(solution)/shard_map/reduce_scatter | solution.py:128
  587.3 150.6 %reduce-scatter.16.cloned.1.call-start = ((), (), s32[]{:S(2)}) async-start(), calls=%async_computation.22 | async-start | bytes 589824
  603.1 17.7 %slice-start = ((s8[6291456]{0:T(1024)(128)(4,1)}), s8[2097152]{0:T(1024)(128)(4,1)S(1)}, s32[]{:S(2)}) async-start(s8[6291456]{0:T(1024)(128)(4,1)} %bitcast.1099), calls=%async_computation.23 | async-start | bytes 4194304
  682.8 176.5 %reduce-scatter.12.cloned.1.call-start = ((), (), s32[]{:S(2)}) async-start(), calls=%async_computation.20 | async-start | bytes 21233664 | tf_op jit(solution)/shard_map/reduce_scatter | solution.py:128
  712.7 219.9 %reduce-scatter.10.cloned.1.call-start = ((), (), s32[]{:S(2)}) async-start(), calls=%async_computation.19 | async-start | bytes 2293760 | tf_op jit(solution)/shard_map/reduce_scatter | solution.py:131
  713.5 237.5 %reduce-scatter.14.cloned.1.call-start = ((), (), s32[]{:S(2)}) async-start(), calls=%async_computation.21 | async-start | bytes 2949120 | tf_op jit(solution)/shard_map/reduce_scatter | solution.py:131
  743.6 115.7 %copy-start.29 = (bf16[1024,512]{1,0:T(8,128)(2,1)S(1)}, bf16[1024,512]{1,0:T(8,128)(2,1)}, u32[]{:S(2)}) copy-start(bf16[1024,512]{1,0:T(8,128)(2,1)} %copy-done.28) | copy-start | bytes 3145732
  (104 other events, 558.2 us)
Sparse Core Ops, SparseCore 0:
  11.4 125.7 all-gather.3
  140.1 74.3 all-gather.5
  217.3 93.1 all-gather.7
  587.4 104.7 reduce-scatter.7
  695.1 34.0 reduce-scatter.15
  733.1 126.1 reduce-scatter.11
  861.7 39.3 reduce-scatter.9
  903.5 47.4 reduce-scatter.13

commit v2 on v1

v2 whole, which is shorter than its diff:
```python
import functools

import numpy as np
import jax
import jax.numpy as jnp
from jax import lax
from jax.experimental import pallas as pl
from jax.experimental.pallas import tpu as pltpu
from jax.sharding import PartitionSpec as P

epsilon = 1e-05
highest = lax.Precision.HIGHEST
bf16 = jnp.bfloat16
f32 = jnp.float32
MESH = pl.DeviceIdType.MESH
ANY = pl.BlockSpec(memory_space=pl.ANY)


def bit_of(index, bit):
    return lax.rem(lax.div(index, 1 << bit), 2)


def flip(index, bit):
    return index + (1 << bit) - 2 * (1 << bit) * bit_of(index, bit)


def greet(dp_count, bits):
    d, f = lax.axis_index("dp"), lax.axis_index("fsdp")
    barrier = pltpu.get_barrier_semaphore()
    for o in range(1, dp_count):
        peer = lax.rem(d + o, dp_count)
        pl.semaphore_signal(barrier, inc=1, device_id={"dp": peer}, device_id_type=MESH)
    for b in range(bits):
        pl.semaphore_signal(barrier, inc=1, device_id={"fsdp": flip(f, b)}, device_id_type=MESH)
    pl.semaphore_wait(barrier, dp_count - 1 + bits)


def near_first(count):
    order = [0]
    for k in range(1, count // 2 + 1):
        order += [k] if k == count - k else [k, count - k]
    return order


def gather_body(dp_count, bits, n, *refs):
    ins, outs = refs[:n], refs[n : 2 * n]
    z_send, z_recv, send, recv, own_sem = refs[2 * n :]
    d, f = lax.axis_index("dp"), lax.axis_index("fsdp")
    cuts = []
    for x in ins:
        cut = x.shape[1] // 256 * 128
        cuts.append(((0, cut), (cut, x.shape[1] - cut)))
    greet(dp_count, bits)
    own = [
        pltpu.make_async_copy(ins[a], outs[a].at[d, f], own_sem.at[a]) for a in range(n)
    ]
    for copy in own:
        copy.start()
    started, arrived, waited = [], {}, set()
    order = near_first(dp_count)
    for o in order[1:]:
        for h in range(2):
            for a in range(n):
                lo, size = cuts[a][h]
                copy = pltpu.make_async_remote_copy(
                    src_ref=ins[a].at[:, pl.ds(lo, size)],
                    dst_ref=outs[a].at[d, f, :, pl.ds(lo, size)],
                    send_sem=z_send.at[o - 1, h, a],
                    recv_sem=z_recv.at[o - 1, h, a],
                    device_id={"dp": lax.rem(d + o, dp_count)},
                    device_id_type=MESH,
                )
                copy.start()
                started.append(copy)
                arrived[(o, 0, h, a)] = copy
    for copy in own:
        copy.wait()
    upper = list(range(1, bits))
    stages = [upper + [0], upper[::-1] + [0]]
    held = [[0], [0]]
    slot = 0
    for s in range(bits):
        fresh = [[], []]
        for mi in range(len(held[0])):
            for o in order:
                for h in range(2):
                    mask, b = held[h][mi], stages[h][s]
                    src_d = lax.rem(d - o + dp_count, dp_count)
                    src_f = f
                    for bb in range(bits):
                        if mask >> bb & 1:
                            src_f = flip(src_f, bb)
                    for a in range(n):
                        key = (o, mask, h, a)
                        if key in arrived and key not in waited:
                            arrived[key].wait_recv()
                            waited.add(key)
                        lo, size = cuts[a][h]
                        piece = outs[a].at[src_d, src_f, :, pl.ds(lo, size)]
                        copy = pltpu.make_async_remote_copy(
                            src_ref=piece,
                            dst_ref=piece,
                            send_sem=send.at[slot],
                            recv_sem=recv.at[slot],
                            device_id={"fsdp": flip(f, b)},
                            device_id_type=MESH,
                        )
                        copy.start()
                        started.append(copy)
                        arrived[(o, mask ^ (1 << b), h, a)] = copy
                        slot += 1
                    if o == 0:
                        fresh[h].append(mask ^ (1 << b))
        held = [held[h] + fresh[h] for h in range(2)]
    for key, copy in arrived.items():
        if key not in waited:
            copy.wait_recv()
    for copy in started:
        copy.wait_send()


def gather_all(arrays, collective_id):
    dp_count, fsdp_count = lax.axis_size("dp"), lax.axis_size("fsdp")
    bits = fsdp_count.bit_length() - 1
    n = len(arrays)
    slots = 2 * dp_count * (fsdp_count - 1) * n
    return pl.pallas_call(
        functools.partial(gather_body, dp_count, bits, n),
        out_shape=[
            jax.ShapeDtypeStruct((dp_count, fsdp_count, *x.shape), x.dtype) for x in arrays
        ],
        in_specs=[ANY] * n,
        out_specs=[ANY] * n,
        scratch_shapes=[
            pltpu.SemaphoreType.DMA((dp_count - 1, 2, n)),
            pltpu.SemaphoreType.DMA((dp_count - 1, 2, n)),
            pltpu.SemaphoreType.DMA((slots,)),
            pltpu.SemaphoreType.DMA((slots,)),
            pltpu.SemaphoreType.DMA((n,)),
        ],
        compiler_params=pltpu.CompilerParams(collective_id=collective_id, has_side_effects=True),
    )(*arrays)


def scatter_body(dp_count, bits, pieces, kinds, *refs):
    n_in, n = len(kinds), len(pieces)
    ins, outs = refs[:n_in], refs[n_in : 2 * n_in]
    per = 6 + 2 * (bits - 1)
    scratch = [refs[2 * n_in + i * per : 2 * n_in + (i + 1) * per] for i in range(n)]
    load_sem, send, recv, store_sem = refs[2 * n_in + n * per :]
    d, f = lax.axis_index("dp"), lax.axis_index("fsdp")
    my = [bit_of(f, b) for b in range(bits)]
    upper = list(range(bits - 1, 0, -1))
    waits, fixed, ends = [None] * n, [{} for _ in range(n)], []
    greet(dp_count, bits)

    def region(i, other=None):
        return (slice(None),) + tuple(
            1 - my[b] if b == other else fixed[i].get(b, slice(None)) for b in upper
        )

    def push(i, at, src, dst, device_id):
        copy = pltpu.make_async_remote_copy(
            src_ref=src,
            dst_ref=dst,
            send_sem=send.at[i, at],
            recv_sem=recv.at[i, at],
            device_id=device_id,
            device_id_type=MESH,
        )
        copy.start()
        ends.append(copy)
        return copy

    def first(i):
        op, lo, cols = pieces[i]
        lead = (slice(None),) * bits
        own = ins[op].at[(*lead, my[0], slice(None), pl.ds(lo, cols))]
        other = ins[op].at[(*lead, 1 - my[0], slice(None), pl.ds(lo, cols))]
        load = pltpu.make_async_copy(own, scratch[i][0], load_sem.at[i])
        load.start()
        waits[i] = (load, push(i, 0, other, scratch[i][1], {"fsdp": flip(f, 0)}))

    def arrive(i, s):
        acc = scratch[i][2]
        if s == 0:
            waits[i][0].wait()
            waits[i][1].wait_recv()
            acc[...] = scratch[i][0][...].astype(f32) + scratch[i][1][...].astype(f32)
        else:
            waits[i].wait_recv()
            here = region(i)
            acc[here] = acc[here] + scratch[i][5 + 2 * s][...].astype(f32)

    def middle(i, s):
        arrive(i, s - 1)
        b = (upper if i % 2 == 0 else upper[::-1])[s - 1]
        out_buf, in_buf = scratch[i][4 + 2 * s], scratch[i][5 + 2 * s]
        out_buf[...] = scratch[i][2][region(i, b)].astype(out_buf.dtype)
        waits[i] = push(i, s, out_buf, in_buf, {"fsdp": flip(f, b)})
        fixed[i][b] = my[b]

    def last(i):
        arrive(i, bits - 1)
        out_buf, in_buf = scratch[i][3], scratch[i][4]
        waits[i] = []
        for o in near_first(dp_count)[1:]:
            peer = lax.rem(d + o, dp_count)
            out_buf[o - 1] = scratch[i][2][(peer, *region(i)[1:])].astype(out_buf.dtype)
            waits[i].append(
                push(i, bits - 1 + o, out_buf.at[o - 1], in_buf.at[o - 1], {"dp": peer})
            )

    def finish(i):
        op, lo, cols = pieces[i]
        for copy in waits[i]:
            copy.wait_recv()
        total = scratch[i][2][(d, *region(i)[1:])]
        for o in range(1, dp_count):
            total = total + scratch[i][4][o - 1].astype(f32)
        scratch[i][5][...] = total
        store = pltpu.make_async_copy(
            scratch[i][5], outs[op].at[:, pl.ds(lo, cols)], store_sem.at[i]
        )
        store.start()
        return store

    stores = []
    for t in range((n + 1) // 2 + bits + 1):
        for i in range(n):
            s = t - i // 2
            if s == 0:
                first(i)
            elif 1 <= s < bits:
                middle(i, s)
            elif s == bits:
                last(i)
            elif s == bits + 1:
                stores.append(finish(i))
    for copy in ends:
        copy.wait_send()
    for store in stores:
        store.wait()


def scatter_all(arrays, splits, collective_id):
    dp_count, fsdp_count = lax.axis_size("dp"), lax.axis_size("fsdp")
    bits = fsdp_count.bit_length() - 1
    arrays = [a.reshape(dp_count, *(2,) * bits, *a.shape[1:]) for a in arrays]
    pieces, scratch = [], []
    for op, (a, k) in enumerate(zip(arrays, splits)):
        rows, cols = a.shape[-2], a.shape[-1] // k
        half = (dp_count, *(2,) * (bits - 1), rows, cols)
        for j in range(k):
            pieces.append((op, j * cols, cols))
            scratch += [pltpu.VMEM(half, a.dtype)] * 2 + [pltpu.VMEM(half, f32)]
            scratch += [pltpu.VMEM((dp_count - 1, rows, cols), a.dtype)] * 2
            scratch += [pltpu.VMEM((rows, cols), f32)]
            for s in range(1, bits):
                shape = (dp_count, *(2,) * (bits - 1 - s), rows, cols)
                scratch += [pltpu.VMEM(shape, a.dtype)] * 2
    n, steps = len(pieces), bits - 1 + dp_count
    return pl.pallas_call(
        functools.partial(scatter_body, dp_count, bits, pieces, [a.dtype for a in arrays]),
        out_shape=[jax.ShapeDtypeStruct(a.shape[-2:], f32) for a in arrays],
        in_specs=[ANY] * len(arrays),
        out_specs=[ANY] * len(arrays),
        scratch_shapes=scratch
        + [
            pltpu.SemaphoreType.DMA((n,)),
            pltpu.SemaphoreType.DMA((n, steps)),
            pltpu.SemaphoreType.DMA((n, steps)),
            pltpu.SemaphoreType.DMA((n,)),
        ],
        compiler_params=pltpu.CompilerParams(
            collective_id=collective_id, has_side_effects=True, vmem_limit_bytes=60 << 20
        ),
    )(*arrays)


def exchange(values):
    return lax.all_to_all(values, "dp", split_axis=0, concat_axis=0, tiled=True)


def params(limit_mib=60):
    return pltpu.CompilerParams(vmem_limit_bytes=limit_mib << 20)


def whole(shape):
    return pl.BlockSpec(shape, lambda i: (0,) * len(shape), pipeline_mode=pl.Buffered(1))


def matmul(left, right):
    return jnp.dot(left, right, preferred_element_type=f32)


def rows_inner(left, right):
    return lax.dot_general(left, right, (((0,), (0,)), ((), ())), preferred_element_type=f32)


def cols_inner(left, right):
    return lax.dot_general(left, right, (((1,), (1,)), ((), ())), preferred_element_type=f32)


def gelu_and_slope(values):
    phi = 0.5 * (1.0 + lax.erf(values * 0.7071067811865476))
    return (
        values * phi,
        phi + values * jnp.exp(-0.5 * values * values) * 0.3989422804014327,
    )


def centred_rows(tokens_ref, rows):
    inputs = tokens_ref[...].reshape(rows, tokens_ref.shape[-1]).astype(f32)
    centred = inputs - jnp.mean(inputs, axis=1, keepdims=True)
    variance = jnp.mean(centred * centred, axis=1, keepdims=True)
    return inputs, centred, lax.rsqrt(variance + epsilon)


def channels_from_rows(ref, values, seqs, chunk, own):
    for place in range(ref.shape[0]):
        for s in range(seqs):
            ref[place, :, s * own : (s + 1) * own] = values[
                s * chunk : (s + 1) * chunk, place * own : (place + 1) * own
            ].astype(ref.dtype)


def rows_from_channels(ref, scratch, seqs, chunk, own):
    for place in range(ref.shape[0]):
        for s in range(seqs):
            scratch[s * chunk : (s + 1) * chunk, place * own : (place + 1) * own] = ref[
                place, :, s * own : (s + 1) * own
            ]


def reduce_body(dims, tokens_ref, gain_ref, bias_ref, weight_ref, normed_ref, out_ref, slope_ref):
    seqs, chunk, own = dims
    _, centred, inverse_std = centred_rows(tokens_ref, seqs * chunk)
    normed = (centred * inverse_std * gain_ref[...] + bias_ref[...]).astype(bf16)
    normed_ref[...] = normed
    reduced, slope = gelu_and_slope(matmul(normed, weight_ref[...]))
    slope_ref[...] = slope
    channels_from_rows(out_ref, reduced, seqs, chunk, own)


def gate_body(tile, normed_ref, weight_ref, gate_ref, slope_ref):
    for j in range(gate_ref.shape[1] // tile):
        at = slice(j * tile, (j + 1) * tile)
        gate, slope = gelu_and_slope(matmul(normed_ref[...], weight_ref[:, at]))
        gate_ref[:, at] = gate.astype(bf16)
        slope_ref[:, at] = slope.astype(bf16)


def middle_body(
    dims, teachers, tile, order_ref, scale_ref, state_ref, gate_ref, slope_ref, expand_ref, weight_ref,
    tokens_ref, cotangent_ref, valid_ref, keep_ref, *refs,
):
    seqs, chunk, own = dims
    teach_refs, refs = refs[:teachers], refs[teachers:]
    (state_out_ref, product_ref, branch_grad_ref, expanded_grad_ref, gate_grad_ref, out_ref,
     full_grad_ref, error_ref, mixed_grad_ref, expanded_ref) = refs
    rows, width = seqs * chunk, tokens_ref.shape[-1]
    rows_from_channels(state_ref, state_out_ref, seqs, chunk, own)
    state_out = state_out_ref[...]
    tiles = [slice(j * tile, (j + 1) * tile) for j in range(gate_ref.shape[1] // tile)]
    branch = jnp.zeros((rows, width), f32)
    for at in tiles:
        expanded = matmul(state_out, expand_ref[:, at])
        expanded_ref[:, at] = expanded
        product = (expanded * gate_ref[:, at].astype(f32)).astype(bf16)
        product_ref[:, at] = product
        branch = branch + matmul(product, weight_ref[at, :])
    valid, keep = valid_ref[...], keep_ref[...]
    full = tokens_ref[...].reshape(rows, width).astype(f32) + valid * branch
    out_ref[...] = full.astype(bf16).reshape(out_ref.shape)
    errors = full - jnp.concatenate([t[0] for t in teach_refs], axis=0).astype(f32)
    error_ref[0] = jnp.sum((keep * errors * errors).reshape(rows // 8, 8, width), axis=0)
    full_grad = cotangent_ref[...].reshape(rows, width).astype(f32) + keep * errors * scale_ref[0]
    full_grad_ref[...] = full_grad
    branch_grad = (valid * full_grad).astype(bf16)
    branch_grad_ref[...] = branch_grad
    mixed_grad = jnp.zeros((rows, state_out.shape[1]), f32)
    for at in tiles:
        product_grad = cols_inner(branch_grad, weight_ref[at, :])
        expanded_grad = (product_grad * gate_ref[:, at].astype(f32)).astype(bf16)
        expanded_grad_ref[:, at] = expanded_grad
        gate_grad_ref[:, at] = (
            product_grad * expanded_ref[:, at] * slope_ref[:, at].astype(f32)
        ).astype(bf16)
        mixed_grad = mixed_grad + cols_inner(expanded_grad, expand_ref[:, at])
    channels_from_rows(mixed_grad_ref, mixed_grad, seqs, chunk, own)


def input_body(
    dims, back_ref, slope_ref, gate_grad_ref, gate_weight_ref, reduce_weight_ref, tokens_ref,
    gain_ref, full_grad_ref, out_ref, reduced_grad_ref, gain_grad_ref, bias_grad_ref, back_rows_ref,
):
    seqs, chunk, own = dims
    rows, width = seqs * chunk, tokens_ref.shape[-1]
    rows_from_channels(back_ref, back_rows_ref, seqs, chunk, own)
    reduced_grad = (back_rows_ref[...].astype(f32) * slope_ref[...]).astype(bf16)
    reduced_grad_ref[...] = reduced_grad
    normed_grad = cols_inner(gate_grad_ref[...], gate_weight_ref[...]) + cols_inner(
        reduced_grad, reduce_weight_ref[...]
    )
    _, centred, inverse_std = centred_rows(tokens_ref, rows)
    unit = centred * inverse_std
    gain_grad_ref[0] = jnp.sum((normed_grad * unit).reshape(rows // 8, 8, width), axis=0)
    bias_grad_ref[0] = jnp.sum(normed_grad.reshape(rows // 8, 8, width), axis=0)
    unit_grad = normed_grad * gain_ref[...]
    result = full_grad_ref[...] + inverse_std * (
        unit_grad
        - jnp.mean(unit_grad, axis=1, keepdims=True)
        - unit * jnp.mean(unit_grad * unit, axis=1, keepdims=True)
    )
    out_ref[...] = result.astype(bf16).reshape(out_ref.shape)


def weight_grad_body(n, *refs):
    lefts, rights, out_ref = refs[:n], refs[n : 2 * n], refs[2 * n]
    total = rows_inner(lefts[0][...], rights[0][...])
    for left, right in zip(lefts[1:], rights[1:]):
        total = total + rows_inner(left[...], right[...])
    out_ref[...] = total.astype(out_ref.dtype)


def weight_grad(lefts, rights, row_tile):
    n, (rows, height), width = len(lefts), lefts[0].shape, rights[0].shape[1]
    return pl.pallas_call(
        functools.partial(weight_grad_body, n),
        grid=(height // row_tile,),
        out_shape=jax.ShapeDtypeStruct((height, width), bf16),
        in_specs=[pl.BlockSpec((rows, row_tile), lambda i: (0, i))] * n + [whole((rows, width))] * n,
        out_specs=pl.BlockSpec((row_tile, width), lambda i: (i, 0)),
        compiler_params=params(),
        cost_estimate=pl.CostEstimate(
            flops=2 * n * rows * height * width,
            bytes_accessed=2 * (n * rows * (height + width) + height * width),
            transcendentals=0,
        ),
    )(*lefts, *rights)


def fourier_table(chunk):
    freq = np.arange(chunk)[:, None]
    time = np.arange(chunk)[None, :]
    angle = (freq * time % (2 * chunk)) * (np.pi / chunk)
    sines = -np.sin(angle)
    sines[0] = 1.0 - 2.0 * (np.arange(chunk) % 2)
    table = np.concatenate([np.cos(angle), sines], axis=0)
    scaling = np.full((2 * chunk, 1), 1.0 / chunk)
    scaling[0] = scaling[chunk] = 0.5 / chunk
    sign = np.tile(1.0 - 2.0 * (np.arange(chunk) % 2), 2)
    sign[chunk] = 1.0 - 2.0 * (chunk % 2)
    return table.astype(np.float32), (table * scaling).astype(np.float32), sign.astype(np.float32)


def high_and_low(table):
    high = table.astype(jnp.bfloat16)
    return np.stack([high, (table - high.astype(np.float32)).astype(jnp.bfloat16)])


def spectrum(table_ref, values):
    return matmul(table_ref[0], values) + matmul(table_ref[1], values)


def to_time(inverse_ref, spec):
    high = spec.astype(bf16)
    low = (spec - high.astype(f32)).astype(bf16)
    return (
        rows_inner(inverse_ref[0], high)
        + rows_inner(inverse_ref[1], high)
        + rows_inner(inverse_ref[0], low)
    )


def packed_product(first, second, edge, conjugate):
    (a_re, a_im), (b_re, b_im) = first, second
    straight, crossed = a_re * b_re, a_im * b_im
    if conjugate:
        real = straight + jnp.where(edge, 0.0, crossed)
        imag = jnp.where(edge, crossed, a_re * b_im - a_im * b_re)
    else:
        real = straight - jnp.where(edge, 0.0, crossed)
        imag = jnp.where(edge, crossed, a_re * b_im + a_im * b_re)
    return real, imag


def pair_sum(pairs, edge, conjugate):
    real, imag = packed_product(*pairs[0], edge, conjugate)
    for first, second in pairs[1:]:
        more = packed_product(first, second, edge, conjugate)
        real, imag = real + more[0], imag + more[1]
    return real, imag


def halves(ref, block, at, chunk):
    return ref[block, :chunk, at], ref[block, chunk:, at]


def convolve_body(table_ref, inverse_ref, kernel_ref, rows_ref, out_ref, spec_ref, back_ref):
    blocks, chunk, columns = rows_ref.shape
    lanes = kernel_ref.shape[2]
    edge = lax.broadcasted_iota(jnp.int32, (chunk, lanes), 0) == 0
    for c in range(blocks):
        spec_ref[c] = spectrum(table_ref, rows_ref[c])
        for g in range(columns // lanes):
            at = slice(g * lanes, (g + 1) * lanes)
            everything = slice(None)
            real, imag = pair_sum(
                [
                    (halves(kernel_ref, k, everything, chunk), halves(spec_ref, c - k, at, chunk))
                    for k in range(c + 1)
                ],
                edge,
                False,
            )
            back_ref[:chunk, at], back_ref[chunk:, at] = real, imag
        out_ref[c] = to_time(inverse_ref, back_ref[...]).astype(out_ref.dtype)


def convolve_back_body(
    table_ref, inverse_ref, kernel_ref, rows_ref, grad_ref, out_ref, kernel_grad_ref,
    spec_ref, grad_spec_ref, back_ref,
):
    blocks, chunk, columns = rows_ref.shape
    lanes = kernel_ref.shape[2]
    edge = lax.broadcasted_iota(jnp.int32, (chunk, lanes), 0) == 0
    everything = slice(None)
    groups = [slice(g * lanes, (g + 1) * lanes) for g in range(columns // lanes)]
    for c in range(blocks):
        spec_ref[c] = spectrum(table_ref, rows_ref[c])
    for c in reversed(range(blocks)):
        grad_spec_ref[c] = spectrum(table_ref, grad_ref[c])
        for at in groups:
            real, imag = pair_sum(
                [
                    (
                        halves(kernel_ref, late - c, everything, chunk),
                        halves(grad_spec_ref, late, at, chunk),
                    )
                    for late in range(c, blocks)
                ],
                edge,
                True,
            )
            back_ref[:chunk, at], back_ref[chunk:, at] = real, imag
        out_ref[c] = to_time(inverse_ref, back_ref[...]).astype(out_ref.dtype)
    for k in range(blocks):
        real, imag = pair_sum(
            [
                (halves(spec_ref, c - k, at, chunk), halves(grad_spec_ref, c, at, chunk))
                for c in range(k, blocks)
                for at in groups
            ],
            edge,
            True,
        )
        kernel_grad_ref[k, :chunk], kernel_grad_ref[k, chunk:] = real, imag


def kernel_factors(decay, frequency, log_step, length):
    fine = 32
    coarse = length // fine
    step_size = jnp.exp(log_step)[:, None]
    real = (step_size * decay)[:, None, :]
    imag = (step_size * frequency)[:, None, :]
    far = (jnp.arange(coarse, dtype=jnp.int32) * fine).astype(f32)[None, :, None]
    near = jnp.arange(fine, dtype=jnp.int32).astype(f32)[None, :, None]
    far_damp, near_damp = jnp.exp(real * far), jnp.exp(real * near)
    return (
        (far_damp * jnp.cos(imag * far), far_damp * jnp.sin(imag * far)),
        (near_damp * jnp.cos(imag * near), near_damp * jnp.sin(imag * near)),
        step_size,
    )


def kernel_forward(weight_pair, factors):
    (far_re, far_im), (near_re, near_im), _ = factors
    w_re, w_im = weight_pair[0][:, None, :], weight_pair[1][:, None, :]
    left = jnp.concatenate([far_re, -far_im], axis=2)
    right = jnp.concatenate(
        [w_re * near_re - w_im * near_im, w_re * near_im + w_im * near_re], axis=2
    )
    rows = jnp.einsum("han,hbn->hab", left, right, precision=highest)
    return rows.reshape(rows.shape[0], -1)


def kernel_backward(grad_rows, weight_pair, decay, frequency, factors):
    (far_re, far_im), (near_re, near_im), step_size = factors
    channels, coarse, states = far_re.shape
    fine = near_re.shape[1]
    tiles = grad_rows.reshape(channels, coarse, fine)
    near_index = jnp.arange(fine, dtype=jnp.int32).astype(f32)
    far_index = (jnp.arange(coarse, dtype=jnp.int32) * fine).astype(f32)[None, :, None]
    stacked = jnp.concatenate([tiles, tiles * near_index], axis=1)
    part = jnp.einsum(
        "hab,hbn->han", stacked, jnp.concatenate([near_re, near_im], axis=2), precision=highest
    )
    u_re, u_im = part[:, :coarse, :states], part[:, :coarse, states:]
    v_re = part[:, coarse:, :states] + far_index * u_re
    v_im = part[:, coarse:, states:] + far_index * u_im
    s_re = jnp.sum(far_re * u_re - far_im * u_im, axis=1)
    s_im = jnp.sum(far_re * u_im + far_im * u_re, axis=1)
    t_re = jnp.sum(far_re * v_re - far_im * v_im, axis=1)
    t_im = jnp.sum(far_re * v_im + far_im * v_re, axis=1)
    w_re, w_im = weight_pair[0], weight_pair[1]
    along_re = step_size * (w_re * t_re - w_im * t_im)
    along_im = -step_size * (w_re * t_im + w_im * t_re)
    return (
        jnp.stack([s_re, -s_im]),
        along_re,
        along_im,
        jnp.sum(decay * along_re + frequency * along_im, axis=1),
    )


def shards(
    tokens,
    cotangent,
    teacher,
    lengths,
    dealing,
    loss_mask,
    norm_gain,
    norm_bias,
    gate_weight,
    reduce_weight,
    state_weight,
    decay_rate,
    frequency,
    log_step,
    expand_weight,
    out_weight,
):
    dp_count, fsdp_count = lax.axis_size("dp"), lax.axis_size("fsdp")
    devices = dp_count * fsdp_count
    group_index = lax.axis_index("fsdp")
    dp_place = lax.axis_index("dp")
    micro_count, seqs, chunk, width = tokens.shape
    rows = seqs * chunk
    seq_length = chunk * dp_count
    gate_width = gate_weight.shape[1]
    reduced_width = reduce_weight.shape[1]
    own = reduced_width // dp_count
    lanes = max(own, 128)
    share = norm_gain.shape[0]
    micros = range(micro_count)
    direct = own % 128 == 0

    small = jnp.zeros((16, 256), bf16).at[0, :share].set(norm_gain).at[1, :share].set(norm_bias)
    first, small = gather_all([jnp.concatenate([gate_weight, reduce_weight], axis=1), small], 1)
    first = first.reshape(width, gate_width + reduced_width)
    gain_row = small[:, :, 0, :share].reshape(1, width).astype(f32)
    bias_row = small[:, :, 1, :share].reshape(1, width).astype(f32)

    per_block = max(1, 512 // chunk)
    steps = seqs // per_block
    middle_block = max(1, 256 // chunk)
    middle_steps = seqs // middle_block

    def sequence_spec(count):
        return pl.BlockSpec((count, chunk, width), lambda i, *_: (i, 0, 0))

    def row_spec(columns, count=per_block):
        return pl.BlockSpec((count * chunk, columns), lambda i, *_: (i, 0))

    def shared(shape, block):
        return pl.BlockSpec(shape, lambda i, *_: block, pipeline_mode=pl.Buffered(1))

    lane_shape = (dp_count, chunk, seqs * own)
    if not direct:
        lane_shape = (1, rows, reduced_width)

    def dims(count):
        return (count, chunk, own) if direct else (1, count * chunk, reduced_width)

    def lane_spec(count):
        if direct:
            return pl.BlockSpec((dp_count, chunk, count * own), lambda i, *_: (0, 0, i))
        return pl.BlockSpec((1, count * chunk, reduced_width), lambda i, *_: (0, i, 0))

    def tokens_spec(m, count):
        return pl.BlockSpec((None, count, chunk, width), lambda i, *_: (m, i, 0, 0))

    def send_lanes(values):
        if not direct:
            values = values.reshape(seqs, chunk, dp_count, own).transpose(2, 1, 0, 3)
            values = values.reshape(dp_count, chunk, seqs * own)
        return exchange(values)

    def receive_lanes(values):
        values = exchange(values)
        if not direct:
            values = values.reshape(dp_count, chunk, seqs, own).transpose(2, 1, 0, 3)
            values = values.reshape(1, rows, reduced_width)
        return values

    def reduce_rows(m):
        return pl.pallas_call(
            functools.partial(reduce_body, dims(per_block)),
            grid=(steps,),
            out_shape=[
                jax.ShapeDtypeStruct((rows, width), bf16),
                jax.ShapeDtypeStruct(lane_shape, bf16),
                jax.ShapeDtypeStruct((rows, reduced_width), f32),
            ],
            in_specs=[
                tokens_spec(m, per_block),
                whole((1, width)),
                whole((1, width)),
                shared((width, reduced_width), (0, gate_width // reduced_width)),
            ],
            out_specs=[row_spec(width), lane_spec(per_block), row_spec(reduced_width)],
            compiler_params=params(),
            cost_estimate=pl.CostEstimate(
                flops=2 * rows * width * reduced_width,
                bytes_accessed=8 * rows * width,
                transcendentals=2 * rows * reduced_width,
            ),
        )(tokens, gain_row, bias_row, first)

    def gate_rows(normed):
        return pl.pallas_call(
            functools.partial(gate_body, 512),
            grid=(steps,),
            out_shape=[jax.ShapeDtypeStruct((rows, gate_width), bf16)] * 2,
            in_specs=[row_spec(width), shared((width, gate_width), (0, 0))],
            out_specs=[row_spec(gate_width)] * 2,
            compiler_params=params(),
            cost_estimate=pl.CostEstimate(
                flops=2 * rows * width * gate_width,
                bytes_accessed=4 * rows * gate_width + 2 * width * gate_width,
                transcendentals=2 * rows * gate_width,
            ),
        )(normed, first)

    normed, lanes_out, slope_reduced = zip(*[reduce_rows(m) for m in micros])
    lanes_in = [send_lanes(x) for x in lanes_out]

    teach = [
        exchange(teacher[m].reshape(dp_count, chunk, width)) for m in micros
    ]
    masked = lax.all_to_all(
        loss_mask.reshape(micro_count, dp_count, chunk), "dp", split_axis=1, concat_axis=1, tiled=True
    )
    local_ids = group_index * seqs + jnp.arange(seqs, dtype=jnp.int32)
    targets = jnp.take(dealing, local_ids, axis=1)
    own_lengths = jnp.take(lengths, local_ids, axis=1)
    positions = dp_place * chunk + jnp.arange(chunk, dtype=jnp.int32)
    valid = (positions[None, None, :] < own_lengths[:, :, None]).astype(f32)
    keep = jnp.take_along_axis(masked, targets[:, :, None], axis=1).astype(f32) * valid
    own_count = jnp.sum(keep)
    valid = valid.reshape(micro_count, rows, 1)
    keep = keep.reshape(micro_count, rows, 1)

    w_expand, w_out, counts = gather_all(
        [expand_weight, out_weight, jnp.full((8, 256), own_count, f32)], 2
    )
    w_expand = w_expand.reshape(reduced_width, gate_width)
    w_out = w_out.reshape(gate_width, width)
    count = jnp.sum(counts[:, :, 0, 0])
    error_scale = (2.0 / (width * count)).reshape(1)

    table_np, inverse_np, sign_np = fourier_table(chunk)
    sign = jnp.asarray(sign_np)[:, None]
    table2, inverse2 = jnp.asarray(high_and_low(table_np)), jnp.asarray(high_and_low(inverse_np))
    factors = kernel_factors(decay_rate, frequency, log_step, seq_length)
    own_kernel = kernel_forward(state_weight, factors)
    kernel = lax.all_gather(own_kernel, "fsdp", axis=0, tiled=True)
    segments = jnp.einsum(
        "kt,hct->ckh", jnp.asarray(table_np), kernel.reshape(own, dp_count, chunk), precision=highest
    )
    previous = jnp.concatenate([jnp.zeros_like(segments[:1]), segments[:-1]], axis=0)
    kernel_spec = jnp.tile(segments + sign * previous, (1, 1, lanes // own))

    blocks = (dp_count, chunk, seqs * own)
    spec_scratch = pltpu.VMEM((dp_count, 2 * chunk, seqs * own), f32)
    back_scratch = pltpu.VMEM((2 * chunk, seqs * own), f32)
    transform_flops = 8 * chunk * chunk * dp_count * seqs * own

    def convolve(values):
        return pl.pallas_call(
            convolve_body,
            out_shape=jax.ShapeDtypeStruct(blocks, bf16),
            scratch_shapes=[spec_scratch, back_scratch],
            compiler_params=params(),
            cost_estimate=pl.CostEstimate(
                flops=5 * transform_flops // 2, bytes_accessed=8 << 20, transcendentals=0
            ),
        )(table2, inverse2, kernel_spec, values)

    def convolve_back(values, grads):
        return pl.pallas_call(
            convolve_back_body,
            out_shape=[
                jax.ShapeDtypeStruct(blocks, bf16),
                jax.ShapeDtypeStruct((dp_count, 2 * chunk, lanes), f32),
            ],
            scratch_shapes=[spec_scratch, spec_scratch, back_scratch],
            compiler_params=params(),
            cost_estimate=pl.CostEstimate(
                flops=7 * transform_flops // 2, bytes_accessed=8 << 20, transcendentals=0
            ),
        )(table2, inverse2, kernel_spec, values, grads)

    mixed = [receive_lanes(convolve(x)) for x in lanes_in]
    gates = [gate_rows(x) for x in normed]

    def middle_rows(m):
        teach_specs = [
            pl.BlockSpec((1, chunk, width), functools.partial(teach_block, s)) for s in range(middle_block)
        ]
        wide, narrow = row_spec(gate_width, middle_block), row_spec(width, middle_block)
        return pl.pallas_call(
            functools.partial(middle_body, dims(middle_block), middle_block, 768),
            grid_spec=pltpu.PrefetchScalarGridSpec(
                num_scalar_prefetch=2,
                grid=(middle_steps,),
                in_specs=[
                    lane_spec(middle_block),
                    wide,
                    wide,
                    shared((reduced_width, gate_width), (0, 0)),
                    shared((gate_width, width), (0, 0)),
                    tokens_spec(m, middle_block),
                    tokens_spec(m, middle_block),
                    row_spec(1, middle_block),
                    row_spec(1, middle_block),
                    *teach_specs,
                ],
                out_specs=[
                    row_spec(reduced_width, middle_block),
                    wide,
                    narrow,
                    wide,
                    wide,
                    sequence_spec(middle_block),
                    narrow,
                    pl.BlockSpec((1, 8, width), lambda i, *_: (i, 0, 0)),
                    lane_spec(middle_block),
                ],
                scratch_shapes=[pltpu.VMEM((middle_block * chunk, gate_width), f32)],
            ),
            out_shape=[
                jax.ShapeDtypeStruct((rows, reduced_width), bf16),
                jax.ShapeDtypeStruct((rows, gate_width), bf16),
                jax.ShapeDtypeStruct((rows, width), bf16),
                jax.ShapeDtypeStruct((rows, gate_width), bf16),
                jax.ShapeDtypeStruct((rows, gate_width), bf16),
                jax.ShapeDtypeStruct((seqs, chunk, width), bf16),
                jax.ShapeDtypeStruct((rows, width), f32),
                jax.ShapeDtypeStruct((middle_steps, 8, width), f32),
                jax.ShapeDtypeStruct(lane_shape, bf16),
            ],
            compiler_params=params(),
            cost_estimate=pl.CostEstimate(
                flops=4 * rows * gate_width * (width + reduced_width),
                bytes_accessed=10 * rows * gate_width + 16 * rows * width,
                transcendentals=0,
            ),
        )(
            targets[m], error_scale, mixed[m], *gates[m], w_expand, w_out, tokens, cotangent,
            valid[m], keep[m], *[teach[m]] * middle_block,
        )

    def teach_block(s, i, order, scale):
        return (order[i * middle_block + s], 0, 0)

    def input_rows(m, back, gate_grad, full_grad):
        eight = pl.BlockSpec((1, 8, width), lambda i, *_: (i, 0, 0))
        return pl.pallas_call(
            functools.partial(input_body, dims(per_block)),
            grid=(steps,),
            in_specs=[
                lane_spec(per_block),
                row_spec(reduced_width),
                row_spec(gate_width),
                shared((width, gate_width), (0, 0)),
                shared((width, reduced_width), (0, gate_width // reduced_width)),
                tokens_spec(m, per_block),
                whole((1, width)),
                row_spec(width),
            ],
            out_specs=[sequence_spec(per_block), row_spec(reduced_width), eight, eight],
            out_shape=[
                jax.ShapeDtypeStruct((seqs, chunk, width), bf16),
                jax.ShapeDtypeStruct((rows, reduced_width), bf16),
                jax.ShapeDtypeStruct((steps, 8, width), f32),
                jax.ShapeDtypeStruct((steps, 8, width), f32),
            ],
            scratch_shapes=[pltpu.VMEM((per_block * chunk, reduced_width), bf16)],
            compiler_params=params(),
            cost_estimate=pl.CostEstimate(
                flops=2 * rows * width * (gate_width + reduced_width),
                bytes_accessed=4 * rows * gate_width + 8 * rows * width,
                transcendentals=0,
            ),
        )(back, slope_reduced[m], gate_grad, first, first, tokens, gain_row, full_grad)

    middle = [middle_rows(m) for m in micros]
    state_out, product, branch_grad, expanded_grad, gate_grad, outputs, full_grad, error_rows, lane_grad = zip(*middle)
    grads_in = [send_lanes(x) for x in lane_grad]
    back, kernel_grads = zip(*[convolve_back(lanes_in[m], grads_in[m]) for m in micros])
    back = [receive_lanes(x) for x in back]
    out_grad = weight_grad(product, branch_grad, 512)
    expand_grad = weight_grad(state_out, expanded_grad, 256)
    gate_weight_grad = weight_grad(normed, gate_grad, 256)
    ends = [input_rows(m, back[m], gate_grad[m], full_grad[m]) for m in micros]
    returned, reduced_grad, gain_rows, bias_rows = zip(*ends)
    reduce_grad = weight_grad(normed, reduced_grad, 512)

    kernel_total = sum(kernel_grads)
    if not direct:
        kernel_total = kernel_total.reshape(dp_count, 2 * chunk, lanes // own, own).sum(axis=2)
    following = jnp.concatenate([kernel_total[1:], jnp.zeros_like(kernel_total[:1])], axis=0)
    kernel_grad = jnp.einsum(
        "kt,ckh->hct", jnp.asarray(inverse_np), kernel_total + sign * following, precision=highest
    ).reshape(own, seq_length)
    kernel_grad = lax.psum_scatter(kernel_grad, "fsdp", scatter_dimension=0, tiled=True)
    pair_grad, decay_grad, frequency_grad, step_grad = kernel_backward(
        kernel_grad, state_weight, decay_rate, frequency, factors
    )

    gain_total = jnp.sum(sum(gain_rows), axis=(0, 1)).reshape(devices, 1, share)
    bias_total = jnp.sum(sum(bias_rows), axis=(0, 1)).reshape(devices, 1, share)
    error_total = jnp.full((devices, 1, share), jnp.sum(sum(error_rows)))
    sums = jnp.concatenate([gain_total, bias_total, error_total], axis=1)
    sums = jnp.pad(sums, ((0, 0), (0, 5), (0, 128 - share)))
    out_sum, expand_sum, gate_sum, reduce_sum, sums = scatter_all(
        [
            out_grad.reshape(devices, -1, width),
            expand_grad.reshape(devices, -1, gate_width),
            gate_weight_grad.reshape(devices, -1, gate_width),
            reduce_grad.reshape(devices, -1, reduced_width),
            sums,
        ],
        [4, 2, 4, 1, 1],
        3,
    )
    loss_value = sums[2, 0] / (width * count)
    return (
        jnp.stack(outputs),
        loss_value,
        jnp.stack(returned),
        sums[0, :share],
        sums[1, :share],
        gate_sum,
        reduce_sum,
        pair_grad,
        decay_grad,
        frequency_grad,
        step_grad,
        expand_sum,
        out_sum,
    )


def solution(mesh):
    in_specs = (
        P(None, "fsdp", "dp", None),
        P(None, "fsdp", "dp", None),
        P(None, ("dp", "fsdp"), None, None),
        P(),
        P(),
        P(None, ("dp", "fsdp"), None),
        P(("dp", "fsdp")),
        P(("dp", "fsdp")),
        P(("dp", "fsdp"), None),
        P(("dp", "fsdp"), None),
        P(None, ("dp", "fsdp"), None),
        P(("dp", "fsdp"), None),
        P(("dp", "fsdp"), None),
        P(("dp", "fsdp")),
        P(("dp", "fsdp"), None),
        P(("dp", "fsdp"), None),
    )
    out_specs = (
        P(None, "fsdp", "dp", None),
        P(),
        P(None, "fsdp", "dp", None),
        P(("dp", "fsdp")),
        P(("dp", "fsdp")),
        P(("dp", "fsdp"), None),
        P(("dp", "fsdp"), None),
        P(None, ("dp", "fsdp"), None),
        P(("dp", "fsdp"), None),
        P(("dp", "fsdp"), None),
        P(("dp", "fsdp")),
        P(("dp", "fsdp"), None),
        P(("dp", "fsdp"), None),
    )
    return jax.shard_map(shards, mesh=mesh, in_specs=in_specs, out_specs=out_specs, check_vma=False)
```

time: 973 us -> 729 us (0.75)
  Pallas kernels: 0 us -> 449 us
  matrix products: 287 us -> 12.4 us
  blocking collectives: 159 us -> 10.4 us
  local copies, waits for them, and re-layouts: 147 us -> 36.3 us
  other arithmetic: 119 us -> 40.1 us
  waiting for transfers between devices: 183 us -> 105 us
    pallas_call x0 -> x19, Pallas kernels: none -> 449 us  [the longest x2 119 us: gather_all(): pl.pallas_call(functools.partial(gather_body, dp_count, bits, n), out_sha...]
    dot_general x34 -> x2, matrix products: 281 us -> 4.96 us  [the longest x1 2.71 us: shards(): jnp.einsum('kt,ckh->hct', jnp.asarray(inverse_np), kernel_total + sign *...]
    psum x2 -> x0, blocking collectives: 149 us -> none  [the longest x1 109 us: shards(): count = lax.psum(jnp.sum(keep), both)]
    reduce_scatter x4 -> x0, waiting for transfers between devices: 123 us -> none  [the longest x2 108 us: scatter_sum(): lax.psum_scatter(tiles.reshape(-1, width), 'fsdp', scatter_dimension=0, t...]
    reshape x10 -> x2, local copies, waits for them, and re-layouts: 37.6 us -> 0.17 us  [the longest x1 0.09 us: shards(): gain_total = jnp.sum(sum(gain_rows), axis=(0, 1)).reshape(devices, 1, share)]
    all_to_all x8 -> x10, waiting for transfers between devices: 57.8 us -> 87.6 us  [exchange(): return lax.all_to_all(values, 'dp', split_axis=0, concat_axis=0, tiled=True)]
    concatenate x6 -> x2, other arithmetic: 30.7 us -> 1.73 us  [the longest x1 1.65 us: shards(): jnp.concatenate([gate_weight, reduce_weight], axis=1)]
    another operation x1 -> x0, local copies, waits for them, and re-layouts: 21.1 us -> none  [scatter_sum(): values.reshape(dp_count, fsdp_count, height, width).transpose(1, 0, 2, 3)]
  transfers between devices with their start and end apart: 18 -> 12, of which waited for: 7 -> 4; matrix products, arithmetic and copies ran while one was open for 51% -> 10% of each run, Pallas kernels for 0% -> 46%
where the time goes in v2:
time: 729 us; the launch traced here: 723 us
  Pallas kernels  449 us (62%)
  waiting for transfers between devices  105 us (14%)
  starting transfers between devices  52.2 us (7%)
  other arithmetic  40.1 us (6%)
  local copies, waits for them, and re-layouts  36.3 us (5%)
  between operations  17.5 us (2%)
  matrix products  12.4 us (2%)
  blocking collectives  10.4 us (1%)
    pallas_call x2, Pallas kernels, gather_all(): pl.pallas_call(functools.partial(gather_body, dp_count, bits, n), out_sha...  119 us
    pallas_call x1, Pallas kernels, scatter_all(): pl.pallas_call(functools.partial(scatter_body, dp_count, bits, pieces, [a...  95.3 us
    all_to_all x10, waiting for transfers between devices, exchange(): return lax.all_to_all(values, 'dp', split_axis=0, concat_axis=0, tiled=True)  87.6 us
    pallas_call x2, Pallas kernels, middle_rows(): pl.pallas_call(functools.partial(middle_body, dims(middle_block), middle_...  64.6 us
    pallas_call x4, Pallas kernels, weight_grad(): pl.pallas_call(functools.partial(weight_grad_body, n), grid=(height // ro...  57.2 us
    all_to_all x10, starting transfers between devices, exchange(): return lax.all_to_all(values, 'dp', split_axis=0, concat_axis=0, tiled=True)  45.8 us
    pallas_call x2, Pallas kernels, input_rows(): pl.pallas_call(functools.partial(input_body, dims(per_block)), grid=(step...  34.1 us
    pallas_call x2, Pallas kernels, gate_rows(): pl.pallas_call(functools.partial(gate_body, 512), grid=(steps,), out_shap...  33.2 us
  transfers between devices with their start and end apart: 12, of which 4 were waited for; matrix products, arithmetic and copies ran while one was open for 10% of the time, Pallas kernels for 46%

profile of v2, /device:TPU:0, one launch (start us, length us, event | category | flops | bytes accessed | tf_op | source)
XLA Modules:
  0.0 722.5 jit_solution(5045785365597503203)
XLA Ops:
  8.5 6.3 all-to-all-start
  18.5 53.2 %shard_map.301 = (bf16[4,8,32,3584]{3,2,1,0:T(8,128)(2,1)}, bf16[4,8,16,256]{3,2,1,0:T(8,128)(2,1)}) custom-call(bf16[32,3584]{1,0:T(8,128)(2,1)} %pad_maximum_fusion.2.refs_0_, bf16[16,256]{1,0:T(8,128)(2,1)} %copy-done.22), custom_call_target="tpu_custom_call" | custom-call | tf_op jit(solution)/shard_map/pallas_call | solution.py:127
  74.1 5.8 shard_map.306
  83.4 5.8 shard_map.302
  89.2 20.9 %all-to-all-done.4.rows_ref = bf16[4,256,512]{2,1,0:T(8,128)(2,1)S(1)} async-done(((bf16[4,256,512]{2,1,0:T(8,128)(2,1)}), bf16[4,256,512]{2,1,0:T(8,128)(2,1)S(1)}, u32[]{:S(2)}, u32[]{:S(2)}) %all-to-all-start.4) | async-done | bytes 1048608 | tf_op jit(solution)/shard_map/all_to_all | solution.py:282
  119.3 21.3 %all-to-all-done.1.rows_ref = bf16[4,256,512]{2,1,0:T(8,128)(2,1)S(1)} async-done(((bf16[4,256,512]{2,1,0:T(8,128)(2,1)}), bf16[4,256,512]{2,1,0:T(8,128)(2,1)S(1)}, u32[]{:S(2)}, u32[]{:S(2)}) %all-to-all-start.1) | async-done | bytes 1048608 | tf_op jit(solution)/shard_map/all_to_all | solution.py:282
  147.4 45.4 %all-to-all-done.6.refs_0_ = bf16[4,256,1024]{2,1,0:T(8,128)(2,1)S(1)} async-done(((bf16[4,256,1024]{2,1,0:T(8,128)(2,1)}), bf16[4,256,1024]{2,1,0:T(8,128)(2,1)S(1)}, u32[]{:S(2)}, u32[]{:S(2)}) %all-to-all-start.6) | async-done | bytes 2097184 | tf_op jit(solution)/shard_map/all_to_all | solution.py:282
  197.7 8.0 %multiply_subtract_fusion = (f32[16,32,512]{2,1,0:T(8,128)S(1)}, f32[16,32,512]{2,1,0:T(8,128)S(1)}, f32[16,32,512]{2,1,0:T(8,128)S(1)}, f32[16,32,512]{2,1,0:T(...) fusion(f32[16,512]{1,0:T(8,128)S(1)} %get-tuple-element.164, f32[16,512]{1,0:T(8,128)S(1)} %get-tuple-element.163, ...), kind=kLoop, calls=%fused_computation.37 | loop fusion | flops 3932160 | bytes 6422784 | tf_op jit(solution)/shard_map/sub | solution.py:583
  207.9 10.4 %all_gather.3 = f32[128,1024]{1,0:T(8,128)S(1)} all-gather(f32[16,1024]{1,0:T(8,128)S(1)} %reshape.208), channel_id=1, replica_groups=mesh['dp'=4,'fsdp'=8] {'fsdp'}, dimensions={0}, use_global_device_ids=true | all-gather | bytes 589824 | tf_op jit(solution)/shard_map/all_gather | solution.py:770
  224.9 16.6 %shard_map.304 = (bf16[1024,3072]{1,0:T(8,128)(2,1)}, bf16[1024,3072]{1,0:T(8,128)(2,1)}) custom-call(bf16[1024,1024]{1,0:T(8,128)(2,1)} %get-tuple-element.92.normed_ref.refs_0_, bf16[1024,3584]{1,0:T(8,128)(2,1)} %bitcast.83), custom_call_target="tpu_custom_call" | custom-call | flops 6442450944 | bytes 18874368 | tf_op jit(solution)/shard_map/pallas_call | solution.py:724
  241.5 7.3 %shard_map.307 = bf16[4,256,512]{2,1,0:T(8,128)(2,1)} custom-call(bf16[2,512,256]{2,1,0:T(8,128)(2,1)} %constant.113.clone.table_ref, bf16[2,512,256]{2,1,0:T(8,128)(2,1)} %constant.114.clone.inverse_ref, f32[4,512,128]{2,1,0:T(8,128)} %multiply_add_fusion.kernel_ref, bf16[4,256,512]{2,1,0:T(8,128)(2,1)} %copy-done.5), custom_call_target="tpu_custom_call" | custom-call | flops 2684354560 | bytes 8388608 | tf_op jit(solution)/shard_map/pallas_call | solution.py:783
  248.8 5.2 all-to-all-start.5
  257.1 16.6 %shard_map.308 = (bf16[1024,3072]{1,0:T(8,128)(2,1)}, bf16[1024,3072]{1,0:T(8,128)(2,1)}) custom-call(bf16[1024,1024]{1,0:T(8,128)(2,1)} %get-tuple-element.99.normed_ref.refs_1_, bf16[1024,3584]{1,0:T(8,128)(2,1)} %bitcast.84), custom_call_target="tpu_custom_call" | custom-call | flops 6442450944 | bytes 18874368 | tf_op jit(solution)/shard_map/pallas_call | solution.py:724
  278.3 65.4 %shard_map.300 = (bf16[4,8,16,3072]{3,2,1,0:T(8,128)(2,1)}, bf16[4,8,96,1024]{3,2,1,0:T(8,128)(2,1)}, f32[4,8,8,256]{3,2,1,0:T(8,128)}) custom-call(bf16[16,3072]{1,0:T(8,128)(2,1)} %refs_0_.1, bf16[96,1024]{1,0:T(8,128)(2,1)} %refs_1_.1, f32[8,256]{1,0:T(8,128)} %broadcast_in_dim.20.refs_2_), custom_call_target="tpu_custom_call" | custom-call | tf_op jit(solution)/shard_map/pallas_call | solution.py:127
  345.9 7.2 %shard_map.303 = bf16[4,256,512]{2,1,0:T(8,128)(2,1)} custom-call(bf16[2,512,256]{2,1,0:T(8,128)(2,1)} %constant.113.clone.table_ref, bf16[2,512,256]{2,1,0:T(8,128)(2,1)} %constant.114.clone.inverse_ref, f32[4,512,128]{2,1,0:T(8,128)} %multiply_add_fusion.kernel_ref, bf16[4,256,512]{2,1,0:T(8,128)(2,1)} %copy-done.4), custom_call_target="tpu_custom_call" | custom-call | flops 2684354560 | bytes 8388608 | tf_op jit(solution)/shard_map/pallas_call | solution.py:783
  357.6 32.3 %shard_map.309 = (bf16[1024,512]{1,0:T(8,128)(2,1)}, bf16[1024,3072]{1,0:T(8,128)(2,1)}, bf16[1024,1024]{1,0:T(8,128)(2,1)}, bf16[1024,3072]{1,0:T(8,128)(2,1)},...) custom-call(s32[4]{0:T(128)} %get-tuple-element.145.order_ref, ...), custom_call_target="tpu_custom_call" | custom-call | flops 19327352832 | bytes 48234496 | tf_op jit(solution)/shard_map/pallas_call | solution.py:815
  389.9 5.1 all-to-all-start.9
  395.0 32.3 %shard_map.305 = (bf16[1024,512]{1,0:T(8,128)(2,1)}, bf16[1024,3072]{1,0:T(8,128)(2,1)}, bf16[1024,1024]{1,0:T(8,128)(2,1)}, bf16[1024,3072]{1,0:T(8,128)(2,1)},...) custom-call(s32[4]{0:T(128)} %get-tuple-element.144.order_ref, ...), custom_call_target="tpu_custom_call" | custom-call | flops 19327352832 | bytes 48234496 | tf_op jit(solution)/shard_map/pallas_call | solution.py:815
  427.4 20.1 %shard_map.312 = bf16[1024,3072]{1,0:T(8,128)(2,1)} custom-call(bf16[1024,1024]{1,0:T(8,128)(2,1)} %get-tuple-element.92.normed_ref.refs_0_, bf16[1024,1024]{1,0:T(8,128)(2,1)} %get-tuple-element.99.normed_ref.refs_1_, bf16[1024,3072]{1,0:T(8,128)(2,1)} %get-tuple-element.111.refs_2_.gate_grad_ref, bf16[1024,3072]{1,0:T(8,128)(2,1)} %get-tuple-element.112.refs_3_.gate_grad_ref), custom_call_target="tpu_custom_call" | custom-call | flops 12884901888 | bytes 23068672 | tf_op jit(solution)/shard_map/pallas_call | solution.py:429
  447.5 5.5 all-to-all-start.7
  454.9 18.2 %shard_map.310 = bf16[3072,1024]{1,0:T(8,128)(2,1)} custom-call(bf16[1024,3072]{1,0:T(8,128)(2,1)} %get-tuple-element.103.refs_0_, bf16[1024,3072]{1,0:T(8,128)(2,1)} %get-tuple-element.104.refs_1_, bf16[1024,1024]{1,0:T(8,128)(2,1)} %get-tuple-element.105.refs_2_, bf16[1024,1024]{1,0:T(8,128)(2,1)} %get-tuple-element.106.refs_3_), custom_call_target="tpu_custom_call" | custom-call | flops 12884901888 | bytes 23068672 | tf_op jit(solution)/shard_map/pallas_call | solution.py:429
  473.0 9.9 %shard_map.315 = (bf16[4,256,512]{2,1,0:T(8,128)(2,1)}, f32[4,512,128]{2,1,0:T(8,128)}) custom-call(bf16[2,512,256]{2,1,0:T(8,128)(2,1)} %constant.113.clone.table_ref, bf16[2,512,256]{2,1,0:T(8,128)(2,1)} %constant.114.clone.inverse_ref, f32[4,512,128]{2,1,0:T(8,128)} %multiply_add_fusion.kernel_ref, bf16[4,256,512]{2,1,0:T(8,128)(2,1)} %copy-done.5, ...), custom_call_target="tpu_custom_call" | custom-call | flops 3758096384 | bytes 8388608 | tf_op jit(solution)/shard_map/pallas_call | solution.py:794
  483.0 5.1 all-to-all-start.10
  488.2 9.9 %shard_map.313 = (bf16[4,256,512]{2,1,0:T(8,128)(2,1)}, f32[4,512,128]{2,1,0:T(8,128)}) custom-call(bf16[2,512,256]{2,1,0:T(8,128)(2,1)} %constant.113.clone.table_ref, bf16[2,512,256]{2,1,0:T(8,128)(2,1)} %constant.114.clone.inverse_ref, f32[4,512,128]{2,1,0:T(8,128)} %multiply_add_fusion.kernel_ref, bf16[4,256,512]{2,1,0:T(8,128)(2,1)} %copy-done.4, ...), custom_call_target="tpu_custom_call" | custom-call | flops 3758096384 | bytes 8388608 | tf_op jit(solution)/shard_map/pallas_call | solution.py:794
  511.4 13.2 %shard_map.311 = bf16[512,3072]{1,0:T(8,128)(2,1)} custom-call(bf16[1024,512]{1,0:T(8,128)(2,1)} %get-tuple-element.107.refs_0_, bf16[1024,512]{1,0:T(8,128)(2,1)} %get-tuple-element.108.refs_1_, bf16[1024,3072]{1,0:T(8,128)(2,1)} %get-tuple-element.109.refs_2_, bf16[1024,3072]{1,0:T(8,128)(2,1)} %get-tuple-element.110.refs_3_), custom_call_target="tpu_custom_call" | custom-call | flops 6442450944 | bytes 17825792 | tf_op jit(solution)/shard_map/pallas_call | solution.py:429
  524.5 17.0 %reduce-scatter.4.cloned.1.call-done = f32[16,1024]{1,0:T(8,128)} async-done(((f32[128,1024]{1,0:T(8,128)}), f32[16,1024]{1,0:T(8,128)}) %reduce-scatter.4.cloned.1.call-update) | async-done | bytes 65552
  544.9 5.4 fusion.7
  555.3 7.9 %subtract_reduce_fusion = (f32[16,512]{1,0:T(8,128)S(1)}, f32[16,512]{1,0:T(8,128)S(1)}, f32[16,512]{1,0:T(8,128)S(1)}, f32[16,512]{1,0:T(8,128)S(1)}) fusion(f32[16,512]{1,0:T(8,128)S(1)} %get-tuple-element.174, f32[32]{0:T(128)S(1)} %get-tuple-element.176, f32[16,512]{1,0:T(8,128)S(1)} %get-tuple-element.173, f32[16,64,1024]{2,1,0:T(8,128)} %fusion.7), kind=kLoop, calls=%fused_computation.29 | loop fusion | flops 6258688 | bytes 4391040 | tf_op jit(solution)/shard_map/reduce_sum | solution.py:605
  565.2 17.0 %shard_map.316 = (bf16[4,256,1024]{2,1,0:T(8,128)(2,1)}, bf16[1024,512]{1,0:T(8,128)(2,1)}, f32[2,8,1024]{2,1,0:T(8,128)}, f32[2,8,1024]{2,1,0:T(8,128)}) custom-call(bf16[4,256,512]{2,1,0:T(8,128)(2,1)} %copy-done, f32[1024,512]{1,0:T(8,128)} %get-tuple-element.120.slope_ref, bf16[1024,3072]{1,0:T(8,128)(2,1)} %get-tuple-element.112.refs_3_.gate_grad_ref, ...), custom_call_target="tpu_custom_call" | custom-call | flops 7516192768 | bytes 20971520 | tf_op jit(solution)/shard_map/pallas_call | solution.py:872
  583.1 17.1 %shard_map.314 = (bf16[4,256,1024]{2,1,0:T(8,128)(2,1)}, bf16[1024,512]{1,0:T(8,128)(2,1)}, f32[2,8,1024]{2,1,0:T(8,128)}, f32[2,8,1024]{2,1,0:T(8,128)}) custom-call(bf16[4,256,512]{2,1,0:T(8,128)(2,1)} %copy-done.1, f32[1024,512]{1,0:T(8,128)} %get-tuple-element.115.slope_ref, bf16[1024,3072]{1,0:T(8,128)(2,1)} %get-tuple-element.111.refs_2_.gate_grad_ref, ...), custom_call_target="tpu_custom_call" | custom-call | flops 7516192768 | bytes 20971520 | tf_op jit(solution)/shard_map/pallas_call | solution.py:872
  602.2 5.8 shard_map.317
  608.8 95.3 %shard_map.318 = (f32[96,1024]{1,0:T(8,128)}, f32[16,3072]{1,0:T(8,128)}, f32[32,3072]{1,0:T(8,128)}, f32[32,512]{1,0:T(8,128)}, f32[8,128]{1,0:T(8,128)}) custom-call(bf16[4,2,2,2,96,1024]{5,4,3,2,1,0:T(8,128)(2,1)} %bitcast.90, bf16[4,2,2,2,16,3072]{5,4,3,2,1,0:T(8,128)(2,1)} %bitcast.91, bf16[4,2,2,2,32,3072]{5,4,3,2,1,0:T(8,128)(2,1)} %bitcast.89, ...), custom_call_target="tpu_custom_call" | custom-call | tf_op jit(solution)/shard_map/pallas_call | solution.py:263
  (153 shorter events, 92.6 us)
Async XLA Ops:
  8.5 71.4 %all-to-all-start = ((s32[2,4,256]{2,0,1:T(2,128)}), s32[2,4,256]{2,0,1:T(2,128)S(1)}, u32[]{:S(2)}, u32[]{:S(2)}) async-start(s32[2,4,256]{2,0,1:T(2,128)} %bitcast.35), calls=%async_computation | async-start | bytes 16384 | tf_op jit(solution)/shard_map/all_to_all | solution.py:744
  79.9 30.2 %all-to-all-start.4 = ((bf16[4,256,512]{2,1,0:T(8,128)(2,1)}), bf16[4,256,512]{2,1,0:T(8,128)(2,1)S(1)}, u32[]{:S(2)}, u32[]{:S(2)}) async-start(bf16[4,256,512]{2,1,0:T(8,128)(2,1)} %get-tuple-element.98), calls=%async_computation.4 | async-start | bytes 2097152 | tf_op jit(solution)/shard_map/all_to_all | solution.py:282
  111.1 29.5 %all-to-all-start.1 = ((bf16[4,256,512]{2,1,0:T(8,128)(2,1)}), bf16[4,256,512]{2,1,0:T(8,128)(2,1)S(1)}, u32[]{:S(2)}, u32[]{:S(2)}) async-start(bf16[4,256,512]{2,1,0:T(8,128)(2,1)} %get-tuple-element.91), calls=%async_computation.1 | async-start | bytes 2097152 | tf_op jit(solution)/shard_map/all_to_all | solution.py:282
  119.3 25.9 %copy-start.24 = (s32[2,32]{1,0:T(2,128)S(1)}, s32[2,32]{1,0:T(2,128)}, u32[]{:S(2)}) copy-start(s32[2,32]{1,0:T(2,128)} %param.30) | copy-start | bytes 772
  119.3 26.8 %copy-start.25 = (s32[2,32]{1,0:T(2,128)S(1)}, s32[2,32]{1,0:T(2,128)}, u32[]{:S(2)}) copy-start(s32[2,32]{1,0:T(2,128)} %param.31) | copy-start | bytes 772
  119.3 27.6 %copy-start.28 = (f32[16]{0:T(128)S(1)}, f32[16]{0:T(128)}, u32[]{:S(2)}) copy-start(f32[16]{0:T(128)} %param.40) | copy-start | bytes 196
  141.5 51.3 %all-to-all-start.6 = ((bf16[4,256,1024]{2,1,0:T(8,128)(2,1)}), bf16[4,256,1024]{2,1,0:T(8,128)(2,1)S(1)}, u32[]{:S(2)}, u32[]{:S(2)}) async-start(bf16[4,256,1024]{2,1,0:T(8,128)(2,1)} %bitcast.16), calls=%async_computation.6 | async-start | bytes 4194304 | tf_op jit(solution)/shard_map/all_to_all | solution.py:282
  145.1 52.5 %copy-start.11 = (f32[2,16,512]{2,1,0:T(8,128)S(1)}, f32[2,16,512]{2,1,0:T(8,128)}, u32[]{:S(2)}) copy-start(f32[2,16,512]{2,1,0:T(8,128)} %param.37) | copy-start | bytes 196612
  145.2 52.5 %copy-start.15 = (f32[16,512]{1,0:T(8,128)S(1)}, f32[16,512]{1,0:T(8,128)}, u32[]{:S(2)}) copy-start(f32[16,512]{1,0:T(8,128)} %param.38) | copy-start | bytes 98308
  145.2 52.5 %copy-start.17 = (f32[16,512]{1,0:T(8,128)S(1)}, f32[16,512]{1,0:T(8,128)}, u32[]{:S(2)}) copy-start(f32[16,512]{1,0:T(8,128)} %param.39) | copy-start | bytes 98308
  192.8 56.0 %all-to-all-start.3 = ((bf16[4,256,1024]{2,1,0:T(8,128)(2,1)}), bf16[4,256,1024]{2,1,0:T(8,128)(2,1)}, u32[]{:S(2)}, u32[]{:S(2)}) async-start(bf16[4,256,1024]{2,1,0:T(8,128)(2,1)} %bitcast.14), calls=%async_computation.3 | async-start | bytes 4194304 | tf_op jit(solution)/shard_map/all_to_all | solution.py:282
  207.7 14.9 %copy-start.23 = (f32[512]{0:T(512)S(1)}, f32[512]{0:T(512)}, u32[]{:S(2)}) copy-start(f32[512]{0:T(512)} %constant.112.clone) | copy-start | bytes 6148
  248.8 104.3 %all-to-all-start.5 = ((bf16[4,256,512]{2,1,0:T(8,128)(2,1)}), bf16[4,256,512]{2,1,0:T(8,128)(2,1)S(1)}, u32[]{:S(2)}, u32[]{:S(2)}) async-start(bf16[4,256,512]{2,1,0:T(8,128)(2,1)} %shard_map.307), calls=%async_computation.5 | async-start | bytes 2097152 | tf_op jit(solution)/shard_map/all_to_all | solution.py:282
  353.1 36.8 %all-to-all-start.2 = ((bf16[4,256,512]{2,1,0:T(8,128)(2,1)}), bf16[4,256,512]{2,1,0:T(8,128)(2,1)}, u32[]{:S(2)}, u32[]{:S(2)}) async-start(bf16[4,256,512]{2,1,0:T(8,128)(2,1)} %shard_map.303), calls=%async_computation.2 | async-start | bytes 2097152 | tf_op jit(solution)/shard_map/all_to_all | solution.py:282
  389.9 57.5 %all-to-all-start.9 = ((bf16[4,256,512]{2,1,0:T(8,128)(2,1)}), bf16[4,256,512]{2,1,0:T(8,128)(2,1)S(1)}, u32[]{:S(2)}, u32[]{:S(2)}) async-start(bf16[4,256,512]{2,1,0:T(8,128)(2,1)} %get-tuple-element.118), calls=%async_computation.9 | async-start | bytes 2097152 | tf_op jit(solution)/shard_map/all_to_all | solution.py:282
  427.4 25.6 %copy-start.13 = (f32[4,8,1024]{2,1,0:T(8,128)S(1)}, f32[4,8,1024]{2,1,0:T(8,128)}, u32[]{:S(2)}) copy-start(f32[4,8,1024]{2,1,0:T(8,128)} %get-tuple-element.128) | copy-start | bytes 393220
  427.4 25.6 %copy-start.14 = (f32[4,8,1024]{2,1,0:T(8,128)S(1)}, f32[4,8,1024]{2,1,0:T(8,128)}, u32[]{:S(2)}) copy-start(f32[4,8,1024]{2,1,0:T(8,128)} %get-tuple-element.127) | copy-start | bytes 393220
  447.5 25.6 %copy-start.7 = (bf16[4,256,512]{2,1,0:T(8,128)(2,1)}, bf16[4,256,512]{2,1,0:T(8,128)(2,1)S(1)}, u32[]{:S(2)}) copy-start(bf16[4,256,512]{2,1,0:T(8,128)(2,1)S(1)} %all-to-all-done.9.grad_ref) | copy-start | bytes 3145732
  447.5 35.5 %all-to-all-start.7 = ((bf16[4,256,512]{2,1,0:T(8,128)(2,1)}), bf16[4,256,512]{2,1,0:T(8,128)(2,1)}, u32[]{:S(2)}, u32[]{:S(2)}) async-start(bf16[4,256,512]{2,1,0:T(8,128)(2,1)} %get-tuple-element.113), calls=%async_computation.7 | async-start | bytes 2097152 | tf_op jit(solution)/shard_map/all_to_all | solution.py:282
  483.0 67.3 %all-to-all-start.10 = ((bf16[4,256,512]{2,1,0:T(8,128)(2,1)}), bf16[4,256,512]{2,1,0:T(8,128)(2,1)S(1)}, u32[]{:S(2)}, u32[]{:S(2)}) async-start(bf16[4,256,512]{2,1,0:T(8,128)(2,1)} %get-tuple-element.119), calls=%async_computation.10 | async-start | bytes 2097152 | tf_op jit(solution)/shard_map/all_to_all | solution.py:282
  488.0 53.5 %reduce-scatter.4.cloned.1.call-start = ((), (), s32[]{:S(2)}) async-start(), calls=%async_computation.12 | async-start | bytes 589824
  550.3 12.9 %copy-start = (bf16[4,256,512]{2,1,0:T(8,128)(2,1)}, bf16[4,256,512]{2,1,0:T(8,128)(2,1)S(1)}, u32[]{:S(2)}) copy-start(bf16[4,256,512]{2,1,0:T(8,128)(2,1)S(1)} %all-to-all-done.10.back_ref) | copy-start | bytes 3145732
  550.3 13.6 %copy-start.16 = (f32[16,512]{1,0:T(8,128)S(1)}, f32[16,512]{1,0:T(8,128)}, u32[]{:S(2)}) copy-start(f32[16,512]{1,0:T(8,128)} %param.38) | copy-start | bytes 98308
  550.3 13.6 %copy-start.18 = (f32[16,512]{1,0:T(8,128)S(1)}, f32[16,512]{1,0:T(8,128)}, u32[]{:S(2)}) copy-start(f32[16,512]{1,0:T(8,128)} %param.39) | copy-start | bytes 98308
  550.3 13.6 %copy-start.26 = (f32[16]{0:T(128)S(1)}, f32[16]{0:T(128)}, u32[]{:S(2)}) copy-start(f32[16]{0:T(128)} %get-tuple-element.171) | copy-start | bytes 196
  550.3 31.9 %all-to-all-start.8 = ((bf16[4,256,512]{2,1,0:T(8,128)(2,1)}), bf16[4,256,512]{2,1,0:T(8,128)(2,1)S(1)}, u32[]{:S(2)}, u32[]{:S(2)}) async-start(bf16[4,256,512]{2,1,0:T(8,128)(2,1)} %get-tuple-element.114), calls=%async_computation.8 | async-start | bytes 2097152 | tf_op jit(solution)/shard_map/all_to_all | solution.py:282
  583.1 17.1 %copy-start.20 = (f32[2,8,1024]{2,1,0:T(8,128)S(1)}, f32[2,8,1024]{2,1,0:T(8,128)}, u32[]{:S(2)}) copy-start(f32[2,8,1024]{2,1,0:T(8,128)} %get-tuple-element.124) | copy-start | bytes 196612
  583.1 18.1 %copy-start.19 = (f32[2,8,1024]{2,1,0:T(8,128)S(1)}, f32[2,8,1024]{2,1,0:T(8,128)}, u32[]{:S(2)}) copy-start(f32[2,8,1024]{2,1,0:T(8,128)} %get-tuple-element.126) | copy-start | bytes 196612
  602.2 5.8 copy-start.27
  608.8 98.4 %copy-start.3 = (bf16[4,256,1024]{2,1,0:T(8,128)(2,1)S(1)}, bf16[4,256,1024]{2,1,0:T(8,128)(2,1)}, u32[]{:S(2)}) copy-start(bf16[4,256,1024]{2,1,0:T(8,128)(2,1)} %get-tuple-element.131) | copy-start | bytes 6291460
  707.2 5.5 copy-start.12
  707.2 6.1 copy-start.9
  (9 other events, 23.6 us)
Sparse Core Ops, SparseCore 0:
  506.9 34.6 reduce-scatter.3

commit v3 on v2

--- a/solution.py
+++ b/solution.py
@@ -42,50 +42,77 @@
     return order
 
 
-def gather_body(dp_count, bits, n, *refs):
-    ins, outs = refs[:n], refs[n : 2 * n]
-    z_send, z_recv, send, recv, own_sem = refs[2 * n :]
+def gather_body(dp_count, bits, n, n_swap, work, *refs):
+    n_work_in, n_work_out, n_work_scratch = work[0] if work else (0, 0, 0)
+    moved = n + n_swap
+    ins, refs = refs[:moved], refs[moved:]
+    work_ins, refs = refs[:n_work_in], refs[n_work_in:]
+    outs, refs = refs[:moved], refs[moved:]
+    work_outs, refs = refs[:n_work_out], refs[n_work_out:]
+    z_send, z_recv, send, recv, own_sem, swap_send, swap_recv = refs[:7]
+    begin, tick, end = work[1](work_ins, work_outs, refs[7:]) if work else (None, None, None)
     d, f = lax.axis_index("dp"), lax.axis_index("fsdp")
     cuts = []
-    for x in ins:
+    for x in ins[:n]:
         cut = x.shape[1] // 256 * 128
         cuts.append(((0, cut), (cut, x.shape[1] - cut)))
+    order = near_first(dp_count)
+    if work:
+        begin()
     greet(dp_count, bits)
-    own = [
-        pltpu.make_async_copy(ins[a], outs[a].at[d, f], own_sem.at[a]) for a in range(n)
+    own = [pltpu.make_async_copy(ins[a], outs[a].at[d, f], own_sem.at[a]) for a in range(n)]
+    own += [
+        pltpu.make_async_copy(ins[a].at[d], outs[a].at[d], own_sem.at[a])
+        for a in range(n, n + n_swap)
     ]
     for copy in own:
         copy.start()
     started, arrived, waited = [], {}, set()
-    order = near_first(dp_count)
+
+    def push(src, dst, send_sem, recv_sem, device_id):
+        copy = pltpu.make_async_remote_copy(
+            src_ref=src,
+            dst_ref=dst,
+            send_sem=send_sem,
+            recv_sem=recv_sem,
+            device_id=device_id,
+            device_id_type=MESH,
+        )
+        copy.start()
+        started.append(copy)
+        return copy
+
     for o in order[1:]:
         for h in range(2):
             for a in range(n):
                 lo, size = cuts[a][h]
-                copy = pltpu.make_async_remote_copy(
-                    src_ref=ins[a].at[:, pl.ds(lo, size)],
-                    dst_ref=outs[a].at[d, f, :, pl.ds(lo, size)],
-                    send_sem=z_send.at[o - 1, h, a],
-                    recv_sem=z_recv.at[o - 1, h, a],
-                    device_id={"dp": lax.rem(d + o, dp_count)},
-                    device_id_type=MESH,
+                arrived[(o, 0, h, a)] = push(
+                    ins[a].at[:, pl.ds(lo, size)],
+                    outs[a].at[d, f, :, pl.ds(lo, size)],
+                    z_send.at[o - 1, h, a],
+                    z_recv.at[o - 1, h, a],
+                    {"dp": lax.rem(d + o, dp_count)},
                 )
-                copy.start()
-                started.append(copy)
-                arrived[(o, 0, h, a)] = copy
     for copy in own:
         copy.wait()
     upper = list(range(1, bits))
     stages = [upper + [0], upper[::-1] + [0]]
-    held = [[0], [0]]
-    slot = 0
-    for s in range(bits):
-        fresh = [[], []]
-        for mi in range(len(held[0])):
-            for o in order:
+    masks = [[[0]], [[0]]]
+    for h in range(2):
+        for s in range(bits):
+            masks[h].append(masks[h][s] + [m ^ (1 << stages[h][s]) for m in masks[h][s]])
+    slot, group = 0, 0
+    for t in range(dp_count + bits - 1):
+        for i in range(dp_count):
+            s, o = t - i, order[i]
+            if not 0 <= s < bits:
+                continue
+            if work:
+                tick(group, dp_count * bits)
+                group += 1
+            for k in range(len(masks[0][s])):
                 for h in range(2):
-                    mask, b = held[h][mi], stages[h][s]
-                    src_d = lax.rem(d - o + dp_count, dp_count)
+                    mask, b = masks[h][s][k], stages[h][s]
                     src_f = f
                     for bb in range(bits):
                         if mask >> bb & 1:
@@ -96,22 +123,25 @@
                             arrived[key].wait_recv()
                             waited.add(key)
                         lo, size = cuts[a][h]
+                        src_d = lax.rem(d - o + dp_count, dp_count)
                         piece = outs[a].at[src_d, src_f, :, pl.ds(lo, size)]
-                        copy = pltpu.make_async_remote_copy(
-                            src_ref=piece,
-                            dst_ref=piece,
-                            send_sem=send.at[slot],
-                            recv_sem=recv.at[slot],
-                            device_id={"fsdp": flip(f, b)},
-                            device_id_type=MESH,
+                        arrived[(o, mask ^ (1 << b), h, a)] = push(
+                            piece, piece, send.at[slot], recv.at[slot], {"fsdp": flip(f, b)}
                         )
-                        copy.start()
-                        started.append(copy)
-                        arrived[(o, mask ^ (1 << b), h, a)] = copy
                         slot += 1
-                    if o == 0:
-                        fresh[h].append(mask ^ (1 << b))
-        held = [held[h] + fresh[h] for h in range(2)]
+        if t == 0:
+            for o in order[1:]:
+                peer = lax.rem(d + o, dp_count)
+                for e in range(n_swap):
+                    arrived[(o, e)] = push(
+                        ins[n + e].at[peer],
+                        outs[n + e].at[d],
+                        swap_send.at[o - 1, e],
+                        swap_recv.at[o - 1, e],
+                        {"dp": peer},
+                    )
+    if work:
+        end()
     for key, copy in arrived.items():
         if key not in waited:
             copy.wait_recv()
@@ -119,27 +149,38 @@
         copy.wait_send()
 
 
-def gather_all(arrays, collective_id):
+def gather_all(arrays, swaps, collective_id, work=None):
+    work_in, work_out, work_scratch, work_body = work or ((), (), (), None)
+    sizes = (len(work_in), len(work_out), len(work_scratch))
     dp_count, fsdp_count = lax.axis_size("dp"), lax.axis_size("fsdp")
     bits = fsdp_count.bit_length() - 1
-    n = len(arrays)
+    n, n_swap = len(arrays), len(swaps)
     slots = 2 * dp_count * (fsdp_count - 1) * n
+    total = dp_count * fsdp_count * sum(x.size * x.dtype.itemsize for x in arrays)
     return pl.pallas_call(
-        functools.partial(gather_body, dp_count, bits, n),
+        functools.partial(gather_body, dp_count, bits, n, n_swap, (sizes, work_body) if work else None),
         out_shape=[
             jax.ShapeDtypeStruct((dp_count, fsdp_count, *x.shape), x.dtype) for x in arrays
-        ],
-        in_specs=[ANY] * n,
-        out_specs=[ANY] * n,
+        ]
+        + [jax.ShapeDtypeStruct(x.shape, x.dtype) for x in swaps]
+        + list(work_out),
+        in_specs=[ANY] * (n + n_swap + sizes[0]),
+        out_specs=[ANY] * (n + n_swap + sizes[1]),
         scratch_shapes=[
             pltpu.SemaphoreType.DMA((dp_count - 1, 2, n)),
             pltpu.SemaphoreType.DMA((dp_count - 1, 2, n)),
             pltpu.SemaphoreType.DMA((slots,)),
             pltpu.SemaphoreType.DMA((slots,)),
-            pltpu.SemaphoreType.DMA((n,)),
+            pltpu.SemaphoreType.DMA((n + n_swap,)),
+            pltpu.SemaphoreType.DMA((dp_count - 1, max(n_swap, 1))),
+            pltpu.SemaphoreType.DMA((dp_count - 1, max(n_swap, 1))),
+            *work_scratch,
         ],
-        compiler_params=pltpu.CompilerParams(collective_id=collective_id, has_side_effects=True),
-    )(*arrays)
+        compiler_params=pltpu.CompilerParams(
+            collective_id=collective_id, has_side_effects=True, vmem_limit_bytes=40 << 20
+        ),
+        cost_estimate=pl.CostEstimate(flops=0, bytes_accessed=20 * total, transcendentals=0),
+    )(*arrays, *swaps, *work_in)
 
 
 def scatter_body(dp_count, bits, pieces, kinds, *refs):
@@ -343,22 +384,90 @@
     channels_from_rows(out_ref, reduced, seqs, chunk, own)
 
 
-def gate_body(tile, normed_ref, weight_ref, gate_ref, slope_ref):
-    for j in range(gate_ref.shape[1] // tile):
-        at = slice(j * tile, (j + 1) * tile)
-        gate, slope = gelu_and_slope(matmul(normed_ref[...], weight_ref[:, at]))
-        gate_ref[:, at] = gate.astype(bf16)
-        slope_ref[:, at] = slope.astype(bf16)
+def gate_work(normed, first, gate_width):
+    rows, width = normed[0].shape
+    micro_count, tile = len(normed), 512
+    across, down = gate_width // tile, rows // tile
+    count = micro_count * across * down
+
+    def body(ins, outs, scratch):
+        rows_refs, weight_ref = ins[:-1], ins[-1]
+        rows_buf, weight_buf, out_buf, load_sem, store_sem = scratch
+        loads = [
+            pltpu.make_async_copy(rows_refs[m], rows_buf.at[pl.ds(m * rows, rows)], load_sem.at[m])
+            for m in range(micro_count)
+        ]
+        loads.append(
+            pltpu.make_async_copy(
+                weight_ref.at[:, pl.ds(0, gate_width)], weight_buf, load_sem.at[micro_count]
+            )
+        )
+        loaded = []
+
+        def stores(k):
+            at = (
+                pl.ds(pl.multiple_of(lax.div(k, across) * tile, tile), tile),
+                pl.ds(pl.multiple_of(lax.rem(k, across) * tile, tile), tile),
+            )
+            slot = lax.rem(k, 2)
+            return [
+                pltpu.make_async_copy(out_buf.at[slot, r], outs[r].at[at], store_sem.at[slot, r])
+                for r in range(2)
+            ]
+
+        def begin():
+            for copy in loads:
+                copy.start()
+
+        def step(k, carry):
+            @pl.when(k >= 2)
+            def _():
+                for copy in stores(k - 2):
+                    copy.wait()
+
+            slot = lax.rem(k, 2)
+            left = rows_buf[pl.ds(pl.multiple_of(lax.div(k, across) * tile, tile), tile), :]
+            right = weight_buf[:, pl.ds(pl.multiple_of(lax.rem(k, across) * tile, tile), tile)]
+            gate, slope = gelu_and_slope(matmul(left, right))
+            out_buf[slot, 0] = gate.astype(bf16)
+            out_buf[slot, 1] = slope.astype(bf16)
+            for copy in stores(k):
+                copy.start()
+            return carry
+
+        def tick(group, groups):
+            if not loaded:
+                for copy in loads:
+                    copy.wait()
+                loaded.append(True)
+            lax.fori_loop(count * group // groups, count * (group + 1) // groups, step, 0)
+
+        def end():
+            for k in (count - 2, count - 1):
+                for copy in stores(k):
+                    copy.wait()
+
+        return begin, tick, end
+
+    shape = jax.ShapeDtypeStruct((micro_count * rows, gate_width), bf16)
+    scratch = [
+        pltpu.VMEM((micro_count * rows, width), bf16),
+        pltpu.VMEM((width, gate_width), bf16),
+        pltpu.VMEM((2, 2, tile, tile), bf16),
+        pltpu.SemaphoreType.DMA((micro_count + 1,)),
+        pltpu.SemaphoreType.DMA((2, 2)),
+    ]
+    return [*normed, first], [shape, shape], scratch, body
 
 
 def middle_body(
     dims, teachers, tile, order_ref, scale_ref, state_ref, gate_ref, slope_ref, expand_ref, weight_ref,
-    tokens_ref, cotangent_ref, valid_ref, keep_ref, *refs,
+    tokens_ref, cotangent_ref, weights_ref, *refs,
 ):
     seqs, chunk, own = dims
     teach_refs, refs = refs[:teachers], refs[teachers:]
     (state_out_ref, product_ref, branch_grad_ref, expanded_grad_ref, gate_grad_ref, out_ref,
-     full_grad_ref, error_ref, mixed_grad_ref, expanded_ref) = refs
+     full_grad_ref, error_ref, mixed_grad_ref, expanded_ref) = refs[-10:]
     rows, width = seqs * chunk, tokens_ref.shape[-1]
     rows_from_channels(state_ref, state_out_ref, seqs, chunk, own)
     state_out = state_out_ref[...]
@@ -370,13 +479,13 @@
         product = (expanded * gate_ref[:, at].astype(f32)).astype(bf16)
         product_ref[:, at] = product
         branch = branch + matmul(product, weight_ref[at, :])
-    valid, keep = valid_ref[...], keep_ref[...]
+    valid, keep = weights_ref[:, :1], weights_ref[:, 1:]
     full = tokens_ref[...].reshape(rows, width).astype(f32) + valid * branch
     out_ref[...] = full.astype(bf16).reshape(out_ref.shape)
     errors = full - jnp.concatenate([t[0] for t in teach_refs], axis=0).astype(f32)
     error_ref[0] = jnp.sum((keep * errors * errors).reshape(rows // 8, 8, width), axis=0)
     full_grad = cotangent_ref[...].reshape(rows, width).astype(f32) + keep * errors * scale_ref[0]
-    full_grad_ref[...] = full_grad
+    full_grad_ref[...] = full_grad.astype(bf16)
     branch_grad = (valid * full_grad).astype(bf16)
     branch_grad_ref[...] = branch_grad
     mixed_grad = jnp.zeros((rows, state_out.shape[1]), f32)
@@ -393,8 +502,9 @@
 
 def input_body(
     dims, back_ref, slope_ref, gate_grad_ref, gate_weight_ref, reduce_weight_ref, tokens_ref,
-    gain_ref, full_grad_ref, out_ref, reduced_grad_ref, gain_grad_ref, bias_grad_ref, back_rows_ref,
+    gain_ref, full_grad_ref, *refs,
 ):
+    out_ref, reduced_grad_ref, gain_grad_ref, bias_grad_ref, back_rows_ref = refs[-5:]
     seqs, chunk, own = dims
     rows, width = seqs * chunk, tokens_ref.shape[-1]
     rows_from_channels(back_ref, back_rows_ref, seqs, chunk, own)
@@ -408,12 +518,301 @@
     gain_grad_ref[0] = jnp.sum((normed_grad * unit).reshape(rows // 8, 8, width), axis=0)
     bias_grad_ref[0] = jnp.sum(normed_grad.reshape(rows // 8, 8, width), axis=0)
     unit_grad = normed_grad * gain_ref[...]
-    result = full_grad_ref[...] + inverse_std * (
+    result = full_grad_ref[...].astype(f32) + inverse_std * (
         unit_grad
         - jnp.mean(unit_grad, axis=1, keepdims=True)
         - unit * jnp.mean(unit_grad * unit, axis=1, keepdims=True)
     )
     out_ref[...] = result.astype(bf16).reshape(out_ref.shape)
+
+
+def product_scatter_body(dp_count, bits, plan, n_left, n_right, *refs):
+    pieces, slots, lane, micros = plan["pieces"], plan["slots"], plan["lane"], plan["micros"]
+    n = len(pieces)
+    lefts, refs = refs[: n_left * micros], refs[n_left * micros :]
+    rights, refs = refs[: n_right * micros], refs[n_right * micros :]
+    small_ref, refs = refs[0], refs[1:]
+    outs, refs = refs[: plan["outputs"]], refs[plan["outputs"] :]
+    left_bufs, refs = refs[:n_left], refs[n_left:]
+    right_buf, left_sem, right_sem, load_sem, send, recv, store_sem = refs[:7]
+    sets = [refs[7 : 7 + 5 + 3 * (bits - 1)], refs[7 + 5 + 3 * (bits - 1) :]]
+    d, f = lax.axis_index("dp"), lax.axis_index("fsdp")
+    my = [bit_of(f, b) for b in range(bits)]
+    upper = list(range(bits - 1, 0, -1))
+    small = n - 1
+
+    def buffers(i):
+        if i == small:
+            return list(sets[1])
+        _, rows, groups, _ = pieces[i]
+        height, slot = rows * groups, i % slots
+        views = []
+        for k, ref in enumerate(sets[0]):
+            arriving = k in (1, 3) or (k >= 5 and (k - 5) % 3 == 2)
+            lead = (slice(None),) * (len(ref.shape) - 3)
+            views.append(ref.at[(i if arriving else slot, *lead, pl.ds(0, height), slice(None))])
+        return views
+
+    bufs = [buffers(i) for i in range(n)]
+    orders = [upper if i % 2 == 0 else upper[::-1] for i in range(n)]
+    pushed, drained, waits, stores = {}, set(), [None] * n, {}
+
+    def push(i, at, src, dst, device_id):
+        copy = pltpu.make_async_remote_copy(
+            src_ref=src,
+            dst_ref=dst,
+            send_sem=send.at[i, at],
+            recv_sem=recv.at[i, at],
+            device_id=device_id,
+            device_id_type=MESH,
+        )
+        copy.start()
+        pushed[(i, at)] = copy
+        return copy
+
+    def drain(i, *ats):
+        for at in ats:
+            if i >= 0 and i != small and (i, at) in pushed and (i, at) not in drained:
+                pushed[(i, at)].wait_send()
+                drained.add((i, at))
+
+    jobs = [(i, *job) for i in range(n) if i != small for job in pieces[i][3]]
+    loads = {}
+
+    def fetch(j):
+        if j < len(jobs):
+            _, _, right, lo, cols, _ = jobs[j]
+            loads[j] = [
+                pltpu.make_async_copy(
+                    rights[right * micros + m].at[:, pl.ds(lo, cols)],
+                    right_buf.at[j % 2, m, :, pl.ds(0, cols)],
+                    right_sem.at[j % 2, m],
+                )
+                for m in range(micros)
+            ]
+            for copy in loads[j]:
+                copy.start()
+
+    left_waited = set()
+    left_loads = [
+        [
+            pltpu.make_async_copy(lefts[a * micros + m], left_bufs[a].at[m], left_sem.at[a, m])
+            for m in range(micros)
+        ]
+        for a in range(n_left)
+    ]
+    small_load = pltpu.make_async_copy(small_ref, sets[1][0], load_sem)
+    small_load.start()
+    for a in range(n_left):
+        for copy in left_loads[a]:
+            copy.start()
+        if a < 2:
+            fetch(a)
+    greet(dp_count, bits)
+
+    def make(i):
+        _, rows, groups, piece_jobs = pieces[i]
+        made = bufs[i][0]
+        drain(i - slots, 0)
+        for j, job in enumerate(jobs):
+            if job[0] != i:
+                continue
+            _, left, right, lo, cols, at_group = job
+            if left not in left_waited:
+                for copy in left_loads[left]:
+                    copy.wait()
+                left_waited.add(left)
+            for copy in loads[j]:
+                copy.wait()
+            height = rows << bits
+
+            def tile(p, carry, left=left, cols=cols, at_group=at_group, j=j, height=height):
+                total = None
+                for m in range(left_bufs[left].shape[0]):
+                    part = rows_inner(
+                        left_bufs[left][m, :, pl.ds(pl.multiple_of(p * height, 128), height)],
+                        right_buf[j % 2, m, :, :cols],
+                    )
+                    total = part if total is None else total + part
+                total = total.astype(bf16)
+                for g in range(cols // lane):
+                    block = total[:, g * lane : (g + 1) * lane].reshape(*(2,) * bits, rows, lane)
+                    lead = (slice(None),) * bits
+                    made[(p, *lead, pl.ds((at_group + g) * rows, rows), slice(None))] = block
+                return carry
+
+            lax.fori_loop(0, dp_count, tile, 0)
+            fetch(j + 2)
+
+    def first(i):
+        made, got = bufs[i][0], bufs[i][1]
+        if i == small:
+            small_load.wait()
+        else:
+            make(i)
+        lead = (slice(None),) * bits
+        waits[i] = push(i, 0, made.at[(*lead, 1 - my[0])], got, {"fsdp": flip(f, 0)})
+
+    def held(i, s):
+        waits[i].wait_recv()
+        if s == 0:
+            lead = (slice(None),) * bits
+            return bufs[i][0].at[(*lead, my[0])], bufs[i][1]
+        return bufs[i][5 + 3 * (s - 1)], bufs[i][5 + 3 * (s - 1) + 2]
+
+    def middle(i, s):
+        own, more = held(i, s - 1)
+        b = orders[i][s - 1]
+        left = [q for q in upper if q not in orders[i][: s - 1]]
+        kept, sent, arriving = bufs[i][5 + 3 * (s - 1) : 8 + 3 * (s - 1)]
+
+        def side(value):
+            return (slice(None),) + tuple(value if q == b else slice(None) for q in left)
+
+        drain(i - slots, s)
+        theirs, mine = side(1 - my[b]), side(my[b])
+        sent[...] = (own[theirs].astype(f32) + more[theirs].astype(f32)).astype(sent.dtype)
+        waits[i] = push(i, s, sent, arriving, {"fsdp": flip(f, b)})
+        kept[...] = own[mine].astype(f32) + more[mine].astype(f32)
+
+    def last(i):
+        own, more = held(i, bits - 1)
+        to_dp, from_dp = bufs[i][2], bufs[i][3]
+        drain(i - slots, *range(bits, bits + dp_count - 1))
+        copies = []
+        for o in near_first(dp_count)[1:]:
+            peer = lax.rem(d + o, dp_count)
+            to_dp[o - 1] = (own[peer] + more[peer].astype(f32)).astype(to_dp.dtype)
+            copies.append(
+                push(i, bits - 1 + o, to_dp.at[o - 1], from_dp.at[o - 1], {"dp": peer})
+            )
+        waits[i] = (copies, own, more)
+
+    def finish(i):
+        copies, own, more = waits[i]
+        result, from_dp = bufs[i][4], bufs[i][3]
+        for copy in copies:
+            copy.wait_recv()
+        for store in stores.pop(i - slots, []):
+            store.wait()
+        total = own[d] + more[d].astype(f32)
+        for o in range(1, dp_count):
+            total = total + from_dp[o - 1].astype(f32)
+        result[...] = total
+        out, rows, groups, piece_jobs = pieces[i]
+        stores[i] = []
+        if i == small:
+            stores[i].append(pltpu.make_async_copy(result, outs[out], store_sem.at[i, 0]))
+        else:
+            lo = piece_jobs[0][2]
+            for g in range(groups):
+                stores[i].append(
+                    pltpu.make_async_copy(
+                        result.at[pl.ds(g * rows, rows)],
+                        outs[out].at[:, pl.ds(lo + g * lane, lane)],
+                        store_sem.at[i, g],
+                    )
+                )
+        for store in stores[i]:
+            store.start()
+
+    for t in range((n + 1) // 2 + bits + 1):
+        for i in range(n):
+            s = t - i // 2
+            if s == 0:
+                first(i)
+            elif 1 <= s < bits:
+                middle(i, s)
+            elif s == bits:
+                last(i)
+            elif s == bits + 1:
+                finish(i)
+    for key, copy in pushed.items():
+        if key not in drained:
+            copy.wait_send()
+    for group in stores.values():
+        for store in group:
+            store.wait()
+
+
+def product_scatter(lefts, rights, small, collective_id):
+    dp_count, fsdp_count = lax.axis_size("dp"), lax.axis_size("fsdp")
+    bits = fsdp_count.bit_length() - 1
+    devices = dp_count * fsdp_count
+    lane, slots, height = 256, 4, 96
+    unique = []
+    for left in lefts:
+        if not any(left is u for u in unique):
+            unique.append(left)
+    pieces = []
+    for k, (left, right) in enumerate(zip(lefts, rights)):
+        at = next(a for a, u in enumerate(unique) if u is left)
+        rows, width = left[0].shape[1] // devices, right[0].shape[1]
+        per_piece = min(height // rows, width // lane)
+        for lo in range(0, width, per_piece * lane):
+            groups = min(per_piece, (width - lo) // lane)
+            jobs = [
+                (at, k, lo + g * lane, min(3, groups - g) * lane, g) for g in range(0, groups, 3)
+            ]
+            pieces.append((k, rows, groups, jobs))
+    pieces.append((len(lefts), small.shape[1], 1, []))
+    n = len(pieces)
+    plan = {
+        "pieces": pieces,
+        "slots": slots,
+        "lane": lane,
+        "outputs": len(lefts) + 1,
+        "micros": len(lefts[0]),
+    }
+
+    def buffer_set(count, lead, rows, columns, dtype):
+        def shaped(many, *dims):
+            return (many, *dims, rows, columns) if lead else (*dims, rows, columns)
+
+        halved = [(2,) * (bits - 1 - s) for s in range(bits)]
+        result = [
+            pltpu.VMEM(shaped(slots, dp_count, *(2,) * bits), dtype),
+            pltpu.VMEM(shaped(count, dp_count, *halved[0]), dtype),
+            pltpu.VMEM(shaped(slots, dp_count - 1), dtype),
+            pltpu.VMEM(shaped(count, dp_count - 1), dtype),
+            pltpu.VMEM(shaped(slots), f32),
+        ]
+        for s in range(1, bits):
+            result += [
+                pltpu.VMEM(shaped(slots, dp_count, *halved[s]), f32),
+                pltpu.VMEM(shaped(slots, dp_count, *halved[s]), dtype),
+                pltpu.VMEM(shaped(count, dp_count, *halved[s]), dtype),
+            ]
+        return result
+
+    micro_count, rows = len(lefts[0]), lefts[0][0].shape[0]
+    steps = bits - 1 + dp_count
+    small = small.reshape(dp_count, *(2,) * bits, *small.shape[1:])
+    widths = [(a[0].shape[1], b[0].shape[1]) for a, b in zip(lefts, rights)]
+    flops = sum(2 * micro_count * rows * a * b for a, b in widths)
+    return pl.pallas_call(
+        functools.partial(product_scatter_body, dp_count, bits, plan, len(unique), len(rights)),
+        out_shape=[jax.ShapeDtypeStruct((a // devices, b), f32) for a, b in widths]
+        + [jax.ShapeDtypeStruct(small.shape[-2:], f32)],
+        in_specs=[ANY] * ((len(unique) + len(rights)) * micro_count + 1),
+        out_specs=[ANY] * (len(lefts) + 1),
+        scratch_shapes=[pltpu.VMEM((micro_count, *u[0].shape), bf16) for u in unique]
+        + [
+            pltpu.VMEM((2, micro_count, rows, 3 * lane), bf16),
+            pltpu.SemaphoreType.DMA((len(unique), micro_count)),
+            pltpu.SemaphoreType.DMA((2, micro_count)),
+            pltpu.SemaphoreType.DMA,
+            pltpu.SemaphoreType.DMA((n, steps)),
+            pltpu.SemaphoreType.DMA((n, steps)),
+            pltpu.SemaphoreType.DMA((n, height // 16)),
+        ]
+        + buffer_set(n - 1, True, height, lane, bf16)
+        + buffer_set(1, False, *small.shape[-2:], f32),
+        compiler_params=pltpu.CompilerParams(
+            collective_id=collective_id, has_side_effects=True, vmem_limit_bytes=62 << 20
+        ),
+        cost_estimate=pl.CostEstimate(flops=flops, bytes_accessed=100 << 20, transcendentals=0),
+    )(*[x for u in unique for x in u], *[x for r in rights for x in r], small)
 
 
 def weight_grad_body(n, *refs):
@@ -649,7 +1048,15 @@
     direct = own % 128 == 0
 
     small = jnp.zeros((16, 256), bf16).at[0, :share].set(norm_gain).at[1, :share].set(norm_bias)
-    first, small = gather_all([jnp.concatenate([gate_weight, reduce_weight], axis=1), small], 1)
+    mask_rows = loss_mask.reshape(micro_count, dp_count, chunk).transpose(1, 0, 2)
+    mask_rows = jnp.pad(mask_rows, ((0, 0), (0, 8 - micro_count), (0, 0)))
+    teacher_rows = [teacher[m].reshape(dp_count, chunk, width) for m in micros]
+    first, small, *swapped = gather_all(
+        [jnp.concatenate([gate_weight, reduce_weight], axis=1), small],
+        [mask_rows, *teacher_rows[1:]],
+        1,
+    )
+    masked = swapped[0].transpose(1, 0, 2)[:micro_count]
     first = first.reshape(width, gate_width + reduced_width)
     gain_row = small[:, :, 0, :share].reshape(1, width).astype(f32)
     bias_row = small[:, :, 1, :share].reshape(1, width).astype(f32)
@@ -658,9 +1065,6 @@
     steps = seqs // per_block
     middle_block = max(1, 256 // chunk)
     middle_steps = seqs // middle_block
-
-    def sequence_spec(count):
-        return pl.BlockSpec((count, chunk, width), lambda i, *_: (i, 0, 0))
 
     def row_spec(columns, count=per_block):
         return pl.BlockSpec((count * chunk, columns), lambda i, *_: (i, 0))
@@ -720,30 +1124,9 @@
             ),
         )(tokens, gain_row, bias_row, first)
 
-    def gate_rows(normed):
-        return pl.pallas_call(
-            functools.partial(gate_body, 512),
-            grid=(steps,),
-            out_shape=[jax.ShapeDtypeStruct((rows, gate_width), bf16)] * 2,
-            in_specs=[row_spec(width), shared((width, gate_width), (0, 0))],
-            out_specs=[row_spec(gate_width)] * 2,
-            compiler_params=params(),
-            cost_estimate=pl.CostEstimate(
-                flops=2 * rows * width * gate_width,
-                bytes_accessed=4 * rows * gate_width + 2 * width * gate_width,
-                transcendentals=2 * rows * gate_width,
-            ),
-        )(normed, first)
-
     normed, lanes_out, slope_reduced = zip(*[reduce_rows(m) for m in micros])
     lanes_in = [send_lanes(x) for x in lanes_out]
 
-    teach = [
-        exchange(teacher[m].reshape(dp_count, chunk, width)) for m in micros
-    ]
-    masked = lax.all_to_all(
-        loss_mask.reshape(micro_count, dp_count, chunk), "dp", split_axis=1, concat_axis=1, tiled=True
-    )
     local_ids = group_index * seqs + jnp.arange(seqs, dtype=jnp.int32)
     targets = jnp.take(dealing, local_ids, axis=1)
     own_lengths = jnp.take(lengths, local_ids, axis=1)
@@ -751,16 +1134,7 @@
     valid = (positions[None, None, :] < own_lengths[:, :, None]).astype(f32)
     keep = jnp.take_along_axis(masked, targets[:, :, None], axis=1).astype(f32) * valid
     own_count = jnp.sum(keep)
-    valid = valid.reshape(micro_count, rows, 1)
-    keep = keep.reshape(micro_count, rows, 1)
-
-    w_expand, w_out, counts = gather_all(
-        [expand_weight, out_weight, jnp.full((8, 256), own_count, f32)], 2
-    )
-    w_expand = w_expand.reshape(reduced_width, gate_width)
-    w_out = w_out.reshape(gate_width, width)
-    count = jnp.sum(counts[:, :, 0, 0])
-    error_scale = (2.0 / (width * count)).reshape(1)
+    row_weights = jnp.stack([valid, keep], axis=-1).reshape(micro_count, rows, 2)
 
     table_np, inverse_np, sign_np = fourier_table(chunk)
     sign = jnp.asarray(sign_np)[:, None]
@@ -804,13 +1178,27 @@
             ),
         )(table2, inverse2, kernel_spec, values, grads)
 
-    mixed = [receive_lanes(convolve(x)) for x in lanes_in]
-    gates = [gate_rows(x) for x in normed]
-
-    def middle_rows(m):
+    convolved = [convolve(x) for x in lanes_in]
+    late = lax.optimization_barrier((expand_weight, out_weight, teacher_rows[0], *convolved))
+    w_expand, w_out, counts, *more, gate, slope = gather_all(
+        [late[0], late[1], jnp.full((8, 256), own_count, f32)],
+        [late[2]],
+        2,
+        gate_work(normed, first, gate_width),
+    )
+    teach = [*more, *swapped[1:]]
+    w_expand = w_expand.reshape(reduced_width, gate_width)
+    w_out = w_out.reshape(gate_width, width)
+    count = jnp.sum(counts[:, :, 0, 0])
+    error_scale = (2.0 / (width * count)).reshape(1)
+    mixed = [receive_lanes(x) for x in convolved]
+    def middle_rows(m, *earlier):
         teach_specs = [
             pl.BlockSpec((1, chunk, width), functools.partial(teach_block, s)) for s in range(middle_block)
         ]
+        gate_spec = pl.BlockSpec(
+            (middle_block * chunk, gate_width), lambda i, *_: (m * middle_steps + i, 0)
+        )
         wide, narrow = row_spec(gate_width, middle_block), row_spec(width, middle_block)
         return pl.pallas_call(
             functools.partial(middle_body, dims(middle_block), middle_block, 768),
@@ -819,15 +1207,15 @@
                 grid=(middle_steps,),
                 in_specs=[
                     lane_spec(middle_block),
-                    wide,
-                    wide,
+                    gate_spec,
+                    gate_spec,
                     shared((reduced_width, gate_width), (0, 0)),
                     shared((gate_width, width), (0, 0)),
                     tokens_spec(m, middle_block),
                     tokens_spec(m, middle_block),
-                    row_spec(1, middle_block),
-                    row_spec(1, middle_block),
+                    row_spec(2, middle_block),
                     *teach_specs,
+                    *[ANY] * len(earlier),
                 ],
                 out_specs=[
                     row_spec(reduced_width, middle_block),
@@ -835,7 +1223,7 @@
                     narrow,
                     wide,
                     wide,
-                    sequence_spec(middle_block),
+                    tokens_spec(m, middle_block),
                     narrow,
                     pl.BlockSpec((1, 8, width), lambda i, *_: (i, 0, 0)),
                     lane_spec(middle_block),
@@ -848,11 +1236,12 @@
                 jax.ShapeDtypeStruct((rows, width), bf16),
                 jax.ShapeDtypeStruct((rows, gate_width), bf16),
                 jax.ShapeDtypeStruct((rows, gate_width), bf16),
-                jax.ShapeDtypeStruct((seqs, chunk, width), bf16),
-                jax.ShapeDtypeStruct((rows, width), f32),
+                jax.ShapeDtypeStruct(tokens.shape, bf16),
+                jax.ShapeDtypeStruct((rows, width), bf16),
                 jax.ShapeDtypeStruct((middle_steps, 8, width), f32),
                 jax.ShapeDtypeStruct(lane_shape, bf16),
             ],
+            input_output_aliases={10 + middle_block: 5} if earlier else {},
             compiler_params=params(),
             cost_estimate=pl.CostEstimate(
                 flops=4 * rows * gate_width * (width + reduced_width),
@@ -860,14 +1249,14 @@
                 transcendentals=0,
             ),
         )(
-            targets[m], error_scale, mixed[m], *gates[m], w_expand, w_out, tokens, cotangent,
-            valid[m], keep[m], *[teach[m]] * middle_block,
+            targets[m], error_scale, mixed[m], gate, slope, w_expand, w_out, tokens, cotangent,
+            row_weights[m], *[teach[m]] * middle_block, *earlier,
         )
 
     def teach_block(s, i, order, scale):
         return (order[i * middle_block + s], 0, 0)
 
-    def input_rows(m, back, gate_grad, full_grad):
+    def input_rows(m, back, gate_grad, full_grad, *earlier):
         eight = pl.BlockSpec((1, 8, width), lambda i, *_: (i, 0, 0))
         return pl.pallas_call(
             functools.partial(input_body, dims(per_block)),
@@ -881,34 +1270,38 @@
                 tokens_spec(m, per_block),
                 whole((1, width)),
                 row_spec(width),
+                *[ANY] * len(earlier),
             ],
-            out_specs=[sequence_spec(per_block), row_spec(reduced_width), eight, eight],
+            out_specs=[tokens_spec(m, per_block), row_spec(reduced_width), eight, eight],
             out_shape=[
-                jax.ShapeDtypeStruct((seqs, chunk, width), bf16),
+                jax.ShapeDtypeStruct(tokens.shape, bf16),
                 jax.ShapeDtypeStruct((rows, reduced_width), bf16),
                 jax.ShapeDtypeStruct((steps, 8, width), f32),
                 jax.ShapeDtypeStruct((steps, 8, width), f32),
             ],
             scratch_shapes=[pltpu.VMEM((per_block * chunk, reduced_width), bf16)],
+            input_output_aliases={8: 0} if earlier else {},
             compiler_params=params(),
             cost_estimate=pl.CostEstimate(
                 flops=2 * rows * width * (gate_width + reduced_width),
                 bytes_accessed=4 * rows * gate_width + 8 * rows * width,
                 transcendentals=0,
             ),
-        )(back, slope_reduced[m], gate_grad, first, first, tokens, gain_row, full_grad)
-
-    middle = [middle_rows(m) for m in micros]
-    state_out, product, branch_grad, expanded_grad, gate_grad, outputs, full_grad, error_rows, lane_grad = zip(*middle)
+        )(back, slope_reduced[m], gate_grad, first, first, tokens, gain_row, full_grad, *earlier)
+
+    middle = []
+    for m in micros:
+        middle.append(middle_rows(m, *[x[5] for x in middle[-1:]]))
+    outputs = middle[-1][5]
+    state_out, product, branch_grad, expanded_grad, gate_grad, _, full_grad, error_rows, lane_grad = zip(*middle)
     grads_in = [send_lanes(x) for x in lane_grad]
     back, kernel_grads = zip(*[convolve_back(lanes_in[m], grads_in[m]) for m in micros])
     back = [receive_lanes(x) for x in back]
-    out_grad = weight_grad(product, branch_grad, 512)
-    expand_grad = weight_grad(state_out, expanded_grad, 256)
-    gate_weight_grad = weight_grad(normed, gate_grad, 256)
-    ends = [input_rows(m, back[m], gate_grad[m], full_grad[m]) for m in micros]
-    returned, reduced_grad, gain_rows, bias_rows = zip(*ends)
-    reduce_grad = weight_grad(normed, reduced_grad, 512)
+    ends = []
+    for m in micros:
+        ends.append(input_rows(m, back[m], gate_grad[m], full_grad[m], *[x[0] for x in ends[-1:]]))
+    returned = ends[-1][0]
+    _, reduced_grad, gain_rows, bias_rows = zip(*ends)
 
     kernel_total = sum(kernel_grads)
     if not direct:
@@ -917,6 +1310,7 @@
     kernel_grad = jnp.einsum(
         "kt,ckh->hct", jnp.asarray(inverse_np), kernel_total + sign * following, precision=highest
     ).reshape(own, seq_length)
+    kernel_grad, _ = lax.optimization_barrier((kernel_grad, reduced_grad))
     kernel_grad = lax.psum_scatter(kernel_grad, "fsdp", scatter_dimension=0, tiled=True)
     pair_grad, decay_grad, frequency_grad, step_grad = kernel_backward(
         kernel_grad, state_weight, decay_rate, frequency, factors
@@ -927,22 +1321,25 @@
     error_total = jnp.full((devices, 1, share), jnp.sum(sum(error_rows)))
     sums = jnp.concatenate([gain_total, bias_total, error_total], axis=1)
     sums = jnp.pad(sums, ((0, 0), (0, 5), (0, 128 - share)))
-    out_sum, expand_sum, gate_sum, reduce_sum, sums = scatter_all(
-        [
-            out_grad.reshape(devices, -1, width),
-            expand_grad.reshape(devices, -1, gate_width),
-            gate_weight_grad.reshape(devices, -1, gate_width),
-            reduce_grad.reshape(devices, -1, reduced_width),
-            sums,
-        ],
-        [4, 2, 4, 1, 1],
-        3,
-    )
+    pairs = [
+        (normed, gate_grad),
+        (state_out, expanded_grad),
+        (product, branch_grad),
+        (normed, reduced_grad),
+    ]
+    if all(left[0].shape[1] // devices % 16 == 0 for left, _ in pairs):
+        lefts, rights = zip(*pairs)
+        gate_sum, expand_sum, out_sum, reduce_sum, sums = product_scatter(lefts, rights, sums, 3)
+    else:
+        made = [weight_grad(left, right, 256) for left, right in pairs]
+        gate_sum, expand_sum, out_sum, reduce_sum, sums = scatter_all(
+            [x.reshape(devices, -1, x.shape[1]) for x in made] + [sums], [4, 2, 4, 1, 1], 3
+        )
     loss_value = sums[2, 0] / (width * count)
     return (
-        jnp.stack(outputs),
+        outputs,
         loss_value,
-        jnp.stack(returned),
+        returned,
         sums[0, :share],
         sums[1, :share],
         gate_sum,

time: 729 us -> 592 us (0.81)
  waiting for transfers between devices: 105 us -> 50.3 us
  Pallas kernels: 449 us -> 407 us
  starting transfers between devices: 52.2 us -> 35 us
  other arithmetic: 40.1 us -> 24.3 us
    pallas_call x9 -> x3, Pallas kernels: 304 us -> 263 us  [the longest x2 160 us: gather_all(): pl.pallas_call(functools.partial(gather_body, dp_count, bits, n, n_swap,...]
    all_to_all x10 -> x8, waiting for transfers between devices: 87.6 us -> 50.3 us  [exchange(): return lax.all_to_all(values, 'dp', split_axis=0, concat_axis=0, tiled=True)]
    unnamed x2, waiting for transfers between devices: 17 us -> 0.02 us
    all_to_all x10 -> x8, starting transfers between devices: 45.8 us -> 35 us  [exchange(): return lax.all_to_all(values, 'dp', split_axis=0, concat_axis=0, tiled=True)]
    another operation x2 -> x1, other arithmetic: 8.69 us -> 0.01 us  [shards(): jnp.stack([valid, keep], axis=-1).reshape(micro_count, rows, 2)]
    unnamed x76 -> x88, local copies, waits for them, and re-layouts: 14.7 us -> 16.7 us
  transfers between devices with their start and end apart: 12 -> 9, of which waited for: 4 -> 4; matrix products, arithmetic and copies ran while one was open for 10% -> 5% of each run, Pallas kernels for 46% -> 53%
where the time goes in v3:
time: 592 us; the launch traced here: 587 us
  Pallas kernels  407 us (69%)
  waiting for transfers between devices  50.3 us (8%)
  starting transfers between devices  35 us (6%)
  local copies, waits for them, and re-layouts  32.9 us (6%)
  other arithmetic  24.3 us (4%)
  between operations  17.4 us (3%)
  blocking collectives  10.6 us (2%)
  matrix products  9.04 us (2%)
    pallas_call x2, Pallas kernels, gather_all(): pl.pallas_call(functools.partial(gather_body, dp_count, bits, n, n_swap,...  160 us
    pallas_call x1, Pallas kernels, product_scatter(): pl.pallas_call(functools.partial(product_scatter_body, dp_count, bits, pl...  103 us
    pallas_call x2, Pallas kernels, middle_rows(): pl.pallas_call(functools.partial(middle_body, dims(middle_block), middle_...  64.5 us
    all_to_all x8, waiting for transfers between devices, exchange(): return lax.all_to_all(values, 'dp', split_axis=0, concat_axis=0, tiled=True)  50.3 us
    all_to_all x8, starting transfers between devices, exchange(): return lax.all_to_all(values, 'dp', split_axis=0, concat_axis=0, tiled=True)  35 us
    pallas_call x2, Pallas kernels, input_rows(): pl.pallas_call(functools.partial(input_body, dims(per_block)), grid=(step...  33.9 us
    pallas_call x2, Pallas kernels, convolve_back(): pl.pallas_call(convolve_back_body, out_shape=[jax.ShapeDtypeStruct(blocks...  19.8 us
    unnamed x88, local copies, waits for them, and re-layouts  16.7 us
  transfers between devices with their start and end apart: 9, of which 4 were waited for; matrix products, arithmetic and copies ran while one was open for 5% of the time, Pallas kernels for 53%

profile of v3, /device:TPU:0, one launch (start us, length us, event | category | flops | bytes accessed | tf_op | source)
XLA Modules:
  0.0 586.9 jit_solution(316553872631261178)
XLA Ops:
  8.0 4.0 fusion.28
  12.3 75.1 %shard_map.300 = (bf16[4,8,32,3584]{3,2,1,0:T(8,128)(2,1)S(1)}, bf16[4,8,16,256]{3,2,1,0:T(8,128)(2,1)S(1)}, s32[4,8,256]{2,1,0:T(8,128)S(1)}, bf16[4,256,1024]{2,1,0:T(8,128)(2,1)S(1)}) custom-call(bf16[32,3584]{1,0:T(8,128)(2,1)S(1)} %pad_maximum_fusion.refs_0_, bf16[16,256]{1,0:T(8,128)(2,1)S(1)} %scatter.9.refs_1_, s32[4,8,256]{2,1,0:T(8,128)S(1)} %pad.18.refs_2_, ...), custom_call_target="tpu_custom_call" | custom-call | bytes 152043520 | tf_op jit(solution)/shard_map/pallas_call | solution.py:160
  87.4 2.9 copy-done
  93.1 5.8 shard_map.301
  98.9 3.7 all-to-all-start
  103.4 5.8 shard_map.303
  109.9 17.8 %all-to-all-done.rows_ref = bf16[4,256,512]{2,1,0:T(8,128)(2,1)S(1)} async-done(((bf16[4,256,512]{2,1,0:T(8,128)(2,1)}), bf16[4,256,512]{2,1,0:T(8,128)(2,1)S(1)}, u32[]{:S(2)}, u32[]{:S(2)}) %all-to-all-start) | async-done | bytes 1048608 | tf_op jit(solution)/shard_map/all_to_all | solution.py:323
  127.8 4.6 all-to-all-start.1
  132.5 8.8 %multiply_subtract_fusion = (f32[16,32,512]{2,1,0:T(8,128)S(1)}, f32[16,32,512]{2,1,0:T(8,128)S(1)}, f32[16,32,512]{2,1,0:T(8,128)S(1)}, f32[16,32,512]{2,1,0:T(...) fusion(f32[16,512]{1,0:T(8,128)S(1)} %get-tuple-element.172, f32[16,512]{1,0:T(8,128)S(1)} %get-tuple-element.171, ...), kind=kLoop, calls=%fused_computation.35 | loop fusion | flops 3932160 | bytes 6422784 | tf_op jit(solution)/shard_map/sub | solution.py:982
  141.2 2.0 fusion
  143.4 10.6 %all_gather.3 = f32[128,1024]{1,0:T(8,128)S(1)} all-gather(f32[16,1024]{1,0:T(8,128)S(1)} %reshape.220), channel_id=1, replica_groups=mesh['dp'=4,'fsdp'=8] {'fsdp'}, dimensions={0}, use_global_device_ids=true | all-gather | bytes 589824 | tf_op jit(solution)/shard_map/all_gather | solution.py:1144
  156.6 7.2 %shard_map.302 = bf16[4,256,512]{2,1,0:T(8,128)(2,1)} custom-call(bf16[2,512,256]{2,1,0:T(8,128)(2,1)} %constant.113.clone.table_ref, bf16[2,512,256]{2,1,0:T(8,128)(2,1)} %constant.114.clone.inverse_ref, f32[4,512,128]{2,1,0:T(8,128)} %multiply_add_fusion.kernel_ref, bf16[4,256,512]{2,1,0:T(8,128)(2,1)} %copy-done.12), custom_call_target="tpu_custom_call" | custom-call | flops 2684354560 | bytes 8388608 | tf_op jit(solution)/shard_map/pallas_call | solution.py:1157
  163.8 5.4 all-to-all-start.3
  174.5 7.4 %shard_map.304 = bf16[4,256,512]{2,1,0:T(8,128)(2,1)} custom-call(bf16[2,512,256]{2,1,0:T(8,128)(2,1)} %constant.113.clone.table_ref, bf16[2,512,256]{2,1,0:T(8,128)(2,1)} %constant.114.clone.inverse_ref, f32[4,512,128]{2,1,0:T(8,128)} %multiply_add_fusion.kernel_ref, bf16[4,256,512]{2,1,0:T(8,128)(2,1)} %all-to-all-done.1.rows_ref), custom_call_target="tpu_custom_call" | custom-call | flops 2684354560 | bytes 8388608 | tf_op jit(solution)/shard_map/pallas_call | solution.py:1157
  185.7 84.7 %shard_map.305 = (bf16[4,8,16,3072]{3,2,1,0:T(8,128)(2,1)S(1)}, bf16[4,8,96,1024]{3,2,1,0:T(8,128)(2,1)}, f32[4,8,8,256]{3,2,1,0:T(8,128)S(1)}, bf16[4,256,1024]...) custom-call(bf16[16,3072]{1,0:T(8,128)(2,1)S(1)} %copy-done.5, ...), custom_call_target="tpu_custom_call" | custom-call | bytes 193986560 | tf_op jit(solution)/shard_map/pallas_call | solution.py:160
  274.7 3.5 all-to-all-start.2
  278.3 32.2 %shard_map.306 = (bf16[1024,512]{1,0:T(8,128)(2,1)}, bf16[1024,3072]{1,0:T(8,128)(2,1)}, bf16[1024,1024]{1,0:T(8,128)(2,1)}, bf16[1024,3072]{1,0:T(8,128)(2,1)},...) custom-call(s32[4]{0:T(128)} %get-tuple-element.154.order_ref, ...), custom_call_target="tpu_custom_call" | custom-call | flops 19327352832 | bytes 48234496 | tf_op jit(solution)/shard_map/pallas_call | solution.py:1203
  310.5 5.4 all-to-all-start.4
  316.0 32.2 %shard_map.307 = (bf16[1024,512]{1,0:T(8,128)(2,1)}, bf16[1024,3072]{1,0:T(8,128)(2,1)}, bf16[1024,1024]{1,0:T(8,128)(2,1)}, bf16[1024,3072]{1,0:T(8,128)(2,1)},...) custom-call(s32[4]{0:T(128)} %get-tuple-element.155.order_ref, ...), custom_call_target="tpu_custom_call", output_to_operand_aliasing={{5}: (11, {})} | custom-call | flops 19327352832 | bytes 48234496 | tf_op jit(solution)/shard_map/pallas_call | solution.py:1203
  348.2 5.1 all-to-all-start.6
  353.3 9.9 %shard_map.308 = (bf16[4,256,512]{2,1,0:T(8,128)(2,1)}, f32[4,512,128]{2,1,0:T(8,128)}) custom-call(bf16[2,512,256]{2,1,0:T(8,128)(2,1)} %constant.113.clone.table_ref, bf16[2,512,256]{2,1,0:T(8,128)(2,1)} %constant.114.clone.inverse_ref, f32[4,512,128]{2,1,0:T(8,128)} %multiply_add_fusion.kernel_ref, bf16[4,256,512]{2,1,0:T(8,128)(2,1)} %copy-done.12, ...), custom_call_target="tpu_custom_call" | custom-call | flops 3758096384 | bytes 8388608 | tf_op jit(solution)/shard_map/pallas_call | solution.py:1168
  363.2 14.4 %all-to-all-done.6.grad_ref = bf16[4,256,512]{2,1,0:T(8,128)(2,1)S(1)} async-done(((bf16[4,256,512]{2,1,0:T(8,128)(2,1)}), bf16[4,256,512]{2,1,0:T(8,128)(2,1)S(1)}, u32[]{:S(2)}, u32[]{:S(2)}) %all-to-all-start.6) | async-done | bytes 1048608 | tf_op jit(solution)/shard_map/all_to_all | solution.py:323
  377.6 3.7 all-to-all-start.5
  381.3 9.9 %shard_map.310 = (bf16[4,256,512]{2,1,0:T(8,128)(2,1)}, f32[4,512,128]{2,1,0:T(8,128)}) custom-call(bf16[2,512,256]{2,1,0:T(8,128)(2,1)} %constant.113.clone.table_ref, bf16[2,512,256]{2,1,0:T(8,128)(2,1)} %constant.114.clone.inverse_ref, f32[4,512,128]{2,1,0:T(8,128)} %multiply_add_fusion.kernel_ref, bf16[4,256,512]{2,1,0:T(8,128)(2,1)} %all-to-all-done.1.rows_ref, ...), custom_call_target="tpu_custom_call" | custom-call | flops 3758096384 | bytes 8388608 | tf_op jit(solution)/shard_map/pallas_call | solution.py:1168
  391.3 15.2 %all-to-all-done.5.back_ref = bf16[4,256,512]{2,1,0:T(8,128)(2,1)S(1)} async-done(((bf16[4,256,512]{2,1,0:T(8,128)(2,1)}), bf16[4,256,512]{2,1,0:T(8,128)(2,1)S(1)}, u32[]{:S(2)}, u32[]{:S(2)}) %all-to-all-start.5) | async-done | bytes 1048608 | tf_op jit(solution)/shard_map/all_to_all | solution.py:323
  406.5 3.5 all-to-all-start.7
  415.4 17.1 %shard_map.309 = (bf16[2,4,256,1024]{3,2,1,0:T(8,128)(2,1)}, bf16[1024,512]{1,0:T(8,128)(2,1)}, f32[2,8,1024]{2,1,0:T(8,128)}, f32[2,8,1024]{2,1,0:T(8,128)}) custom-call(bf16[4,256,512]{2,1,0:T(8,128)(2,1)} %copy-done.9, f32[1024,512]{1,0:T(8,128)} %get-tuple-element.124.slope_ref, bf16[1024,3072]{1,0:T(8,128)(2,1)} %get-tuple-element.116.gate_grad_ref.refs_6_, ...), custom_call_target="tpu_custom_call" | custom-call | flops 7516192768 | bytes 20971520 | tf_op jit(solution)/shard_map/pallas_call | solution.py:1261
  432.4 2.8 all-to-all-done.7.back_ref
  436.2 16.9 %shard_map.311 = (bf16[2,4,256,1024]{3,2,1,0:T(8,128)(2,1)}, bf16[1024,512]{1,0:T(8,128)(2,1)}, f32[2,8,1024]{2,1,0:T(8,128)}, f32[2,8,1024]{2,1,0:T(8,128)}) custom-call(bf16[4,256,512]{2,1,0:T(8,128)(2,1)} %copy-done.10, f32[1024,512]{1,0:T(8,128)} %get-tuple-element.129.slope_ref, ...), custom_call_target="tpu_custom_call", output_to_operand_aliasing={{0}: (8, {})} | custom-call | flops 7516192768 | bytes 20971520 | tf_op jit(solution)/shard_map/pallas_call | solution.py:1261
  456.8 103.2 %shard_map.312 = (f32[32,3072]{1,0:T(8,128)}, f32[16,3072]{1,0:T(8,128)}, f32[96,1024]{1,0:T(8,128)}, f32[32,512]{1,0:T(8,128)}, f32[8,128]{1,0:T(8,128)}) custom-call(bf16[1024,1024]{1,0:T(8,128)(2,1)} %get-tuple-element.101.refs_4_.refs_0_, bf16[1024,1024]{1,0:T(8,128)(2,1)} %get-tuple-element.102.refs_5_.refs_1_, ...), custom_call_target="tpu_custom_call" | custom-call | flops 34359738368 | bytes 104857600 | tf_op jit(solution)/shard_map/pallas_call | solution.py:793
  564.7 4.0 fusion.7
  568.9 5.1 subtract_reduce_fusion
  (158 shorter events, 39.4 us)
Async XLA Ops:
  98.9 28.8 %all-to-all-start = ((bf16[4,256,512]{2,1,0:T(8,128)(2,1)}), bf16[4,256,512]{2,1,0:T(8,128)(2,1)S(1)}, u32[]{:S(2)}, u32[]{:S(2)}) async-start(bf16[4,256,512]{2,1,0:T(8,128)(2,1)} %get-tuple-element.95), calls=%async_computation | async-start | bytes 2097152 | tf_op jit(solution)/shard_map/all_to_all | solution.py:323
  103.3 5.9 copy-start.39
  103.3 6.5 %copy-start.20 = (f32[2,16,512]{2,1,0:T(8,128)S(1)}, f32[2,16,512]{2,1,0:T(8,128)}, u32[]{:S(2)}) copy-start(f32[2,16,512]{2,1,0:T(8,128)} %param.37) | copy-start | bytes 196612
  103.4 6.5 %copy-start.25 = (f32[16,512]{1,0:T(8,128)S(1)}, f32[16,512]{1,0:T(8,128)}, u32[]{:S(2)}) copy-start(f32[16,512]{1,0:T(8,128)} %param.38) | copy-start | bytes 98308
  103.4 6.5 %copy-start.27 = (f32[16,512]{1,0:T(8,128)S(1)}, f32[16,512]{1,0:T(8,128)}, u32[]{:S(2)}) copy-start(f32[16,512]{1,0:T(8,128)} %param.39) | copy-start | bytes 98308
  127.8 13.5 %copy-start.12 = (bf16[4,256,512]{2,1,0:T(8,128)(2,1)}, bf16[4,256,512]{2,1,0:T(8,128)(2,1)S(1)}, u32[]{:S(2)}) copy-start(bf16[4,256,512]{2,1,0:T(8,128)(2,1)S(1)} %all-to-all-done.rows_ref) | copy-start | bytes 3145732
  127.8 36.0 %all-to-all-start.1 = ((bf16[4,256,512]{2,1,0:T(8,128)(2,1)}), bf16[4,256,512]{2,1,0:T(8,128)(2,1)}, u32[]{:S(2)}, u32[]{:S(2)}) async-start(bf16[4,256,512]{2,1,0:T(8,128)(2,1)} %get-tuple-element.96), calls=%async_computation.1 | async-start | bytes 2097152 | tf_op jit(solution)/shard_map/all_to_all | solution.py:323
  143.3 11.0 %copy-start.17 = (f32[512,256,1]{1,0,2:T(8,128)S(1)}, f32[512,256,1]{1,0,2:T(8,128)}, u32[]{:S(2)}) copy-start(f32[512,256,1]{1,0,2:T(8,128)} %constant.149) | copy-start | bytes 1572868
  163.8 6.1 %copy-start.35 = (s32[2,32]{1,0:T(2,128)S(1)}, s32[2,32]{1,0:T(2,128)}, u32[]{:S(2)}) copy-start(s32[2,32]{1,0:T(2,128)} %param.30) | copy-start | bytes 772
  163.8 110.9 %all-to-all-start.3 = ((bf16[4,256,512]{2,1,0:T(8,128)(2,1)}), bf16[4,256,512]{2,1,0:T(8,128)(2,1)}, u32[]{:S(2)}, u32[]{:S(2)}) async-start(bf16[4,256,512]{2,1,0:T(8,128)(2,1)} %shard_map.302), calls=%async_computation.3 | async-start | bytes 2097152 | tf_op jit(solution)/shard_map/all_to_all | solution.py:323
  174.5 8.0 %copy-start.1 = (bf16[1,1,1024,1024]{3,2,1,0:T(8,128)(2,1)S(1)}, bf16[1,1,1024,1024]{3,2,1,0:T(8,128)(2,1)}, u32[]{:S(2)}) copy-start(bf16[1,1,1024,1024]{3,2,1,0:T(8,128)(2,1)} %get-tuple-element.162) | copy-start | bytes 6291460
  174.5 8.0 %copy-start.4 = (bf16[96,1024]{1,0:T(8,128)(2,1)S(1)}, bf16[96,1024]{1,0:T(8,128)(2,1)}, u32[]{:S(2)}) copy-start(bf16[96,1024]{1,0:T(8,128)(2,1)} %refs_1_) | copy-start | bytes 589828
  174.5 8.0 %copy-start.5 = (bf16[16,3072]{1,0:T(8,128)(2,1)S(1)}, bf16[16,3072]{1,0:T(8,128)(2,1)}, u32[]{:S(2)}) copy-start(bf16[16,3072]{1,0:T(8,128)(2,1)} %refs_0_) | copy-start | bytes 294916
  274.7 35.8 %all-to-all-start.2 = ((bf16[4,256,512]{2,1,0:T(8,128)(2,1)}), bf16[4,256,512]{2,1,0:T(8,128)(2,1)S(1)}, u32[]{:S(2)}, u32[]{:S(2)}) async-start(bf16[4,256,512]{2,1,0:T(8,128)(2,1)} %shard_map.304), calls=%async_computation.2 | async-start | bytes 2097152 | tf_op jit(solution)/shard_map/all_to_all | solution.py:323
  310.5 5.5 copy-start.13
  310.5 37.7 %all-to-all-start.4 = ((bf16[4,256,512]{2,1,0:T(8,128)(2,1)}), bf16[4,256,512]{2,1,0:T(8,128)(2,1)S(1)}, u32[]{:S(2)}, u32[]{:S(2)}) async-start(bf16[4,256,512]{2,1,0:T(8,128)(2,1)} %get-tuple-element.122), calls=%async_computation.4 | async-start | bytes 2097152 | tf_op jit(solution)/shard_map/all_to_all | solution.py:323
  348.2 29.4 %all-to-all-start.6 = ((bf16[4,256,512]{2,1,0:T(8,128)(2,1)}), bf16[4,256,512]{2,1,0:T(8,128)(2,1)S(1)}, u32[]{:S(2)}, u32[]{:S(2)}) async-start(bf16[4,256,512]{2,1,0:T(8,128)(2,1)} %get-tuple-element.127), calls=%async_computation.6 | async-start | bytes 2097152 | tf_op jit(solution)/shard_map/all_to_all | solution.py:323
  377.6 28.9 %all-to-all-start.5 = ((bf16[4,256,512]{2,1,0:T(8,128)(2,1)}), bf16[4,256,512]{2,1,0:T(8,128)(2,1)S(1)}, u32[]{:S(2)}, u32[]{:S(2)}) async-start(bf16[4,256,512]{2,1,0:T(8,128)(2,1)} %get-tuple-element.123), calls=%async_computation.5 | async-start | bytes 2097152 | tf_op jit(solution)/shard_map/all_to_all | solution.py:323
  391.3 18.8 %copy-start.23 = (f32[4,8,1024]{2,1,0:T(8,128)S(1)}, f32[4,8,1024]{2,1,0:T(8,128)}, u32[]{:S(2)}) copy-start(f32[4,8,1024]{2,1,0:T(8,128)} %get-tuple-element.137) | copy-start | bytes 393220
  391.3 18.8 %copy-start.24 = (f32[4,8,1024]{2,1,0:T(8,128)S(1)}, f32[4,8,1024]{2,1,0:T(8,128)}, u32[]{:S(2)}) copy-start(f32[4,8,1024]{2,1,0:T(8,128)} %get-tuple-element.138) | copy-start | bytes 393220
  406.5 6.7 %copy-start.9 = (bf16[4,256,512]{2,1,0:T(8,128)(2,1)}, bf16[4,256,512]{2,1,0:T(8,128)(2,1)S(1)}, u32[]{:S(2)}) copy-start(bf16[4,256,512]{2,1,0:T(8,128)(2,1)S(1)} %all-to-all-done.5.back_ref) | copy-start | bytes 3145732
  406.5 28.7 %all-to-all-start.7 = ((bf16[4,256,512]{2,1,0:T(8,128)(2,1)}), bf16[4,256,512]{2,1,0:T(8,128)(2,1)S(1)}, u32[]{:S(2)}, u32[]{:S(2)}) async-start(bf16[4,256,512]{2,1,0:T(8,128)(2,1)} %get-tuple-element.128), calls=%async_computation.7 | async-start | bytes 2097152 | tf_op jit(solution)/shard_map/all_to_all | solution.py:323
  410.0 153.2 %reduce-scatter.4.cloned.1.call-start = ((), (), s32[]{:S(2)}) async-start(), calls=%async_computation.9 | async-start | bytes 589824
  436.2 16.9 %copy-start.31 = (f32[2,8,1024]{2,1,0:T(8,128)S(1)}, f32[2,8,1024]{2,1,0:T(8,128)}, u32[]{:S(2)}) copy-start(f32[2,8,1024]{2,1,0:T(8,128)} %get-tuple-element.133) | copy-start | bytes 196612
  436.2 17.8 %copy-start.30 = (f32[2,8,1024]{2,1,0:T(8,128)S(1)}, f32[2,8,1024]{2,1,0:T(8,128)}, u32[]{:S(2)}) copy-start(f32[2,8,1024]{2,1,0:T(8,128)} %get-tuple-element.135) | copy-start | bytes 196612
  568.8 5.8 copy-start.26
  568.8 5.8 copy-start.28
  568.8 5.8 copy-start.36
  568.8 7.1 %copy-start.19 = (f32[32,3072]{1,0:T(8,128)S(1)}, f32[32,3072]{1,0:T(8,128)}, u32[]{:S(2)}) copy-start(f32[32,3072]{1,0:T(8,128)} %get-tuple-element.201) | copy-start | bytes 1179652
  568.8 7.8 %copy-start.29 = (f32[32,512]{1,0:T(8,128)S(1)}, f32[32,512]{1,0:T(8,128)}, u32[]{:S(2)}) copy-start(f32[32,512]{1,0:T(8,128)} %get-tuple-element.202) | copy-start | bytes 196612
  568.9 8.5 %copy-start.22 = (f32[16,3072]{1,0:T(8,128)S(1)}, f32[16,3072]{1,0:T(8,128)}, u32[]{:S(2)}) copy-start(f32[16,3072]{1,0:T(8,128)} %get-tuple-element.207) | copy-start | bytes 589828
  568.9 9.1 %copy-start.18 = (f32[96,1024]{1,0:T(8,128)S(1)}, f32[96,1024]{1,0:T(8,128)}, u32[]{:S(2)}) copy-start(f32[96,1024]{1,0:T(8,128)} %get-tuple-element.208) | copy-start | bytes 1179652
  (17 other events, 48.2 us)
Sparse Core Ops, SparseCore 0:
  456.1 36.0 reduce-scatter.3

commit v4 on v3

--- a/solution.py
+++ b/solution.py
@@ -13,7 +13,7 @@
 bf16 = jnp.bfloat16
 f32 = jnp.float32
 MESH = pl.DeviceIdType.MESH
-ANY = pl.BlockSpec(memory_space=pl.ANY)
+ANY = pl.BlockSpec(memory_space=pltpu.HBM)
 
 
 def bit_of(index, bit):
@@ -42,10 +42,13 @@
     return order
 
 
-def gather_body(dp_count, bits, n, n_swap, work, *refs):
-    n_work_in, n_work_out, n_work_scratch = work[0] if work else (0, 0, 0)
+def gather_body(dp_count, bits, n, leads, work, *refs):
+    n_swap = len(leads)
+    n_work_in, n_work_out = work[0] if work else (0, 0)
     moved = n + n_swap
-    ins, refs = refs[:moved], refs[moved:]
+    ins, refs = list(refs[:moved]), refs[moved:]
+    for e, lead in enumerate(leads):
+        ins[n + e] = ins[n + e].at[lead]
     work_ins, refs = refs[:n_work_in], refs[n_work_in:]
     outs, refs = refs[:moved], refs[moved:]
     work_outs, refs = refs[:n_work_out], refs[n_work_out:]
@@ -151,18 +154,19 @@
 
 def gather_all(arrays, swaps, collective_id, work=None):
     work_in, work_out, work_scratch, work_body = work or ((), (), (), None)
-    sizes = (len(work_in), len(work_out), len(work_scratch))
+    sizes = (len(work_in), len(work_out))
+    leads, swaps = [lead for lead, _ in swaps], [x for _, x in swaps]
     dp_count, fsdp_count = lax.axis_size("dp"), lax.axis_size("fsdp")
     bits = fsdp_count.bit_length() - 1
     n, n_swap = len(arrays), len(swaps)
     slots = 2 * dp_count * (fsdp_count - 1) * n
     total = dp_count * fsdp_count * sum(x.size * x.dtype.itemsize for x in arrays)
     return pl.pallas_call(
-        functools.partial(gather_body, dp_count, bits, n, n_swap, (sizes, work_body) if work else None),
+        functools.partial(gather_body, dp_count, bits, n, leads, (sizes, work_body) if work else None),
         out_shape=[
             jax.ShapeDtypeStruct((dp_count, fsdp_count, *x.shape), x.dtype) for x in arrays
         ]
-        + [jax.ShapeDtypeStruct(x.shape, x.dtype) for x in swaps]
+        + [jax.ShapeDtypeStruct(x.shape[1:], x.dtype) for x in swaps]
         + list(work_out),
         in_specs=[ANY] * (n + n_swap + sizes[0]),
         out_specs=[ANY] * (n + n_swap + sizes[1]),
@@ -177,7 +181,7 @@
             *work_scratch,
         ],
         compiler_params=pltpu.CompilerParams(
-            collective_id=collective_id, has_side_effects=True, vmem_limit_bytes=40 << 20
+            collective_id=collective_id, has_side_effects=True, vmem_limit_bytes=62 << 20
         ),
         cost_estimate=pl.CostEstimate(flops=0, bytes_accessed=20 * total, transcendentals=0),
     )(*arrays, *swaps, *work_in)
@@ -384,8 +388,8 @@
     channels_from_rows(out_ref, reduced, seqs, chunk, own)
 
 
-def gate_work(normed, first, gate_width):
-    rows, width = normed[0].shape
+def gate_work(normed, weight):
+    (rows, width), gate_width = normed[0].shape, weight.shape[1]
     micro_count, tile = len(normed), 512
     across, down = gate_width // tile, rows // tile
     count = micro_count * across * down
@@ -398,9 +402,7 @@
             for m in range(micro_count)
         ]
         loads.append(
-            pltpu.make_async_copy(
-                weight_ref.at[:, pl.ds(0, gate_width)], weight_buf, load_sem.at[micro_count]
-            )
+            pltpu.make_async_copy(weight_ref, weight_buf, load_sem.at[micro_count])
         )
         loaded = []
 
@@ -457,7 +459,7 @@
         pltpu.SemaphoreType.DMA((micro_count + 1,)),
         pltpu.SemaphoreType.DMA((2, 2)),
     ]
-    return [*normed, first], [shape, shape], scratch, body
+    return [*normed, weight], [shape, shape], scratch, body
 
 
 def middle_body(
@@ -531,11 +533,11 @@
     n = len(pieces)
     lefts, refs = refs[: n_left * micros], refs[n_left * micros :]
     rights, refs = refs[: n_right * micros], refs[n_right * micros :]
-    small_ref, refs = refs[0], refs[1:]
+    ready_ref, small_ref, refs = refs[0], refs[1], refs[2:]
     outs, refs = refs[: plan["outputs"]], refs[plan["outputs"] :]
     left_bufs, refs = refs[:n_left], refs[n_left:]
-    right_buf, left_sem, right_sem, load_sem, send, recv, store_sem = refs[:7]
-    sets = [refs[7 : 7 + 5 + 3 * (bits - 1)], refs[7 + 5 + 3 * (bits - 1) :]]
+    right_buf, left_sem, right_sem, load_sem, ready_sem, send, recv, store_sem = refs[:8]
+    sets = [refs[8 : 8 + 5 + 3 * (bits - 1)], refs[8 + 5 + 3 * (bits - 1) :]]
     d, f = lax.axis_index("dp"), lax.axis_index("fsdp")
     my = [bit_of(f, b) for b in range(bits)]
     upper = list(range(bits - 1, 0, -1))
@@ -576,7 +578,8 @@
                 pushed[(i, at)].wait_send()
                 drained.add((i, at))
 
-    jobs = [(i, *job) for i in range(n) if i != small for job in pieces[i][3]]
+    ready = plan["ready"]
+    jobs = [(i, *job) for i in range(ready, n - 1) for job in pieces[i][3]]
     loads = {}
 
     def fetch(j):
@@ -603,6 +606,22 @@
     ]
     small_load = pltpu.make_async_copy(small_ref, sets[1][0], load_sem)
     small_load.start()
+    lead = (slice(None),) * (bits + 1)
+    ready_loads = []
+    for i in range(ready):
+        _, rows, groups, piece_jobs = pieces[i]
+        ready_loads.append(
+            [
+                pltpu.make_async_copy(
+                    ready_ref.at[(*lead, slice(None), pl.ds(piece_jobs[0][2] + g * lane, lane))],
+                    bufs[i][0].at[(*lead, pl.ds(g * rows, rows), slice(None))],
+                    ready_sem.at[i, g],
+                )
+                for g in range(groups)
+            ]
+        )
+        for copy in ready_loads[i]:
+            copy.start()
     for a in range(n_left):
         for copy in left_loads[a]:
             copy.start()
@@ -648,6 +667,9 @@
         made, got = bufs[i][0], bufs[i][1]
         if i == small:
             small_load.wait()
+        elif i < ready:
+            for copy in ready_loads[i]:
+                copy.wait()
         else:
             make(i)
         lead = (slice(None),) * bits
@@ -686,16 +708,16 @@
             copies.append(
                 push(i, bits - 1 + o, to_dp.at[o - 1], from_dp.at[o - 1], {"dp": peer})
             )
-        waits[i] = (copies, own, more)
-
-    def finish(i):
-        copies, own, more = waits[i]
-        result, from_dp = bufs[i][4], bufs[i][3]
-        for copy in copies:
-            copy.wait_recv()
+        waits[i] = copies
         for store in stores.pop(i - slots, []):
             store.wait()
-        total = own[d] + more[d].astype(f32)
+        bufs[i][4][...] = own[d] + more[d].astype(f32)
+
+    def finish(i):
+        result, from_dp = bufs[i][4], bufs[i][3]
+        for copy in waits[i]:
+            copy.wait_recv()
+        total = result[...]
         for o in range(1, dp_count):
             total = total + from_dp[o - 1].astype(f32)
         result[...] = total
@@ -717,16 +739,18 @@
             store.start()
 
     for t in range((n + 1) // 2 + bits + 1):
-        for i in range(n):
-            s = t - i // 2
-            if s == 0:
-                first(i)
-            elif 1 <= s < bits:
-                middle(i, s)
-            elif s == bits:
-                last(i)
-            elif s == bits + 1:
-                finish(i)
+        for s in (*range(1, bits + 2), 0):
+            for i in range(2 * (t - s), min(2 * (t - s) + 2, n)):
+                if i < 0:
+                    continue
+                if s == 0:
+                    first(i)
+                elif s < bits:
+                    middle(i, s)
+                elif s == bits:
+                    last(i)
+                else:
+                    finish(i)
     for key, copy in pushed.items():
         if key not in drained:
             copy.wait_send()
@@ -735,7 +759,7 @@
             store.wait()
 
 
-def product_scatter(lefts, rights, small, collective_id):
+def product_scatter(lefts, rights, ready, small, collective_id):
     dp_count, fsdp_count = lax.axis_size("dp"), lax.axis_size("fsdp")
     bits = fsdp_count.bit_length() - 1
     devices = dp_count * fsdp_count
@@ -763,6 +787,7 @@
         "lane": lane,
         "outputs": len(lefts) + 1,
         "micros": len(lefts[0]),
+        "ready": sum(1 for k, _, _, jobs in pieces[:-1] if k == 0 and jobs[-1][2] + jobs[-1][3] <= ready.shape[1]),
     }
 
     def buffer_set(count, lead, rows, columns, dtype):
@@ -788,13 +813,14 @@
     micro_count, rows = len(lefts[0]), lefts[0][0].shape[0]
     steps = bits - 1 + dp_count
     small = small.reshape(dp_count, *(2,) * bits, *small.shape[1:])
+    ready = ready.reshape(dp_count, *(2,) * bits, -1, ready.shape[1])
     widths = [(a[0].shape[1], b[0].shape[1]) for a, b in zip(lefts, rights)]
     flops = sum(2 * micro_count * rows * a * b for a, b in widths)
     return pl.pallas_call(
         functools.partial(product_scatter_body, dp_count, bits, plan, len(unique), len(rights)),
         out_shape=[jax.ShapeDtypeStruct((a // devices, b), f32) for a, b in widths]
         + [jax.ShapeDtypeStruct(small.shape[-2:], f32)],
-        in_specs=[ANY] * ((len(unique) + len(rights)) * micro_count + 1),
+        in_specs=[ANY] * ((len(unique) + len(rights)) * micro_count + 2),
         out_specs=[ANY] * (len(lefts) + 1),
         scratch_shapes=[pltpu.VMEM((micro_count, *u[0].shape), bf16) for u in unique]
         + [
@@ -802,6 +828,7 @@
             pltpu.SemaphoreType.DMA((len(unique), micro_count)),
             pltpu.SemaphoreType.DMA((2, micro_count)),
             pltpu.SemaphoreType.DMA,
+            pltpu.SemaphoreType.DMA((slots, height // 16)),
             pltpu.SemaphoreType.DMA((n, steps)),
             pltpu.SemaphoreType.DMA((n, steps)),
             pltpu.SemaphoreType.DMA((n, height // 16)),
@@ -812,7 +839,7 @@
             collective_id=collective_id, has_side_effects=True, vmem_limit_bytes=62 << 20
         ),
         cost_estimate=pl.CostEstimate(flops=flops, bytes_accessed=100 << 20, transcendentals=0),
-    )(*[x for u in unique for x in u], *[x for r in rights for x in r], small)
+    )(*[x for u in unique for x in u], *[x for r in rights for x in r], ready, small)
 
 
 def weight_grad_body(n, *refs):
@@ -823,8 +850,8 @@
     out_ref[...] = total.astype(out_ref.dtype)
 
 
-def weight_grad(lefts, rights, row_tile):
-    n, (rows, height), width = len(lefts), lefts[0].shape, rights[0].shape[1]
+def weight_grad(lefts, rights, row_tile, width=None):
+    n, (rows, height), width = len(lefts), lefts[0].shape, width or rights[0].shape[1]
     return pl.pallas_call(
         functools.partial(weight_grad_body, n),
         grid=(height // row_tile,),
@@ -1050,14 +1077,15 @@
     small = jnp.zeros((16, 256), bf16).at[0, :share].set(norm_gain).at[1, :share].set(norm_bias)
     mask_rows = loss_mask.reshape(micro_count, dp_count, chunk).transpose(1, 0, 2)
     mask_rows = jnp.pad(mask_rows, ((0, 0), (0, 8 - micro_count), (0, 0)))
-    teacher_rows = [teacher[m].reshape(dp_count, chunk, width) for m in micros]
-    first, small, *swapped = gather_all(
-        [jnp.concatenate([gate_weight, reduce_weight], axis=1), small],
-        [mask_rows, *teacher_rows[1:]],
+    teacher_rows = teacher.reshape(micro_count, dp_count, chunk, width)
+    w_gate, w_reduce, small, *swapped = gather_all(
+        [gate_weight, reduce_weight, small],
+        [(0, mask_rows[None]), *[(m, teacher_rows) for m in micros[1:]]],
         1,
     )
     masked = swapped[0].transpose(1, 0, 2)[:micro_count]
-    first = first.reshape(width, gate_width + reduced_width)
+    w_gate = w_gate.reshape(width, gate_width)
+    w_reduce = w_reduce.reshape(width, reduced_width)
     gain_row = small[:, :, 0, :share].reshape(1, width).astype(f32)
     bias_row = small[:, :, 1, :share].reshape(1, width).astype(f32)
 
@@ -1100,7 +1128,7 @@
             values = values.reshape(1, rows, reduced_width)
         return values
 
-    def reduce_rows(m):
+    def reduce_rows(m, gain_row):
         return pl.pallas_call(
             functools.partial(reduce_body, dims(per_block)),
             grid=(steps,),
@@ -1113,7 +1141,7 @@
                 tokens_spec(m, per_block),
                 whole((1, width)),
                 whole((1, width)),
-                shared((width, reduced_width), (0, gate_width // reduced_width)),
+                whole((width, reduced_width)),
             ],
             out_specs=[row_spec(width), lane_spec(per_block), row_spec(reduced_width)],
             compiler_params=params(),
@@ -1122,10 +1150,7 @@
                 bytes_accessed=8 * rows * width,
                 transcendentals=2 * rows * reduced_width,
             ),
-        )(tokens, gain_row, bias_row, first)
-
-    normed, lanes_out, slope_reduced = zip(*[reduce_rows(m) for m in micros])
-    lanes_in = [send_lanes(x) for x in lanes_out]
+        )(tokens, gain_row, bias_row, w_reduce)
 
     local_ids = group_index * seqs + jnp.arange(seqs, dtype=jnp.int32)
     targets = jnp.take(dealing, local_ids, axis=1)
@@ -1135,12 +1160,25 @@
     keep = jnp.take_along_axis(masked, targets[:, :, None], axis=1).astype(f32) * valid
     own_count = jnp.sum(keep)
     row_weights = jnp.stack([valid, keep], axis=-1).reshape(micro_count, rows, 2)
+    counts = jnp.full((8, 256), own_count, f32)
+    row_weights = [row_weights[m] for m in micros]
+
+    reduced_rows = [reduce_rows(0, gain_row)]
+    held = lax.optimization_barrier((decay_rate, frequency, log_step, reduced_rows[0][1]))
+    factors = kernel_factors(*held[:3], seq_length)
+    own_kernel = kernel_forward(state_weight, factors)
+    for m in micros[1:]:
+        later_gain, own_kernel, row_weights, targets, counts = lax.optimization_barrier(
+            (gain_row, own_kernel, row_weights, targets, counts)
+        )
+        reduced_rows.append(reduce_rows(m, later_gain))
+    normed, lanes_out, slope_reduced = zip(*reduced_rows)
+    lanes_in = [send_lanes(x) for x in lanes_out]
+
 
     table_np, inverse_np, sign_np = fourier_table(chunk)
     sign = jnp.asarray(sign_np)[:, None]
     table2, inverse2 = jnp.asarray(high_and_low(table_np)), jnp.asarray(high_and_low(inverse_np))
-    factors = kernel_factors(decay_rate, frequency, log_step, seq_length)
-    own_kernel = kernel_forward(state_weight, factors)
     kernel = lax.all_gather(own_kernel, "fsdp", axis=0, tiled=True)
     segments = jnp.einsum(
         "kt,hct->ckh", jnp.asarray(table_np), kernel.reshape(own, dp_count, chunk), precision=highest
@@ -1179,12 +1217,12 @@
         )(table2, inverse2, kernel_spec, values, grads)
 
     convolved = [convolve(x) for x in lanes_in]
-    late = lax.optimization_barrier((expand_weight, out_weight, teacher_rows[0], *convolved))
+    late = lax.optimization_barrier((expand_weight, out_weight, *convolved))
     w_expand, w_out, counts, *more, gate, slope = gather_all(
-        [late[0], late[1], jnp.full((8, 256), own_count, f32)],
-        [late[2]],
+        [late[0], late[1], counts],
+        [(0, teacher_rows)],
         2,
-        gate_work(normed, first, gate_width),
+        gate_work(normed, w_gate),
     )
     teach = [*more, *swapped[1:]]
     w_expand = w_expand.reshape(reduced_width, gate_width)
@@ -1266,7 +1304,7 @@
                 row_spec(reduced_width),
                 row_spec(gate_width),
                 shared((width, gate_width), (0, 0)),
-                shared((width, reduced_width), (0, gate_width // reduced_width)),
+                shared((width, reduced_width), (0, 0)),
                 tokens_spec(m, per_block),
                 whole((1, width)),
                 row_spec(width),
@@ -1287,7 +1325,7 @@
                 bytes_accessed=4 * rows * gate_width + 8 * rows * width,
                 transcendentals=0,
             ),
-        )(back, slope_reduced[m], gate_grad, first, first, tokens, gain_row, full_grad, *earlier)
+        )(back, slope_reduced[m], gate_grad, w_gate, w_reduce, tokens, gain_row, full_grad, *earlier)
 
     middle = []
     for m in micros:
@@ -1296,7 +1334,9 @@
     state_out, product, branch_grad, expanded_grad, gate_grad, _, full_grad, error_rows, lane_grad = zip(*middle)
     grads_in = [send_lanes(x) for x in lane_grad]
     back, kernel_grads = zip(*[convolve_back(lanes_in[m], grads_in[m]) for m in micros])
-    back = [receive_lanes(x) for x in back]
+    ready = weight_grad(normed, gate_grad, 256, gate_width // 2)
+    held_back, ready = lax.optimization_barrier((back[0], ready))
+    back = [receive_lanes(x) for x in (held_back, *back[1:])]
     ends = []
     for m in micros:
         ends.append(input_rows(m, back[m], gate_grad[m], full_grad[m], *[x[0] for x in ends[-1:]]))
@@ -1329,7 +1369,9 @@
     ]
     if all(left[0].shape[1] // devices % 16 == 0 for left, _ in pairs):
         lefts, rights = zip(*pairs)
-        gate_sum, expand_sum, out_sum, reduce_sum, sums = product_scatter(lefts, rights, sums, 3)
+        gate_sum, expand_sum, out_sum, reduce_sum, sums = product_scatter(
+            lefts, rights, ready, sums, 3
+        )
     else:
         made = [weight_grad(left, right, 256) for left, right in pairs]
         gate_sum, expand_sum, out_sum, reduce_sum, sums = scatter_all(

time: 592 us -> 574 us (0.970)
  waiting for transfers between devices: 50.3 us -> 25.3 us
  Pallas kernels: 407 us -> 422 us
  local copies, waits for them, and re-layouts: 32.9 us -> 22 us
    all_to_all x8, waiting for transfers between devices: 50.3 us -> 25.3 us  [exchange(): return lax.all_to_all(values, 'dp', split_axis=0, concat_axis=0, tiled=True)]
    pallas_call x2 -> x3, Pallas kernels: 160 us -> 184 us  [the longest x2 173 us: gather_all(): pl.pallas_call(functools.partial(gather_body, dp_count, bits, n, leads, (...]
    unnamed x88 -> x60, local copies, waits for them, and re-layouts: 16.7 us -> 6.69 us
    pallas_call x1, Pallas kernels: 103 us -> 94 us  [product_scatter(): pl.pallas_call(functools.partial(product_scatter_body, dp_count, bits, pl...]
  transfers between devices with their start and end apart: 9 -> 9, of which waited for: 4 -> 5; matrix products, arithmetic and copies ran while one was open for 5% -> 6% of each run, Pallas kernels for 53% -> 56%
where the time goes in v4:
time: 574 us; the launch traced here: 570 us
  Pallas kernels  422 us (74%)
  starting transfers between devices  35.3 us (6%)
  other arithmetic  25.7 us (4%)
  waiting for transfers between devices  25.3 us (4%)
  local copies, waits for them, and re-layouts  22 us (4%)
  between operations  17.3 us (3%)
  matrix products  11.3 us (2%)
  blocking collectives  10.2 us (2%)
    pallas_call x2, Pallas kernels, gather_all(): pl.pallas_call(functools.partial(gather_body, dp_count, bits, n, leads, (...  173 us
    pallas_call x1, Pallas kernels, product_scatter(): pl.pallas_call(functools.partial(product_scatter_body, dp_count, bits, pl...  94 us
    pallas_call x2, Pallas kernels, middle_rows(): pl.pallas_call(functools.partial(middle_body, dims(middle_block), middle_...  64.5 us
    all_to_all x8, starting transfers between devices, exchange(): return lax.all_to_all(values, 'dp', split_axis=0, concat_axis=0, tiled=True)  35.3 us
    pallas_call x2, Pallas kernels, input_rows(): pl.pallas_call(functools.partial(input_body, dims(per_block)), grid=(step...  33.9 us
    all_to_all x8, waiting for transfers between devices, exchange(): return lax.all_to_all(values, 'dp', split_axis=0, concat_axis=0, tiled=True)  25.3 us
    pallas_call x2, Pallas kernels, convolve_back(): pl.pallas_call(convolve_back_body, out_shape=[jax.ShapeDtypeStruct(blocks...  19.9 us
    pallas_call x2, Pallas kernels, convolve(): pl.pallas_call(convolve_body, out_shape=jax.ShapeDtypeStruct(blocks, bf16...  14.5 us
  transfers between devices with their start and end apart: 9, of which 5 were waited for; matrix products, arithmetic and copies ran while one was open for 6% of the time, Pallas kernels for 56%

profile of v4, /device:TPU:0, one launch (start us, length us, event | category | flops | bytes accessed | tf_op | source)
XLA Modules:
  0.0 569.6 jit_solution(15260190713224743631)
XLA Ops:
  10.6 80.3 %shard_map.300 = (bf16[4,8,32,3072]{3,2,1,0:T(8,128)(2,1)}, bf16[4,8,32,512]{3,2,1,0:T(8,128)(2,1)}, bf16[4,8,16,256]{3,2,1,0:T(8,128)(2,1)}, s32[4,8,256]{2,1,0:T(8,128)}, bf16[4,256,1024]{2,1,0:T(8,128)(2,1)}) custom-call(bf16[32,3072]{1,0:T(8,128)(2,1)} %refs_0_.1, bf16[32,512]{1,0:T(8,128)(2,1)} %refs_1_.1, bf16[16,256]{1,0:T(8,128)(2,1)} %copy-done.20, ...), custom_call_target="tpu_custom_call" | custom-call | bytes 152043520 | tf_op jit(solution)/shard_map/pallas_call | solution.py:164
  93.3 5.8 %shard_map.301 = (bf16[1024,1024]{1,0:T(8,128)(2,1)}, bf16[4,256,512]{2,1,0:T(8,128)(2,1)}, f32[1024,512]{1,0:T(8,128)}) custom-call(bf16[2,4,256,1024]{3,2,1,0:T(8,128)(2,1)} %tokens_ref.11, f32[1,1024]{1,0:T(1,128)} %reshape.246.gain_ref, f32[1,1024]{1,0:T(1,128)} %reshape.247.bias_ref, bf16[1024,512]{1,0:T(8,128)(2,1)} %bitcast.76), custom_call_target="tpu_custom_call" | custom-call | flops 1073741824 | bytes 8388608 | tf_op jit(solution)/shard_map/pallas_call | solution.py:1132
  99.1 3.8 all-to-all-start
  109.1 8.8 %multiply_subtract_fusion = (f32[16,32,512]{2,1,0:T(8,128)S(1)}, f32[16,32,512]{2,1,0:T(8,128)S(1)}, f32[16,32,512]{2,1,0:T(8,128)S(1)}, f32[16,32,512]{2,1,0:T(...) fusion(f32[16,512]{1,0:T(8,128)S(1)} %get-tuple-element.192, f32[16,512]{1,0:T(8,128)S(1)} %get-tuple-element.191, ...), kind=kLoop, calls=%fused_computation.35 | loop fusion | flops 3932160 | bytes 6422784 | tf_op jit(solution)/shard_map/sub | solution.py:1009
  117.8 2.0 fusion
  121.9 5.7 %shard_map.303 = (bf16[1024,1024]{1,0:T(8,128)(2,1)}, bf16[4,256,512]{2,1,0:T(8,128)(2,1)}, f32[1024,512]{1,0:T(8,128)}) custom-call(bf16[2,4,256,1024]{3,2,1,0:T(8,128)(2,1)} %tokens_ref.11, f32[1,1024]{1,0:T(1,128)} %reshape.246.gain_ref, f32[1,1024]{1,0:T(1,128)} %reshape.247.bias_ref, bf16[1024,512]{1,0:T(8,128)(2,1)} %bitcast.77), custom_call_target="tpu_custom_call" | custom-call | flops 1073741824 | bytes 8388608 | tf_op jit(solution)/shard_map/pallas_call | solution.py:1132
  128.0 4.8 all-to-all-start.1
  132.8 10.2 %all_gather.3 = f32[128,1024]{1,0:T(8,128)S(1)} all-gather(f32[16,1024]{1,0:T(8,128)S(1)} %reshape.234), channel_id=1, replica_groups=mesh['dp'=4,'fsdp'=8] {'fsdp'}, dimensions={0}, use_global_device_ids=true | all-gather | bytes 589824 | tf_op jit(solution)/shard_map/all_gather | solution.py:1182
  143.2 2.1 convolution_bitcast_fusion
  146.5 7.3 %shard_map.302 = bf16[4,256,512]{2,1,0:T(8,128)(2,1)} custom-call(bf16[2,512,256]{2,1,0:T(8,128)(2,1)} %constant.113.clone.table_ref, bf16[2,512,256]{2,1,0:T(8,128)(2,1)} %constant.114.clone.inverse_ref, f32[4,512,128]{2,1,0:T(8,128)} %multiply_add_fusion.kernel_ref, bf16[4,256,512]{2,1,0:T(8,128)(2,1)} %copy-done.1), custom_call_target="tpu_custom_call" | custom-call | flops 2684354560 | bytes 8388608 | tf_op jit(solution)/shard_map/pallas_call | solution.py:1195
  153.8 3.7 all-to-all-done.1.rows_ref
  157.5 4.6 all-to-all-start.3
  162.9 7.2 %shard_map.304 = bf16[4,256,512]{2,1,0:T(8,128)(2,1)} custom-call(bf16[2,512,256]{2,1,0:T(8,128)(2,1)} %constant.113.clone.table_ref, bf16[2,512,256]{2,1,0:T(8,128)(2,1)} %constant.114.clone.inverse_ref, f32[4,512,128]{2,1,0:T(8,128)} %multiply_add_fusion.kernel_ref, bf16[4,256,512]{2,1,0:T(8,128)(2,1)} %all-to-all-done.1.rows_ref), custom_call_target="tpu_custom_call" | custom-call | flops 2684354560 | bytes 8388608 | tf_op jit(solution)/shard_map/pallas_call | solution.py:1195
  170.1 92.2 %shard_map.305 = (bf16[4,8,16,3072]{3,2,1,0:T(8,128)(2,1)}, bf16[4,8,96,1024]{3,2,1,0:T(8,128)(2,1)}, f32[4,8,8,256]{3,2,1,0:T(8,128)}, bf16[4,256,1024]{2,1,0:T...) custom-call(bf16[16,3072]{1,0:T(8,128)(2,1)} %refs_0_.2, bf16[96,1024]{1,0:T(8,128)(2,1)} %refs_1_.2, ...), custom_call_target="tpu_custom_call" | custom-call | bytes 193986560 | tf_op jit(solution)/shard_map/pallas_call | solution.py:164
  264.6 3.5 all-to-all-start.2
  268.1 32.3 %shard_map.306 = (bf16[1024,512]{1,0:T(8,128)(2,1)}, bf16[1024,3072]{1,0:T(8,128)(2,1)}, bf16[1024,1024]{1,0:T(8,128)(2,1)}, bf16[1024,3072]{1,0:T(8,128)(2,1)},...) custom-call(s32[4]{0:T(128)} %get-tuple-element.176.order_ref, ...), custom_call_target="tpu_custom_call" | custom-call | flops 19327352832 | bytes 48234496 | tf_op jit(solution)/shard_map/pallas_call | solution.py:1241
  300.4 5.0 all-to-all-start.4
  305.5 32.2 %shard_map.307 = (bf16[1024,512]{1,0:T(8,128)(2,1)}, bf16[1024,3072]{1,0:T(8,128)(2,1)}, bf16[1024,1024]{1,0:T(8,128)(2,1)}, bf16[1024,3072]{1,0:T(8,128)(2,1)},...) custom-call(s32[4]{0:T(128)} %get-tuple-element.177.order_ref, ...), custom_call_target="tpu_custom_call", output_to_operand_aliasing={{5}: (11, {})} | custom-call | flops 19327352832 | bytes 48234496 | tf_op jit(solution)/shard_map/pallas_call | solution.py:1241
  337.7 5.3 all-to-all-start.6
  343.0 11.4 %shard_map.309 = bf16[1024,1536]{1,0:T(8,128)(2,1)} custom-call(bf16[1024,1024]{1,0:T(8,128)(2,1)} %get-tuple-element.118.refs_4_.refs_0_, bf16[1024,1024]{1,0:T(8,128)(2,1)} %get-tuple-element.119.refs_5_.refs_1_, bf16[1024,3072]{1,0:T(8,128)(2,1)} %get-tuple-element.136.refs_2_.gate_grad_ref.refs_6_, ...), custom_call_target="tpu_custom_call" | custom-call | flops 6442450944 | bytes 13631488 | tf_op jit(solution)/shard_map/pallas_call | solution.py:855
  354.4 9.9 %shard_map.308 = (bf16[4,256,512]{2,1,0:T(8,128)(2,1)}, f32[4,512,128]{2,1,0:T(8,128)}) custom-call(bf16[2,512,256]{2,1,0:T(8,128)(2,1)} %constant.113.clone.table_ref, bf16[2,512,256]{2,1,0:T(8,128)(2,1)} %constant.114.clone.inverse_ref, f32[4,512,128]{2,1,0:T(8,128)} %multiply_add_fusion.kernel_ref, bf16[4,256,512]{2,1,0:T(8,128)(2,1)} %copy-done.1, ...), custom_call_target="tpu_custom_call" | custom-call | flops 3758096384 | bytes 8388608 | tf_op jit(solution)/shard_map/pallas_call | solution.py:1206
  364.4 2.8 all-to-all-done.6.grad_ref
  368.1 3.9 all-to-all-start.5
  372.1 10.0 %shard_map.311 = (bf16[4,256,512]{2,1,0:T(8,128)(2,1)}, f32[4,512,128]{2,1,0:T(8,128)}) custom-call(bf16[2,512,256]{2,1,0:T(8,128)(2,1)} %constant.113.clone.table_ref, bf16[2,512,256]{2,1,0:T(8,128)(2,1)} %constant.114.clone.inverse_ref, f32[4,512,128]{2,1,0:T(8,128)} %multiply_add_fusion.kernel_ref, bf16[4,256,512]{2,1,0:T(8,128)(2,1)} %all-to-all-done.1.rows_ref, ...), custom_call_target="tpu_custom_call" | custom-call | flops 3758096384 | bytes 8388608 | tf_op jit(solution)/shard_map/pallas_call | solution.py:1206
  382.1 15.1 %all-to-all-done.5.back_ref = bf16[4,256,512]{2,1,0:T(8,128)(2,1)S(1)} async-done(((bf16[4,256,512]{2,1,0:T(8,128)(2,1)}), bf16[4,256,512]{2,1,0:T(8,128)(2,1)S(1)}, u32[]{:S(2)}, u32[]{:S(2)}) %all-to-all-start.5) | async-done | bytes 1048608 | tf_op jit(solution)/shard_map/all_to_all | solution.py:327
  397.2 4.3 all-to-all-start.7
  406.5 17.0 %shard_map.310 = (bf16[2,4,256,1024]{3,2,1,0:T(8,128)(2,1)}, bf16[1024,512]{1,0:T(8,128)(2,1)}, f32[2,8,1024]{2,1,0:T(8,128)}, f32[2,8,1024]{2,1,0:T(8,128)}) custom-call(bf16[4,256,512]{2,1,0:T(8,128)(2,1)} %copy-done.2, f32[1024,512]{1,0:T(8,128)} %get-tuple-element.145.slope_ref, bf16[1024,3072]{1,0:T(8,128)(2,1)} %get-tuple-element.136.refs_2_.gate_grad_ref.refs_6_, ...), custom_call_target="tpu_custom_call" | custom-call | flops 7516192768 | bytes 20971520 | tf_op jit(solution)/shard_map/pallas_call | solution.py:1299
  423.5 3.3 all-to-all-done.7.back_ref
  426.8 16.9 %shard_map.312 = (bf16[2,4,256,1024]{3,2,1,0:T(8,128)(2,1)}, bf16[1024,512]{1,0:T(8,128)(2,1)}, f32[2,8,1024]{2,1,0:T(8,128)}, f32[2,8,1024]{2,1,0:T(8,128)}) custom-call(bf16[4,256,512]{2,1,0:T(8,128)(2,1)} %all-to-all-done.7.back_ref, f32[1024,512]{1,0:T(8,128)} %get-tuple-element.150.slope_ref, ...), custom_call_target="tpu_custom_call", output_to_operand_aliasing={{0}: (8, {})} | custom-call | flops 7516192768 | bytes 20971520 | tf_op jit(solution)/shard_map/pallas_call | solution.py:1299
  447.4 94.0 %shard_map.313 = (f32[32,3072]{1,0:T(8,128)}, f32[16,3072]{1,0:T(8,128)}, f32[96,1024]{1,0:T(8,128)}, f32[32,512]{1,0:T(8,128)}, f32[8,128]{1,0:T(8,128)}) custom-call(bf16[1024,1024]{1,0:T(8,128)(2,1)} %get-tuple-element.118.refs_4_.refs_0_, bf16[1024,1024]{1,0:T(8,128)(2,1)} %get-tuple-element.119.refs_5_.refs_1_, ...), custom_call_target="tpu_custom_call" | custom-call | flops 34359738368 | bytes 104857600 | tf_op jit(solution)/shard_map/pallas_call | solution.py:819
  546.1 5.3 fusion.7
  551.4 5.1 subtract_reduce_fusion
  (129 shorter events, 36.2 us)
Async XLA Ops:
  93.3 9.7 %copy-start.22 = (s32[2,32]{1,0:T(2,128)S(1)}, s32[2,32]{1,0:T(2,128)}, u32[]{:S(2)}) copy-start(s32[2,32]{1,0:T(2,128)} %param.31) | copy-start | bytes 772
  93.3 12.0 %copy-start.23 = (s32[2,32]{1,0:T(2,128)S(1)}, s32[2,32]{1,0:T(2,128)}, u32[]{:S(2)}) copy-start(s32[2,32]{1,0:T(2,128)} %param.30) | copy-start | bytes 772
  93.3 15.2 %copy-start.25 = (f32[16]{0:T(128)S(1)}, f32[16]{0:T(128)}, u32[]{:S(2)}) copy-start(f32[16]{0:T(128)} %param.40) | copy-start | bytes 196
  93.3 15.7 %copy-start.9 = (f32[2,16,512]{2,1,0:T(8,128)S(1)}, f32[2,16,512]{2,1,0:T(8,128)}, u32[]{:S(2)}) copy-start(f32[2,16,512]{2,1,0:T(8,128)} %param.37) | copy-start | bytes 196612
  93.3 15.7 %copy-start.13 = (f32[16,512]{1,0:T(8,128)S(1)}, f32[16,512]{1,0:T(8,128)}, u32[]{:S(2)}) copy-start(f32[16,512]{1,0:T(8,128)} %param.38) | copy-start | bytes 98308
  93.3 15.7 %copy-start.15 = (f32[16,512]{1,0:T(8,128)S(1)}, f32[16,512]{1,0:T(8,128)}, u32[]{:S(2)}) copy-start(f32[16,512]{1,0:T(8,128)} %param.39) | copy-start | bytes 98308
  99.1 28.9 %all-to-all-start = ((bf16[4,256,512]{2,1,0:T(8,128)(2,1)}), bf16[4,256,512]{2,1,0:T(8,128)(2,1)S(1)}, u32[]{:S(2)}, u32[]{:S(2)}) async-start(bf16[4,256,512]{2,1,0:T(8,128)(2,1)} %get-tuple-element.106), calls=%async_computation | async-start | bytes 2097152 | tf_op jit(solution)/shard_map/all_to_all | solution.py:327
  128.0 17.3 %copy-start.1 = (bf16[4,256,512]{2,1,0:T(8,128)(2,1)}, bf16[4,256,512]{2,1,0:T(8,128)(2,1)S(1)}, u32[]{:S(2)}) copy-start(bf16[4,256,512]{2,1,0:T(8,128)(2,1)S(1)} %all-to-all-done.rows_ref) | copy-start | bytes 3145732
  128.0 29.5 %all-to-all-start.1 = ((bf16[4,256,512]{2,1,0:T(8,128)(2,1)}), bf16[4,256,512]{2,1,0:T(8,128)(2,1)}, u32[]{:S(2)}, u32[]{:S(2)}) async-start(bf16[4,256,512]{2,1,0:T(8,128)(2,1)} %get-tuple-element.114), calls=%async_computation.1 | async-start | bytes 2097152 | tf_op jit(solution)/shard_map/all_to_all | solution.py:327
  132.8 12.6 %copy-start.21 = (f32[512]{0:T(512)S(1)}, f32[512]{0:T(512)}, u32[]{:S(2)}) copy-start(f32[512]{0:T(512)} %constant.112.clone) | copy-start | bytes 6148
  157.5 107.0 %all-to-all-start.3 = ((bf16[4,256,512]{2,1,0:T(8,128)(2,1)}), bf16[4,256,512]{2,1,0:T(8,128)(2,1)}, u32[]{:S(2)}, u32[]{:S(2)}) async-start(bf16[4,256,512]{2,1,0:T(8,128)(2,1)} %shard_map.302), calls=%async_computation.3 | async-start | bytes 2097152 | tf_op jit(solution)/shard_map/all_to_all | solution.py:327
  264.6 35.8 %all-to-all-start.2 = ((bf16[4,256,512]{2,1,0:T(8,128)(2,1)}), bf16[4,256,512]{2,1,0:T(8,128)(2,1)S(1)}, u32[]{:S(2)}, u32[]{:S(2)}) async-start(bf16[4,256,512]{2,1,0:T(8,128)(2,1)} %shard_map.304), calls=%async_computation.2 | async-start | bytes 2097152 | tf_op jit(solution)/shard_map/all_to_all | solution.py:327
  300.4 5.1 copy-start.3
  300.4 37.3 %all-to-all-start.4 = ((bf16[4,256,512]{2,1,0:T(8,128)(2,1)}), bf16[4,256,512]{2,1,0:T(8,128)(2,1)S(1)}, u32[]{:S(2)}, u32[]{:S(2)}) async-start(bf16[4,256,512]{2,1,0:T(8,128)(2,1)} %get-tuple-element.142), calls=%async_computation.4 | async-start | bytes 2097152 | tf_op jit(solution)/shard_map/all_to_all | solution.py:327
  337.7 16.8 %copy-start.4 = (bf16[4,256,512]{2,1,0:T(8,128)(2,1)}, bf16[4,256,512]{2,1,0:T(8,128)(2,1)S(1)}, u32[]{:S(2)}) copy-start(bf16[4,256,512]{2,1,0:T(8,128)(2,1)S(1)} %all-to-all-done.4.grad_ref) | copy-start | bytes 3145732
  337.7 29.5 %all-to-all-start.6 = ((bf16[4,256,512]{2,1,0:T(8,128)(2,1)}), bf16[4,256,512]{2,1,0:T(8,128)(2,1)S(1)}, u32[]{:S(2)}, u32[]{:S(2)}) async-start(bf16[4,256,512]{2,1,0:T(8,128)(2,1)} %get-tuple-element.148), calls=%async_computation.6 | async-start | bytes 2097152 | tf_op jit(solution)/shard_map/all_to_all | solution.py:327
  368.1 29.1 %all-to-all-start.5 = ((bf16[4,256,512]{2,1,0:T(8,128)(2,1)}), bf16[4,256,512]{2,1,0:T(8,128)(2,1)S(1)}, u32[]{:S(2)}, u32[]{:S(2)}) async-start(bf16[4,256,512]{2,1,0:T(8,128)(2,1)} %get-tuple-element.144), calls=%async_computation.5 | async-start | bytes 2097152 | tf_op jit(solution)/shard_map/all_to_all | solution.py:327
  372.0 29.5 %copy-start.11 = (f32[4,8,1024]{2,1,0:T(8,128)S(1)}, f32[4,8,1024]{2,1,0:T(8,128)}, u32[]{:S(2)}) copy-start(f32[4,8,1024]{2,1,0:T(8,128)} %get-tuple-element.159) | copy-start | bytes 393220
  372.1 29.5 %copy-start.12 = (f32[4,8,1024]{2,1,0:T(8,128)S(1)}, f32[4,8,1024]{2,1,0:T(8,128)}, u32[]{:S(2)}) copy-start(f32[4,8,1024]{2,1,0:T(8,128)} %get-tuple-element.160) | copy-start | bytes 393220
  372.1 30.9 %copy-start = (f32[4,512,128]{2,1,0:T(8,128)S(1)}, f32[4,512,128]{2,1,0:T(8,128)}, u32[]{:S(2)}) copy-start(f32[4,512,128]{2,1,0:T(8,128)} %get-tuple-element.165) | copy-start | bytes 3145732
  397.2 7.1 %copy-start.2 = (bf16[4,256,512]{2,1,0:T(8,128)(2,1)}, bf16[4,256,512]{2,1,0:T(8,128)(2,1)S(1)}, u32[]{:S(2)}) copy-start(bf16[4,256,512]{2,1,0:T(8,128)(2,1)S(1)} %all-to-all-done.5.back_ref) | copy-start | bytes 3145732
  397.2 29.6 %all-to-all-start.7 = ((bf16[4,256,512]{2,1,0:T(8,128)(2,1)}), bf16[4,256,512]{2,1,0:T(8,128)(2,1)}, u32[]{:S(2)}, u32[]{:S(2)}) async-start(bf16[4,256,512]{2,1,0:T(8,128)(2,1)} %get-tuple-element.149), calls=%async_computation.7 | async-start | bytes 2097152 | tf_op jit(solution)/shard_map/all_to_all | solution.py:327
  401.5 143.0 %reduce-scatter.4.cloned.1.call-start = ((), (), s32[]{:S(2)}) async-start(), calls=%async_computation.9 | async-start | bytes 589824
  426.8 17.9 %copy-start.19 = (f32[2,8,1024]{2,1,0:T(8,128)S(1)}, f32[2,8,1024]{2,1,0:T(8,128)}, u32[]{:S(2)}) copy-start(f32[2,8,1024]{2,1,0:T(8,128)} %get-tuple-element.155) | copy-start | bytes 196612
  426.8 18.8 %copy-start.18 = (f32[2,8,1024]{2,1,0:T(8,128)S(1)}, f32[2,8,1024]{2,1,0:T(8,128)}, u32[]{:S(2)}) copy-start(f32[2,8,1024]{2,1,0:T(8,128)} %get-tuple-element.157) | copy-start | bytes 196612
  551.4 5.8 %copy-start.14 = (f32[16,512]{1,0:T(8,128)S(1)}, f32[16,512]{1,0:T(8,128)}, u32[]{:S(2)}) copy-start(f32[16,512]{1,0:T(8,128)} %param.38) | copy-start | bytes 98308
  551.4 5.8 %copy-start.16 = (f32[16,512]{1,0:T(8,128)S(1)}, f32[16,512]{1,0:T(8,128)}, u32[]{:S(2)}) copy-start(f32[16,512]{1,0:T(8,128)} %param.39) | copy-start | bytes 98308
  551.4 5.8 %copy-start.24 = (f32[16]{0:T(128)S(1)}, f32[16]{0:T(128)}, u32[]{:S(2)}) copy-start(f32[16]{0:T(128)} %get-tuple-element.197) | copy-start | bytes 196
  551.4 7.1 %copy-start.8 = (f32[32,3072]{1,0:T(8,128)S(1)}, f32[32,3072]{1,0:T(8,128)}, u32[]{:S(2)}) copy-start(f32[32,3072]{1,0:T(8,128)} %get-tuple-element.221) | copy-start | bytes 1179652
  551.4 7.8 %copy-start.17 = (f32[32,512]{1,0:T(8,128)S(1)}, f32[32,512]{1,0:T(8,128)}, u32[]{:S(2)}) copy-start(f32[32,512]{1,0:T(8,128)} %get-tuple-element.222) | copy-start | bytes 196612
  551.4 8.5 %copy-start.10 = (f32[16,3072]{1,0:T(8,128)S(1)}, f32[16,3072]{1,0:T(8,128)}, u32[]{:S(2)}) copy-start(f32[16,3072]{1,0:T(8,128)} %get-tuple-element.227) | copy-start | bytes 589828
  551.4 9.1 %copy-start.7 = (f32[96,1024]{1,0:T(8,128)S(1)}, f32[96,1024]{1,0:T(8,128)}, u32[]{:S(2)}) copy-start(f32[96,1024]{1,0:T(8,128)} %get-tuple-element.228) | copy-start | bytes 1179652
  (3 other events, 4.4 us)
Sparse Core Ops, SparseCore 0:
  444.8 36.3 reduce-scatter.3

commit v5 on v4

--- a/solution.py
+++ b/solution.py
@@ -9,7 +9,7 @@
 from jax.sharding import PartitionSpec as P
 
 epsilon = 1e-05
-highest = lax.Precision.HIGHEST
+high = lax.Precision.HIGH
 bf16 = jnp.bfloat16
 f32 = jnp.float32
 MESH = pl.DeviceIdType.MESH
@@ -1008,7 +1008,7 @@
     right = jnp.concatenate(
         [w_re * near_re - w_im * near_im, w_re * near_im + w_im * near_re], axis=2
     )
-    rows = jnp.einsum("han,hbn->hab", left, right, precision=highest)
+    rows = jnp.einsum("han,hbn->hab", left, right, precision=high)
     return rows.reshape(rows.shape[0], -1)
 
 
@@ -1021,7 +1021,7 @@
     far_index = (jnp.arange(coarse, dtype=jnp.int32) * fine).astype(f32)[None, :, None]
     stacked = jnp.concatenate([tiles, tiles * near_index], axis=1)
     part = jnp.einsum(
-        "hab,hbn->han", stacked, jnp.concatenate([near_re, near_im], axis=2), precision=highest
+        "hab,hbn->han", stacked, jnp.concatenate([near_re, near_im], axis=2), precision=high
     )
     u_re, u_im = part[:, :coarse, :states], part[:, :coarse, states:]
     v_re = part[:, coarse:, :states] + far_index * u_re
@@ -1074,7 +1074,7 @@
     micros = range(micro_count)
     direct = own % 128 == 0
 
-    small = jnp.zeros((16, 256), bf16).at[0, :share].set(norm_gain).at[1, :share].set(norm_bias)
+    small = jnp.pad(jnp.stack([norm_gain, norm_bias]), ((0, 14), (0, 256 - share)))
     mask_rows = loss_mask.reshape(micro_count, dp_count, chunk).transpose(1, 0, 2)
     mask_rows = jnp.pad(mask_rows, ((0, 0), (0, 8 - micro_count), (0, 0)))
     teacher_rows = teacher.reshape(micro_count, dp_count, chunk, width)
@@ -1181,7 +1181,7 @@
     table2, inverse2 = jnp.asarray(high_and_low(table_np)), jnp.asarray(high_and_low(inverse_np))
     kernel = lax.all_gather(own_kernel, "fsdp", axis=0, tiled=True)
     segments = jnp.einsum(
-        "kt,hct->ckh", jnp.asarray(table_np), kernel.reshape(own, dp_count, chunk), precision=highest
+        "kt,hct->ckh", jnp.asarray(table_np), kernel.reshape(own, dp_count, chunk), precision=high
     )
     previous = jnp.concatenate([jnp.zeros_like(segments[:1]), segments[:-1]], axis=0)
     kernel_spec = jnp.tile(segments + sign * previous, (1, 1, lanes // own))
@@ -1297,27 +1297,27 @@
     def input_rows(m, back, gate_grad, full_grad, *earlier):
         eight = pl.BlockSpec((1, 8, width), lambda i, *_: (i, 0, 0))
         return pl.pallas_call(
-            functools.partial(input_body, dims(per_block)),
-            grid=(steps,),
+            functools.partial(input_body, dims(middle_block)),
+            grid=(middle_steps,),
             in_specs=[
-                lane_spec(per_block),
-                row_spec(reduced_width),
-                row_spec(gate_width),
+                lane_spec(middle_block),
+                row_spec(reduced_width, middle_block),
+                row_spec(gate_width, middle_block),
                 shared((width, gate_width), (0, 0)),
                 shared((width, reduced_width), (0, 0)),
-                tokens_spec(m, per_block),
+                tokens_spec(m, middle_block),
                 whole((1, width)),
-                row_spec(width),
+                row_spec(width, middle_block),
                 *[ANY] * len(earlier),
             ],
-            out_specs=[tokens_spec(m, per_block), row_spec(reduced_width), eight, eight],
+            out_specs=[tokens_spec(m, middle_block), row_spec(reduced_width, middle_block), eight, eight],
             out_shape=[
                 jax.ShapeDtypeStruct(tokens.shape, bf16),
                 jax.ShapeDtypeStruct((rows, reduced_width), bf16),
-                jax.ShapeDtypeStruct((steps, 8, width), f32),
-                jax.ShapeDtypeStruct((steps, 8, width), f32),
+                jax.ShapeDtypeStruct((middle_steps, 8, width), f32),
+                jax.ShapeDtypeStruct((middle_steps, 8, width), f32),
             ],
-            scratch_shapes=[pltpu.VMEM((per_block * chunk, reduced_width), bf16)],
+            scratch_shapes=[pltpu.VMEM((middle_block * chunk, reduced_width), bf16)],
             input_output_aliases={8: 0} if earlier else {},
             compiler_params=params(),
             cost_estimate=pl.CostEstimate(
@@ -1348,7 +1348,7 @@
         kernel_total = kernel_total.reshape(dp_count, 2 * chunk, lanes // own, own).sum(axis=2)
     following = jnp.concatenate([kernel_total[1:], jnp.zeros_like(kernel_total[:1])], axis=0)
     kernel_grad = jnp.einsum(
-        "kt,ckh->hct", jnp.asarray(inverse_np), kernel_total + sign * following, precision=highest
+        "kt,ckh->hct", jnp.asarray(inverse_np), kernel_total + sign * following, precision=high
     ).reshape(own, seq_length)
     kernel_grad, _ = lax.optimization_barrier((kernel_grad, reduced_grad))
     kernel_grad = lax.psum_scatter(kernel_grad, "fsdp", scatter_dimension=0, tiled=True)

time: 574 us -> 579 us (level)
  blocking collectives: 10.2 us -> 21.8 us
    all_gather x1, blocking collectives: 10.2 us -> 21.8 us  [shards(): kernel = lax.all_gather(own_kernel, 'fsdp', axis=0, tiled=True)]
  transfers between devices with their start and end apart: 9 -> 9, of which waited for: 5 -> 4; matrix products, arithmetic and copies ran while one was open for 6% -> 6% of each run, Pallas kernels for 56% -> 56%
where the time goes in v5:
time: 579 us; the launch traced here: 575 us
  Pallas kernels  422 us (73%)
  starting transfers between devices  34.9 us (6%)
  other arithmetic  27.1 us (5%)
  waiting for transfers between devices  24.3 us (4%)
  blocking collectives  21.8 us (4%)
  local copies, waits for them, and re-layouts  19.9 us (3%)
  between operations  17.2 us (3%)
  matrix products  7.4 us (1%)
    pallas_call x2, Pallas kernels, gather_all(): pl.pallas_call(functools.partial(gather_body, dp_count, bits, n, leads, (...  174 us
    pallas_call x1, Pallas kernels, product_scatter(): pl.pallas_call(functools.partial(product_scatter_body, dp_count, bits, pl...  94.6 us
    pallas_call x2, Pallas kernels, middle_rows(): pl.pallas_call(functools.partial(middle_body, dims(middle_block), middle_...  64.5 us
    all_to_all x8, starting transfers between devices, exchange(): return lax.all_to_all(values, 'dp', split_axis=0, concat_axis=0, tiled=True)  34.8 us
    pallas_call x2, Pallas kernels, input_rows(): pl.pallas_call(functools.partial(input_body, dims(middle_block)), grid=(m...  32.2 us
    all_to_all x8, waiting for transfers between devices, exchange(): return lax.all_to_all(values, 'dp', split_axis=0, concat_axis=0, tiled=True)  24.2 us
    all_gather x1, blocking collectives, shards(): kernel = lax.all_gather(own_kernel, 'fsdp', axis=0, tiled=True)  21.8 us
    pallas_call x2, Pallas kernels, convolve_back(): pl.pallas_call(convolve_back_body, out_shape=[jax.ShapeDtypeStruct(blocks...  19.9 us
  transfers between devices with their start and end apart: 9, of which 4 were waited for; matrix products, arithmetic and copies ran while one was open for 6% of the time, Pallas kernels for 56%

profile of v5, /device:TPU:0, one launch (start us, length us, event | category | flops | bytes accessed | tf_op | source)
XLA Modules:
  0.0 574.8 jit_solution(3430224733305337827)
XLA Ops:
  9.8 80.3 %shard_map.300 = (bf16[4,8,32,3072]{3,2,1,0:T(8,128)(2,1)}, bf16[4,8,32,512]{3,2,1,0:T(8,128)(2,1)}, bf16[4,8,16,256]{3,2,1,0:T(8,128)(2,1)}, s32[4,8,256]{2,1,0:T(8,128)}, bf16[4,256,1024]{2,1,0:T(8,128)(2,1)}) custom-call(bf16[32,3072]{1,0:T(8,128)(2,1)} %refs_0_.1, bf16[32,512]{1,0:T(8,128)(2,1)} %refs_1_.1, bf16[16,256]{1,0:T(8,128)(2,1)} %fusion.28.refs_2_, ...), custom_call_target="tpu_custom_call" | custom-call | bytes 152043520 | tf_op jit(solution)/shard_map/pallas_call | solution.py:164
  92.6 5.8 %shard_map.301 = (bf16[1024,1024]{1,0:T(8,128)(2,1)}, bf16[4,256,512]{2,1,0:T(8,128)(2,1)}, f32[1024,512]{1,0:T(8,128)}) custom-call(bf16[2,4,256,1024]{3,2,1,0:T(8,128)(2,1)} %tokens_ref.11, f32[1,1024]{1,0:T(1,128)} %reshape.185.gain_ref, f32[1,1024]{1,0:T(1,128)} %reshape.186.bias_ref, bf16[1024,512]{1,0:T(8,128)(2,1)} %bitcast.76), custom_call_target="tpu_custom_call" | custom-call | flops 1073741824 | bytes 8388608 | tf_op jit(solution)/shard_map/pallas_call | solution.py:1132
  98.4 3.6 all-to-all-start
  108.1 8.8 %multiply_subtract_fusion = (f32[16,32,512]{2,1,0:T(8,128)S(1)}, f32[16,32,512]{2,1,0:T(8,128)S(1)}, f32[16,32,512]{2,1,0:T(8,128)S(1)}, f32[16,32,512]{2,1,0:T(...) fusion(f32[16,512]{1,0:T(8,128)S(1)} %get-tuple-element.168, f32[16,512]{1,0:T(8,128)S(1)} %get-tuple-element.167, ...), kind=kLoop, calls=%fused_computation.35 | loop fusion | flops 3932160 | bytes 6422784 | tf_op jit(solution)/shard_map/sub | solution.py:1009
  120.1 5.7 shard_map.303
  127.1 4.2 all-to-all-start.1
  131.3 21.8 %all_gather.3 = f32[128,1024]{1,0:T(8,128)S(1)} all-gather(f32[16,1024]{1,0:T(8,128)S(1)} %reshape.173), channel_id=1, replica_groups=mesh['dp'=4,'fsdp'=8] {'fsdp'}, dimensions={0}, use_global_device_ids=true | all-gather | bytes 589824 | tf_op jit(solution)/shard_map/all_gather | solution.py:1182
  153.3 1.6 convolution_bitcast_fusion
  156.2 7.3 %shard_map.302 = bf16[4,256,512]{2,1,0:T(8,128)(2,1)} custom-call(bf16[2,512,256]{2,1,0:T(8,128)(2,1)} %constant.60.clone.table_ref, bf16[2,512,256]{2,1,0:T(8,128)(2,1)} %constant.61.clone.inverse_ref, f32[4,512,128]{2,1,0:T(8,128)} %multiply_add_fusion.kernel_ref, bf16[4,256,512]{2,1,0:T(8,128)(2,1)} %copy-done.1), custom_call_target="tpu_custom_call" | custom-call | flops 2684354560 | bytes 8388608 | tf_op jit(solution)/shard_map/pallas_call | solution.py:1195
  163.5 5.2 all-to-all-start.3
  169.3 7.2 %shard_map.304 = bf16[4,256,512]{2,1,0:T(8,128)(2,1)} custom-call(bf16[2,512,256]{2,1,0:T(8,128)(2,1)} %constant.60.clone.table_ref, bf16[2,512,256]{2,1,0:T(8,128)(2,1)} %constant.61.clone.inverse_ref, f32[4,512,128]{2,1,0:T(8,128)} %multiply_add_fusion.kernel_ref, bf16[4,256,512]{2,1,0:T(8,128)(2,1)} %all-to-all-done.1.rows_ref), custom_call_target="tpu_custom_call" | custom-call | flops 2684354560 | bytes 8388608 | tf_op jit(solution)/shard_map/pallas_call | solution.py:1195
  176.6 93.3 %shard_map.305 = (bf16[4,8,16,3072]{3,2,1,0:T(8,128)(2,1)}, bf16[4,8,96,1024]{3,2,1,0:T(8,128)(2,1)}, f32[4,8,8,256]{3,2,1,0:T(8,128)}, bf16[4,256,1024]{2,1,0:T...) custom-call(bf16[16,3072]{1,0:T(8,128)(2,1)} %refs_0_.2, bf16[96,1024]{1,0:T(8,128)(2,1)} %refs_1_.2, ...), custom_call_target="tpu_custom_call" | custom-call | bytes 193986560 | tf_op jit(solution)/shard_map/pallas_call | solution.py:164
  269.9 1.5 slice_reduce_fusion
  272.1 3.5 all-to-all-start.2
  275.7 32.2 %shard_map.306 = (bf16[1024,512]{1,0:T(8,128)(2,1)}, bf16[1024,3072]{1,0:T(8,128)(2,1)}, bf16[1024,1024]{1,0:T(8,128)(2,1)}, bf16[1024,3072]{1,0:T(8,128)(2,1)},...) custom-call(s32[4]{0:T(128)} %get-tuple-element.152.order_ref, ...), custom_call_target="tpu_custom_call" | custom-call | flops 19327352832 | bytes 48234496 | tf_op jit(solution)/shard_map/pallas_call | solution.py:1241
  307.9 5.0 all-to-all-start.4
  313.0 32.2 %shard_map.307 = (bf16[1024,512]{1,0:T(8,128)(2,1)}, bf16[1024,3072]{1,0:T(8,128)(2,1)}, bf16[1024,1024]{1,0:T(8,128)(2,1)}, bf16[1024,3072]{1,0:T(8,128)(2,1)},...) custom-call(s32[4]{0:T(128)} %get-tuple-element.153.order_ref, ...), custom_call_target="tpu_custom_call", output_to_operand_aliasing={{5}: (11, {})} | custom-call | flops 19327352832 | bytes 48234496 | tf_op jit(solution)/shard_map/pallas_call | solution.py:1241
  345.2 5.3 all-to-all-start.6
  350.5 11.4 %shard_map.309 = bf16[1024,1536]{1,0:T(8,128)(2,1)} custom-call(bf16[1024,1024]{1,0:T(8,128)(2,1)} %get-tuple-element.94.refs_4_.refs_0_, bf16[1024,1024]{1,0:T(8,128)(2,1)} %get-tuple-element.95.refs_5_.refs_1_, bf16[1024,3072]{1,0:T(8,128)(2,1)} %get-tuple-element.112.refs_2_.gate_grad_ref.refs_6_, ...), custom_call_target="tpu_custom_call" | custom-call | flops 6442450944 | bytes 13631488 | tf_op jit(solution)/shard_map/pallas_call | solution.py:855
  361.9 9.9 %shard_map.308 = (bf16[4,256,512]{2,1,0:T(8,128)(2,1)}, f32[4,512,128]{2,1,0:T(8,128)}) custom-call(bf16[2,512,256]{2,1,0:T(8,128)(2,1)} %constant.60.clone.table_ref, bf16[2,512,256]{2,1,0:T(8,128)(2,1)} %constant.61.clone.inverse_ref, f32[4,512,128]{2,1,0:T(8,128)} %multiply_add_fusion.kernel_ref, bf16[4,256,512]{2,1,0:T(8,128)(2,1)} %copy-done.1, ...), custom_call_target="tpu_custom_call" | custom-call | flops 3758096384 | bytes 8388608 | tf_op jit(solution)/shard_map/pallas_call | solution.py:1206
  371.8 3.0 all-to-all-done.6.grad_ref
  375.8 3.7 all-to-all-start.5
  379.5 10.0 %shard_map.311 = (bf16[4,256,512]{2,1,0:T(8,128)(2,1)}, f32[4,512,128]{2,1,0:T(8,128)}) custom-call(bf16[2,512,256]{2,1,0:T(8,128)(2,1)} %constant.60.clone.table_ref, bf16[2,512,256]{2,1,0:T(8,128)(2,1)} %constant.61.clone.inverse_ref, f32[4,512,128]{2,1,0:T(8,128)} %multiply_add_fusion.kernel_ref, bf16[4,256,512]{2,1,0:T(8,128)(2,1)} %all-to-all-done.1.rows_ref, ...), custom_call_target="tpu_custom_call" | custom-call | flops 3758096384 | bytes 8388608 | tf_op jit(solution)/shard_map/pallas_call | solution.py:1206
  389.5 15.1 %all-to-all-done.5.back_ref = bf16[4,256,512]{2,1,0:T(8,128)(2,1)S(1)} async-done(((bf16[4,256,512]{2,1,0:T(8,128)(2,1)}), bf16[4,256,512]{2,1,0:T(8,128)(2,1)S(1)}, u32[]{:S(2)}, u32[]{:S(2)}) %all-to-all-start.5) | async-done | bytes 1048608 | tf_op jit(solution)/shard_map/all_to_all | solution.py:327
  404.7 4.3 all-to-all-start.7
  410.4 1.3 add.85
  413.1 16.3 %shard_map.310 = (bf16[2,4,256,1024]{3,2,1,0:T(8,128)(2,1)}, bf16[1024,512]{1,0:T(8,128)(2,1)}, f32[4,8,1024]{2,1,0:T(8,128)}, f32[4,8,1024]{2,1,0:T(8,128)}) custom-call(bf16[4,256,512]{2,1,0:T(8,128)(2,1)} %copy-done.2, f32[1024,512]{1,0:T(8,128)} %get-tuple-element.121.slope_ref, bf16[1024,3072]{1,0:T(8,128)(2,1)} %get-tuple-element.112.refs_2_.gate_grad_ref.refs_6_, ...), custom_call_target="tpu_custom_call" | custom-call | flops 7516192768 | bytes 20971520 | tf_op jit(solution)/shard_map/pallas_call | solution.py:1299
  429.3 4.9 all-to-all-done.7.back_ref
  434.2 15.9 %shard_map.312 = (bf16[2,4,256,1024]{3,2,1,0:T(8,128)(2,1)}, bf16[1024,512]{1,0:T(8,128)(2,1)}, f32[4,8,1024]{2,1,0:T(8,128)}, f32[4,8,1024]{2,1,0:T(8,128)}) custom-call(bf16[4,256,512]{2,1,0:T(8,128)(2,1)} %all-to-all-done.7.back_ref, f32[1024,512]{1,0:T(8,128)} %get-tuple-element.126.slope_ref, ...), custom_call_target="tpu_custom_call", output_to_operand_aliasing={{0}: (8, {})} | custom-call | flops 7516192768 | bytes 20971520 | tf_op jit(solution)/shard_map/pallas_call | solution.py:1299
  453.9 94.6 %shard_map.313 = (f32[32,3072]{1,0:T(8,128)}, f32[16,3072]{1,0:T(8,128)}, f32[96,1024]{1,0:T(8,128)}, f32[32,512]{1,0:T(8,128)}, f32[8,128]{1,0:T(8,128)}) custom-call(bf16[1024,1024]{1,0:T(8,128)(2,1)} %get-tuple-element.94.refs_4_.refs_0_, bf16[1024,1024]{1,0:T(8,128)(2,1)} %get-tuple-element.95.refs_5_.refs_1_, ...), custom_call_target="tpu_custom_call" | custom-call | flops 34359738368 | bytes 104857600 | tf_op jit(solution)/shard_map/pallas_call | solution.py:819
  553.2 3.5 fusion.7
  556.8 5.1 subtract_reduce_fusion
  (126 shorter events, 33.9 us)
Async XLA Ops:
  92.5 9.5 %copy-start.21 = (s32[2,32]{1,0:T(2,128)S(1)}, s32[2,32]{1,0:T(2,128)}, u32[]{:S(2)}) copy-start(s32[2,32]{1,0:T(2,128)} %param.27) | copy-start | bytes 772
  92.5 11.8 %copy-start.22 = (s32[2,32]{1,0:T(2,128)S(1)}, s32[2,32]{1,0:T(2,128)}, u32[]{:S(2)}) copy-start(s32[2,32]{1,0:T(2,128)} %param.26) | copy-start | bytes 772
  92.5 15.0 %copy-start.24 = (f32[16]{0:T(128)S(1)}, f32[16]{0:T(128)}, u32[]{:S(2)}) copy-start(f32[16]{0:T(128)} %param.36) | copy-start | bytes 196
  92.5 15.5 %copy-start.9 = (f32[2,16,512]{2,1,0:T(8,128)S(1)}, f32[2,16,512]{2,1,0:T(8,128)}, u32[]{:S(2)}) copy-start(f32[2,16,512]{2,1,0:T(8,128)} %param.33) | copy-start | bytes 196612
  92.5 15.5 %copy-start.15 = (f32[16,512]{1,0:T(8,128)S(1)}, f32[16,512]{1,0:T(8,128)}, u32[]{:S(2)}) copy-start(f32[16,512]{1,0:T(8,128)} %param.34) | copy-start | bytes 98308
  92.5 15.5 %copy-start.17 = (f32[16,512]{1,0:T(8,128)S(1)}, f32[16,512]{1,0:T(8,128)}, u32[]{:S(2)}) copy-start(f32[16,512]{1,0:T(8,128)} %param.35) | copy-start | bytes 98308
  98.4 28.7 %all-to-all-start = ((bf16[4,256,512]{2,1,0:T(8,128)(2,1)}), bf16[4,256,512]{2,1,0:T(8,128)(2,1)S(1)}, u32[]{:S(2)}, u32[]{:S(2)}) async-start(bf16[4,256,512]{2,1,0:T(8,128)(2,1)} %get-tuple-element.82), calls=%async_computation | async-start | bytes 2097152 | tf_op jit(solution)/shard_map/all_to_all | solution.py:327
  127.1 28.0 %copy-start.1 = (bf16[4,256,512]{2,1,0:T(8,128)(2,1)}, bf16[4,256,512]{2,1,0:T(8,128)(2,1)S(1)}, u32[]{:S(2)}) copy-start(bf16[4,256,512]{2,1,0:T(8,128)(2,1)S(1)} %all-to-all-done.rows_ref) | copy-start | bytes 3145732
  127.1 36.4 %all-to-all-start.1 = ((bf16[4,256,512]{2,1,0:T(8,128)(2,1)}), bf16[4,256,512]{2,1,0:T(8,128)(2,1)}, u32[]{:S(2)}, u32[]{:S(2)}) async-start(bf16[4,256,512]{2,1,0:T(8,128)(2,1)} %get-tuple-element.90), calls=%async_computation.1 | async-start | bytes 2097152 | tf_op jit(solution)/shard_map/all_to_all | solution.py:327
  131.3 23.7 %copy-start.20 = (f32[512]{0:T(512)S(1)}, f32[512]{0:T(512)}, u32[]{:S(2)}) copy-start(f32[512]{0:T(512)} %constant.59.clone) | copy-start | bytes 6148
  163.5 108.6 %all-to-all-start.3 = ((bf16[4,256,512]{2,1,0:T(8,128)(2,1)}), bf16[4,256,512]{2,1,0:T(8,128)(2,1)}, u32[]{:S(2)}, u32[]{:S(2)}) async-start(bf16[4,256,512]{2,1,0:T(8,128)(2,1)} %shard_map.302), calls=%async_computation.3 | async-start | bytes 2097152 | tf_op jit(solution)/shard_map/all_to_all | solution.py:327
  272.1 35.8 %all-to-all-start.2 = ((bf16[4,256,512]{2,1,0:T(8,128)(2,1)}), bf16[4,256,512]{2,1,0:T(8,128)(2,1)S(1)}, u32[]{:S(2)}, u32[]{:S(2)}) async-start(bf16[4,256,512]{2,1,0:T(8,128)(2,1)} %shard_map.304), calls=%async_computation.2 | async-start | bytes 2097152 | tf_op jit(solution)/shard_map/all_to_all | solution.py:327
  307.9 5.1 copy-start.3
  307.9 37.3 %all-to-all-start.4 = ((bf16[4,256,512]{2,1,0:T(8,128)(2,1)}), bf16[4,256,512]{2,1,0:T(8,128)(2,1)S(1)}, u32[]{:S(2)}, u32[]{:S(2)}) async-start(bf16[4,256,512]{2,1,0:T(8,128)(2,1)} %get-tuple-element.118), calls=%async_computation.4 | async-start | bytes 2097152 | tf_op jit(solution)/shard_map/all_to_all | solution.py:327
  345.2 16.7 %copy-start.4 = (bf16[4,256,512]{2,1,0:T(8,128)(2,1)}, bf16[4,256,512]{2,1,0:T(8,128)(2,1)S(1)}, u32[]{:S(2)}) copy-start(bf16[4,256,512]{2,1,0:T(8,128)(2,1)S(1)} %all-to-all-done.4.grad_ref) | copy-start | bytes 3145732
  345.2 29.6 %all-to-all-start.6 = ((bf16[4,256,512]{2,1,0:T(8,128)(2,1)}), bf16[4,256,512]{2,1,0:T(8,128)(2,1)S(1)}, u32[]{:S(2)}, u32[]{:S(2)}) async-start(bf16[4,256,512]{2,1,0:T(8,128)(2,1)} %get-tuple-element.124), calls=%async_computation.6 | async-start | bytes 2097152 | tf_op jit(solution)/shard_map/all_to_all | solution.py:327
  375.8 28.9 %all-to-all-start.5 = ((bf16[4,256,512]{2,1,0:T(8,128)(2,1)}), bf16[4,256,512]{2,1,0:T(8,128)(2,1)S(1)}, u32[]{:S(2)}, u32[]{:S(2)}) async-start(bf16[4,256,512]{2,1,0:T(8,128)(2,1)} %get-tuple-element.120), calls=%async_computation.5 | async-start | bytes 2097152 | tf_op jit(solution)/shard_map/all_to_all | solution.py:327
  379.5 29.5 %copy-start.11 = (f32[4,8,1024]{2,1,0:T(8,128)S(1)}, f32[4,8,1024]{2,1,0:T(8,128)}, u32[]{:S(2)}) copy-start(f32[4,8,1024]{2,1,0:T(8,128)} %get-tuple-element.135) | copy-start | bytes 393220
  379.5 29.5 %copy-start.12 = (f32[4,8,1024]{2,1,0:T(8,128)S(1)}, f32[4,8,1024]{2,1,0:T(8,128)}, u32[]{:S(2)}) copy-start(f32[4,8,1024]{2,1,0:T(8,128)} %get-tuple-element.136) | copy-start | bytes 393220
  379.5 30.9 %copy-start = (f32[4,512,128]{2,1,0:T(8,128)S(1)}, f32[4,512,128]{2,1,0:T(8,128)}, u32[]{:S(2)}) copy-start(f32[4,512,128]{2,1,0:T(8,128)} %get-tuple-element.141) | copy-start | bytes 3145732
  404.7 7.1 %copy-start.2 = (bf16[4,256,512]{2,1,0:T(8,128)(2,1)}, bf16[4,256,512]{2,1,0:T(8,128)(2,1)S(1)}, u32[]{:S(2)}) copy-start(bf16[4,256,512]{2,1,0:T(8,128)(2,1)S(1)} %all-to-all-done.5.back_ref) | copy-start | bytes 3145732
  404.7 29.5 %all-to-all-start.7 = ((bf16[4,256,512]{2,1,0:T(8,128)(2,1)}), bf16[4,256,512]{2,1,0:T(8,128)(2,1)}, u32[]{:S(2)}, u32[]{:S(2)}) async-start(bf16[4,256,512]{2,1,0:T(8,128)(2,1)} %get-tuple-element.125), calls=%async_computation.7 | async-start | bytes 2097152 | tf_op jit(solution)/shard_map/all_to_all | solution.py:327
  408.9 142.7 %reduce-scatter.4.cloned.1.call-start = ((), (), s32[]{:S(2)}) async-start(), calls=%async_computation.9 | async-start | bytes 589824
  434.2 16.9 %copy-start.14 = (f32[4,8,1024]{2,1,0:T(8,128)S(1)}, f32[4,8,1024]{2,1,0:T(8,128)}, u32[]{:S(2)}) copy-start(f32[4,8,1024]{2,1,0:T(8,128)} %get-tuple-element.131) | copy-start | bytes 393220
  434.2 17.9 %copy-start.13 = (f32[4,8,1024]{2,1,0:T(8,128)S(1)}, f32[4,8,1024]{2,1,0:T(8,128)}, u32[]{:S(2)}) copy-start(f32[4,8,1024]{2,1,0:T(8,128)} %get-tuple-element.133) | copy-start | bytes 393220
  556.7 5.8 %copy-start.16 = (f32[16,512]{1,0:T(8,128)S(1)}, f32[16,512]{1,0:T(8,128)}, u32[]{:S(2)}) copy-start(f32[16,512]{1,0:T(8,128)} %param.34) | copy-start | bytes 98308
  556.7 5.8 %copy-start.18 = (f32[16,512]{1,0:T(8,128)S(1)}, f32[16,512]{1,0:T(8,128)}, u32[]{:S(2)}) copy-start(f32[16,512]{1,0:T(8,128)} %param.35) | copy-start | bytes 98308
  556.7 5.8 %copy-start.23 = (f32[16]{0:T(128)S(1)}, f32[16]{0:T(128)}, u32[]{:S(2)}) copy-start(f32[16]{0:T(128)} %get-tuple-element.173) | copy-start | bytes 196
  556.8 7.1 %copy-start.8 = (f32[32,3072]{1,0:T(8,128)S(1)}, f32[32,3072]{1,0:T(8,128)}, u32[]{:S(2)}) copy-start(f32[32,3072]{1,0:T(8,128)} %get-tuple-element.197) | copy-start | bytes 1179652
  556.8 7.8 %copy-start.19 = (f32[32,512]{1,0:T(8,128)S(1)}, f32[32,512]{1,0:T(8,128)}, u32[]{:S(2)}) copy-start(f32[32,512]{1,0:T(8,128)} %get-tuple-element.198) | copy-start | bytes 196612
  556.8 8.5 %copy-start.10 = (f32[16,3072]{1,0:T(8,128)S(1)}, f32[16,3072]{1,0:T(8,128)}, u32[]{:S(2)}) copy-start(f32[16,3072]{1,0:T(8,128)} %get-tuple-element.203) | copy-start | bytes 589828
  556.8 9.1 %copy-start.7 = (f32[96,1024]{1,0:T(8,128)S(1)}, f32[96,1024]{1,0:T(8,128)}, u32[]{:S(2)}) copy-start(f32[96,1024]{1,0:T(8,128)} %get-tuple-element.204) | copy-start | bytes 1179652
  (2 other events, 3.8 us)
Sparse Core Ops, SparseCore 0:
  451.2 36.2 reduce-scatter.3

commit v6 on v5

--- a/solution.py
+++ b/solution.py
@@ -42,7 +42,11 @@
     return order
 
 
-def gather_body(dp_count, bits, n, leads, work, *refs):
+def far_first(count):
+    return sorted(range(count), key=lambda o: (o > 0, -min(o, count - o)))
+
+
+def gather_body(dp_count, bits, n, leads, order, work, *refs):
     n_swap = len(leads)
     n_work_in, n_work_out = work[0] if work else (0, 0)
     moved = n + n_swap
@@ -59,7 +63,6 @@
     for x in ins[:n]:
         cut = x.shape[1] // 256 * 128
         cuts.append(((0, cut), (cut, x.shape[1] - cut)))
-    order = near_first(dp_count)
     if work:
         begin()
     greet(dp_count, bits)
@@ -159,10 +162,13 @@
     dp_count, fsdp_count = lax.axis_size("dp"), lax.axis_size("fsdp")
     bits = fsdp_count.bit_length() - 1
     n, n_swap = len(arrays), len(swaps)
+    order = near_first(dp_count) if work else far_first(dp_count)
     slots = 2 * dp_count * (fsdp_count - 1) * n
     total = dp_count * fsdp_count * sum(x.size * x.dtype.itemsize for x in arrays)
     return pl.pallas_call(
-        functools.partial(gather_body, dp_count, bits, n, leads, (sizes, work_body) if work else None),
+        functools.partial(
+            gather_body, dp_count, bits, n, leads, order, (sizes, work_body) if work else None
+        ),
         out_shape=[
             jax.ShapeDtypeStruct((dp_count, fsdp_count, *x.shape), x.dtype) for x in arrays
         ]
@@ -533,7 +539,9 @@
     n = len(pieces)
     lefts, refs = refs[: n_left * micros], refs[n_left * micros :]
     rights, refs = refs[: n_right * micros], refs[n_right * micros :]
-    ready_ref, small_ref, refs = refs[0], refs[1], refs[2:]
+    parts = plan["parts"]
+    ready_refs, small_ref, refs = refs[:parts], refs[parts], refs[parts + 1 :]
+    part_width = ready_refs[0].shape[-1]
     outs, refs = refs[: plan["outputs"]], refs[plan["outputs"] :]
     left_bufs, refs = refs[:n_left], refs[n_left:]
     right_buf, left_sem, right_sem, load_sem, ready_sem, send, recv, store_sem = refs[:8]
@@ -613,7 +621,9 @@
         ready_loads.append(
             [
                 pltpu.make_async_copy(
-                    ready_ref.at[(*lead, slice(None), pl.ds(piece_jobs[0][2] + g * lane, lane))],
+                    ready_refs[piece_jobs[0][2] // part_width].at[
+                        (*lead, slice(None), pl.ds(piece_jobs[0][2] % part_width + g * lane, lane))
+                    ],
                     bufs[i][0].at[(*lead, pl.ds(g * rows, rows), slice(None))],
                     ready_sem.at[i, g],
                 )
@@ -787,7 +797,8 @@
         "lane": lane,
         "outputs": len(lefts) + 1,
         "micros": len(lefts[0]),
-        "ready": sum(1 for k, _, _, jobs in pieces[:-1] if k == 0 and jobs[-1][2] + jobs[-1][3] <= ready.shape[1]),
+        "ready": sum(1 for k, _, _, jobs in pieces[:-1] if k == 0 and jobs[-1][2] + jobs[-1][3] <= sum(x.shape[1] for x in ready)),
+        "parts": len(ready),
     }
 
     def buffer_set(count, lead, rows, columns, dtype):
@@ -813,14 +824,14 @@
     micro_count, rows = len(lefts[0]), lefts[0][0].shape[0]
     steps = bits - 1 + dp_count
     small = small.reshape(dp_count, *(2,) * bits, *small.shape[1:])
-    ready = ready.reshape(dp_count, *(2,) * bits, -1, ready.shape[1])
+    ready = [x.reshape(dp_count, *(2,) * bits, -1, x.shape[1]) for x in ready]
     widths = [(a[0].shape[1], b[0].shape[1]) for a, b in zip(lefts, rights)]
     flops = sum(2 * micro_count * rows * a * b for a, b in widths)
     return pl.pallas_call(
         functools.partial(product_scatter_body, dp_count, bits, plan, len(unique), len(rights)),
         out_shape=[jax.ShapeDtypeStruct((a // devices, b), f32) for a, b in widths]
         + [jax.ShapeDtypeStruct(small.shape[-2:], f32)],
-        in_specs=[ANY] * ((len(unique) + len(rights)) * micro_count + 2),
+        in_specs=[ANY] * ((len(unique) + len(rights)) * micro_count + len(ready) + 1),
         out_specs=[ANY] * (len(lefts) + 1),
         scratch_shapes=[pltpu.VMEM((micro_count, *u[0].shape), bf16) for u in unique]
         + [
@@ -839,7 +850,7 @@
             collective_id=collective_id, has_side_effects=True, vmem_limit_bytes=62 << 20
         ),
         cost_estimate=pl.CostEstimate(flops=flops, bytes_accessed=100 << 20, transcendentals=0),
-    )(*[x for u in unique for x in u], *[x for r in rights for x in r], ready, small)
+    )(*[x for u in unique for x in u], *[x for r in rights for x in r], *ready, small)
 
 
 def weight_grad_body(n, *refs):
@@ -850,13 +861,14 @@
     out_ref[...] = total.astype(out_ref.dtype)
 
 
-def weight_grad(lefts, rights, row_tile, width=None):
+def weight_grad(lefts, rights, row_tile, width=None, part=0):
     n, (rows, height), width = len(lefts), lefts[0].shape, width or rights[0].shape[1]
     return pl.pallas_call(
         functools.partial(weight_grad_body, n),
         grid=(height // row_tile,),
         out_shape=jax.ShapeDtypeStruct((height, width), bf16),
-        in_specs=[pl.BlockSpec((rows, row_tile), lambda i: (0, i))] * n + [whole((rows, width))] * n,
+        in_specs=[pl.BlockSpec((rows, row_tile), lambda i: (0, i))] * n
+        + [pl.BlockSpec((rows, width), lambda i: (0, part), pipeline_mode=pl.Buffered(1))] * n,
         out_specs=pl.BlockSpec((row_tile, width), lambda i: (i, 0)),
         compiler_params=params(),
         cost_estimate=pl.CostEstimate(
@@ -1334,9 +1346,13 @@
     state_out, product, branch_grad, expanded_grad, gate_grad, _, full_grad, error_rows, lane_grad = zip(*middle)
     grads_in = [send_lanes(x) for x in lane_grad]
     back, kernel_grads = zip(*[convolve_back(lanes_in[m], grads_in[m]) for m in micros])
-    ready = weight_grad(normed, gate_grad, 256, gate_width // 2)
-    held_back, ready = lax.optimization_barrier((back[0], ready))
-    back = [receive_lanes(x) for x in (held_back, *back[1:])]
+    ready, held_back = [], []
+    for m in micros:
+        part = weight_grad(normed, gate_grad, 256, gate_width // micro_count, m)
+        held, part = lax.optimization_barrier((back[m], part))
+        held_back.append(held)
+        ready.append(part)
+    back = [receive_lanes(x) for x in held_back]
     ends = []
     for m in micros:
         ends.append(input_rows(m, back[m], gate_grad[m], full_grad[m], *[x[0] for x in ends[-1:]]))

time: 579 us -> 577 us (level)
  waiting for transfers between devices: 24.3 us -> 12.8 us
  starting transfers between devices: 34.9 us -> 44.3 us
    all_to_all x8, waiting for transfers between devices: 24.2 us -> 12.8 us  [exchange(): return lax.all_to_all(values, 'dp', split_axis=0, concat_axis=0, tiled=True)]
    pallas_call x1 -> x2, Pallas kernels: 11.4 us -> 22.9 us  [weight_grad(): pl.pallas_call(functools.partial(weight_grad_body, n), grid=(height // ro...]
    pallas_call x2, Pallas kernels: 174 us -> 163 us  [gather_all(): pl.pallas_call(functools.partial(gather_body, dp_count, bits, n, leads, o...]
    all_to_all x8, starting transfers between devices: 34.8 us -> 44.3 us  [exchange(): return lax.all_to_all(values, 'dp', split_axis=0, concat_axis=0, tiled=True)]
  transfers between devices with their start and end apart: 9 -> 9, of which waited for: 4 -> 4; matrix products, arithmetic and copies ran while one was open for 6% -> 6% of each run, Pallas kernels for 56% -> 58%
where the time goes in v6:
time: 577 us; the launch traced here: 572 us
  Pallas kernels  422 us (73%)
  starting transfers between devices  44.3 us (8%)
  other arithmetic  27.1 us (5%)
  blocking collectives  21.6 us (4%)
  local copies, waits for them, and re-layouts  19.9 us (3%)
  between operations  17.2 us (3%)
  waiting for transfers between devices  12.8 us (2%)
  matrix products  7.4 us (1%)
    pallas_call x2, Pallas kernels, gather_all(): pl.pallas_call(functools.partial(gather_body, dp_count, bits, n, leads, o...  163 us
    pallas_call x1, Pallas kernels, product_scatter(): pl.pallas_call(functools.partial(product_scatter_body, dp_count, bits, pl...  92.9 us
    pallas_call x2, Pallas kernels, middle_rows(): pl.pallas_call(functools.partial(middle_body, dims(middle_block), middle_...  64.5 us
    all_to_all x8, starting transfers between devices, exchange(): return lax.all_to_all(values, 'dp', split_axis=0, concat_axis=0, tiled=True)  44.3 us
    pallas_call x2, Pallas kernels, input_rows(): pl.pallas_call(functools.partial(input_body, dims(middle_block)), grid=(m...  32.1 us
    pallas_call x2, Pallas kernels, weight_grad(): pl.pallas_call(functools.partial(weight_grad_body, n), grid=(height // ro...  22.9 us
    all_gather x1, blocking collectives, shards(): kernel = lax.all_gather(own_kernel, 'fsdp', axis=0, tiled=True)  21.6 us
    pallas_call x2, Pallas kernels, convolve_back(): pl.pallas_call(convolve_back_body, out_shape=[jax.ShapeDtypeStruct(blocks...  19.9 us
  transfers between devices with their start and end apart: 9, of which 4 were waited for; matrix products, arithmetic and copies ran while one was open for 6% of the time, Pallas kernels for 58%

profile of v6, /device:TPU:0, one launch (start us, length us, event | category | flops | bytes accessed | tf_op | source)
XLA Modules:
  0.0 572.0 jit_solution(11704059972720095816)
XLA Ops:
  9.8 70.0 %shard_map.300 = (bf16[4,8,32,3072]{3,2,1,0:T(8,128)(2,1)}, bf16[4,8,32,512]{3,2,1,0:T(8,128)(2,1)}, bf16[4,8,16,256]{3,2,1,0:T(8,128)(2,1)}, s32[4,8,256]{2,1,0:T(8,128)}, bf16[4,256,1024]{2,1,0:T(8,128)(2,1)}) custom-call(bf16[32,3072]{1,0:T(8,128)(2,1)} %refs_0_.1, bf16[32,512]{1,0:T(8,128)(2,1)} %refs_1_.1, bf16[16,256]{1,0:T(8,128)(2,1)} %fusion.28.refs_2_, ...), custom_call_target="tpu_custom_call" | custom-call | bytes 152043520 | tf_op jit(solution)/shard_map/pallas_call | solution.py:168
  82.2 5.8 %shard_map.301 = (bf16[1024,1024]{1,0:T(8,128)(2,1)}, bf16[4,256,512]{2,1,0:T(8,128)(2,1)}, f32[1024,512]{1,0:T(8,128)}) custom-call(bf16[2,4,256,1024]{3,2,1,0:T(8,128)(2,1)} %tokens_ref.11, f32[1,1024]{1,0:T(1,128)} %reshape.189.gain_ref, f32[1,1024]{1,0:T(1,128)} %reshape.190.bias_ref, bf16[1024,512]{1,0:T(8,128)(2,1)} %bitcast.77), custom_call_target="tpu_custom_call" | custom-call | flops 1073741824 | bytes 8388608 | tf_op jit(solution)/shard_map/pallas_call | solution.py:1144
  88.0 13.1 %all-to-all-start = ((bf16[4,256,512]{2,1,0:T(8,128)(2,1)}), bf16[4,256,512]{2,1,0:T(8,128)(2,1)S(1)}, u32[]{:S(2)}, u32[]{:S(2)}) async-start(bf16[4,256,512]{2,1,0:T(8,128)(2,1)} %get-tuple-element.84), calls=%async_computation | async-start | bytes 2097152 | tf_op jit(solution)/shard_map/all_to_all | solution.py:333
  107.2 8.8 %multiply_subtract_fusion = (f32[16,32,512]{2,1,0:T(8,128)S(1)}, f32[16,32,512]{2,1,0:T(8,128)S(1)}, f32[16,32,512]{2,1,0:T(8,128)S(1)}, f32[16,32,512]{2,1,0:T(...) fusion(f32[16,512]{1,0:T(8,128)S(1)} %get-tuple-element.172, f32[16,512]{1,0:T(8,128)S(1)} %get-tuple-element.171, ...), kind=kLoop, calls=%fused_computation.35 | loop fusion | flops 3932160 | bytes 6422784 | tf_op jit(solution)/shard_map/sub | solution.py:1021
  119.2 5.7 shard_map.303
  126.1 4.2 all-to-all-start.1
  130.3 21.6 %all_gather.3 = f32[128,1024]{1,0:T(8,128)S(1)} all-gather(f32[16,1024]{1,0:T(8,128)S(1)} %reshape.176), channel_id=1, replica_groups=mesh['dp'=4,'fsdp'=8] {'fsdp'}, dimensions={0}, use_global_device_ids=true | all-gather | bytes 589824 | tf_op jit(solution)/shard_map/all_gather | solution.py:1194
  152.2 1.7 convolution_bitcast_fusion
  155.0 7.3 %shard_map.302 = bf16[4,256,512]{2,1,0:T(8,128)(2,1)} custom-call(bf16[2,512,256]{2,1,0:T(8,128)(2,1)} %constant.60.clone.table_ref, bf16[2,512,256]{2,1,0:T(8,128)(2,1)} %constant.61.clone.inverse_ref, f32[4,512,128]{2,1,0:T(8,128)} %multiply_add_fusion.kernel_ref, bf16[4,256,512]{2,1,0:T(8,128)(2,1)} %copy-done.1), custom_call_target="tpu_custom_call" | custom-call | flops 2684354560 | bytes 8388608 | tf_op jit(solution)/shard_map/pallas_call | solution.py:1207
  162.3 5.2 all-to-all-start.3
  168.2 7.2 %shard_map.304 = bf16[4,256,512]{2,1,0:T(8,128)(2,1)} custom-call(bf16[2,512,256]{2,1,0:T(8,128)(2,1)} %constant.60.clone.table_ref, bf16[2,512,256]{2,1,0:T(8,128)(2,1)} %constant.61.clone.inverse_ref, f32[4,512,128]{2,1,0:T(8,128)} %multiply_add_fusion.kernel_ref, bf16[4,256,512]{2,1,0:T(8,128)(2,1)} %all-to-all-done.1.rows_ref), custom_call_target="tpu_custom_call" | custom-call | flops 2684354560 | bytes 8388608 | tf_op jit(solution)/shard_map/pallas_call | solution.py:1207
  175.4 93.3 %shard_map.305 = (bf16[4,8,16,3072]{3,2,1,0:T(8,128)(2,1)}, bf16[4,8,96,1024]{3,2,1,0:T(8,128)(2,1)}, f32[4,8,8,256]{3,2,1,0:T(8,128)}, bf16[4,256,1024]{2,1,0:T...) custom-call(bf16[16,3072]{1,0:T(8,128)(2,1)} %refs_0_.2, bf16[96,1024]{1,0:T(8,128)(2,1)} %refs_1_.2, ...), custom_call_target="tpu_custom_call" | custom-call | bytes 193986560 | tf_op jit(solution)/shard_map/pallas_call | solution.py:168
  268.7 1.5 slice_reduce_fusion
  271.0 3.5 all-to-all-start.2
  274.5 32.2 %shard_map.306 = (bf16[1024,512]{1,0:T(8,128)(2,1)}, bf16[1024,3072]{1,0:T(8,128)(2,1)}, bf16[1024,1024]{1,0:T(8,128)(2,1)}, bf16[1024,3072]{1,0:T(8,128)(2,1)},...) custom-call(s32[4]{0:T(128)} %get-tuple-element.156.order_ref, ...), custom_call_target="tpu_custom_call" | custom-call | flops 19327352832 | bytes 48234496 | tf_op jit(solution)/shard_map/pallas_call | solution.py:1253
  306.8 5.0 all-to-all-start.4
  311.8 32.2 %shard_map.307 = (bf16[1024,512]{1,0:T(8,128)(2,1)}, bf16[1024,3072]{1,0:T(8,128)(2,1)}, bf16[1024,1024]{1,0:T(8,128)(2,1)}, bf16[1024,3072]{1,0:T(8,128)(2,1)},...) custom-call(s32[4]{0:T(128)} %get-tuple-element.157.order_ref, ...), custom_call_target="tpu_custom_call", output_to_operand_aliasing={{5}: (11, {})} | custom-call | flops 19327352832 | bytes 48234496 | tf_op jit(solution)/shard_map/pallas_call | solution.py:1253
  344.1 5.3 all-to-all-start.6
  349.3 11.4 %shard_map.309 = bf16[1024,1536]{1,0:T(8,128)(2,1)} custom-call(bf16[1024,1024]{1,0:T(8,128)(2,1)} %get-tuple-element.96.refs_4_.refs_0_, bf16[1024,1024]{1,0:T(8,128)(2,1)} %get-tuple-element.97.refs_5_.refs_1_, bf16[1024,3072]{1,0:T(8,128)(2,1)} %get-tuple-element.114.refs_2_.gate_grad_ref.refs_6_, ...), custom_call_target="tpu_custom_call" | custom-call | flops 6442450944 | bytes 13631488 | tf_op jit(solution)/shard_map/pallas_call | solution.py:866
  360.8 9.9 %shard_map.308 = (bf16[4,256,512]{2,1,0:T(8,128)(2,1)}, f32[4,512,128]{2,1,0:T(8,128)}) custom-call(bf16[2,512,256]{2,1,0:T(8,128)(2,1)} %constant.60.clone.table_ref, bf16[2,512,256]{2,1,0:T(8,128)(2,1)} %constant.61.clone.inverse_ref, f32[4,512,128]{2,1,0:T(8,128)} %multiply_add_fusion.kernel_ref, bf16[4,256,512]{2,1,0:T(8,128)(2,1)} %copy-done.1, ...), custom_call_target="tpu_custom_call" | custom-call | flops 3758096384 | bytes 8388608 | tf_op jit(solution)/shard_map/pallas_call | solution.py:1218
  370.7 3.0 all-to-all-done.6.grad_ref
  374.6 3.7 all-to-all-start.5
  378.3 11.4 %shard_map.312 = bf16[1024,1536]{1,0:T(8,128)(2,1)} custom-call(bf16[1024,1024]{1,0:T(8,128)(2,1)} %get-tuple-element.96.refs_4_.refs_0_, bf16[1024,1024]{1,0:T(8,128)(2,1)} %get-tuple-element.97.refs_5_.refs_1_, bf16[1024,3072]{1,0:T(8,128)(2,1)} %get-tuple-element.114.refs_2_.gate_grad_ref.refs_6_, ...), custom_call_target="tpu_custom_call" | custom-call | flops 6442450944 | bytes 13631488 | tf_op jit(solution)/shard_map/pallas_call | solution.py:866
  389.8 10.0 %shard_map.311 = (bf16[4,256,512]{2,1,0:T(8,128)(2,1)}, f32[4,512,128]{2,1,0:T(8,128)}) custom-call(bf16[2,512,256]{2,1,0:T(8,128)(2,1)} %constant.60.clone.table_ref, bf16[2,512,256]{2,1,0:T(8,128)(2,1)} %constant.61.clone.inverse_ref, f32[4,512,128]{2,1,0:T(8,128)} %multiply_add_fusion.kernel_ref, bf16[4,256,512]{2,1,0:T(8,128)(2,1)} %all-to-all-done.1.rows_ref, ...), custom_call_target="tpu_custom_call" | custom-call | flops 3758096384 | bytes 8388608 | tf_op jit(solution)/shard_map/pallas_call | solution.py:1218
  399.8 3.7 all-to-all-done.5.back_ref
  403.5 4.3 all-to-all-start.7
  411.9 16.3 %shard_map.310 = (bf16[2,4,256,1024]{3,2,1,0:T(8,128)(2,1)}, bf16[1024,512]{1,0:T(8,128)(2,1)}, f32[4,8,1024]{2,1,0:T(8,128)}, f32[4,8,1024]{2,1,0:T(8,128)}) custom-call(bf16[4,256,512]{2,1,0:T(8,128)(2,1)} %copy-done.2, f32[1024,512]{1,0:T(8,128)} %get-tuple-element.123.slope_ref, bf16[1024,3072]{1,0:T(8,128)(2,1)} %get-tuple-element.114.refs_2_.gate_grad_ref.refs_6_, ...), custom_call_target="tpu_custom_call" | custom-call | flops 7516192768 | bytes 20971520 | tf_op jit(solution)/shard_map/pallas_call | solution.py:1311
  428.2 4.9 all-to-all-done.7.back_ref
  433.1 15.9 %shard_map.313 = (bf16[2,4,256,1024]{3,2,1,0:T(8,128)(2,1)}, bf16[1024,512]{1,0:T(8,128)(2,1)}, f32[4,8,1024]{2,1,0:T(8,128)}, f32[4,8,1024]{2,1,0:T(8,128)}) custom-call(bf16[4,256,512]{2,1,0:T(8,128)(2,1)} %all-to-all-done.7.back_ref, f32[1024,512]{1,0:T(8,128)} %get-tuple-element.129.slope_ref, ...), custom_call_target="tpu_custom_call", output_to_operand_aliasing={{0}: (8, {})} | custom-call | flops 7516192768 | bytes 20971520 | tf_op jit(solution)/shard_map/pallas_call | solution.py:1311
  452.8 92.9 %shard_map.314 = (f32[32,3072]{1,0:T(8,128)}, f32[16,3072]{1,0:T(8,128)}, f32[96,1024]{1,0:T(8,128)}, f32[32,512]{1,0:T(8,128)}, f32[8,128]{1,0:T(8,128)}) custom-call(bf16[1024,1024]{1,0:T(8,128)(2,1)} %get-tuple-element.96.refs_4_.refs_0_, bf16[1024,1024]{1,0:T(8,128)(2,1)} %get-tuple-element.97.refs_5_.refs_1_, ...), custom_call_target="tpu_custom_call" | custom-call | flops 34359738368 | bytes 104857600 | tf_op jit(solution)/shard_map/pallas_call | solution.py:830
  550.4 3.5 fusion.7
  554.0 5.1 subtract_reduce_fusion
  (127 shorter events, 35.1 us)
Async XLA Ops:
  82.2 19.0 %copy-start.21 = (s32[2,32]{1,0:T(2,128)S(1)}, s32[2,32]{1,0:T(2,128)}, u32[]{:S(2)}) copy-start(s32[2,32]{1,0:T(2,128)} %param.27) | copy-start | bytes 772
  82.2 21.3 %copy-start.22 = (s32[2,32]{1,0:T(2,128)S(1)}, s32[2,32]{1,0:T(2,128)}, u32[]{:S(2)}) copy-start(s32[2,32]{1,0:T(2,128)} %param.26) | copy-start | bytes 772
  82.2 24.4 %copy-start.24 = (f32[16]{0:T(128)S(1)}, f32[16]{0:T(128)}, u32[]{:S(2)}) copy-start(f32[16]{0:T(128)} %param.36) | copy-start | bytes 196
  82.2 24.9 %copy-start.9 = (f32[2,16,512]{2,1,0:T(8,128)S(1)}, f32[2,16,512]{2,1,0:T(8,128)}, u32[]{:S(2)}) copy-start(f32[2,16,512]{2,1,0:T(8,128)} %param.33) | copy-start | bytes 196612
  82.2 25.0 %copy-start.15 = (f32[16,512]{1,0:T(8,128)S(1)}, f32[16,512]{1,0:T(8,128)}, u32[]{:S(2)}) copy-start(f32[16,512]{1,0:T(8,128)} %param.34) | copy-start | bytes 98308
  82.2 24.9 %copy-start.17 = (f32[16,512]{1,0:T(8,128)S(1)}, f32[16,512]{1,0:T(8,128)}, u32[]{:S(2)}) copy-start(f32[16,512]{1,0:T(8,128)} %param.35) | copy-start | bytes 98308
  88.0 38.1 %all-to-all-start = ((bf16[4,256,512]{2,1,0:T(8,128)(2,1)}), bf16[4,256,512]{2,1,0:T(8,128)(2,1)S(1)}, u32[]{:S(2)}, u32[]{:S(2)}) async-start(bf16[4,256,512]{2,1,0:T(8,128)(2,1)} %get-tuple-element.84), calls=%async_computation | async-start | bytes 2097152 | tf_op jit(solution)/shard_map/all_to_all | solution.py:333
  126.1 27.8 %copy-start.1 = (bf16[4,256,512]{2,1,0:T(8,128)(2,1)}, bf16[4,256,512]{2,1,0:T(8,128)(2,1)S(1)}, u32[]{:S(2)}) copy-start(bf16[4,256,512]{2,1,0:T(8,128)(2,1)S(1)} %all-to-all-done.rows_ref) | copy-start | bytes 3145732
  126.1 36.2 %all-to-all-start.1 = ((bf16[4,256,512]{2,1,0:T(8,128)(2,1)}), bf16[4,256,512]{2,1,0:T(8,128)(2,1)}, u32[]{:S(2)}, u32[]{:S(2)}) async-start(bf16[4,256,512]{2,1,0:T(8,128)(2,1)} %get-tuple-element.92), calls=%async_computation.1 | async-start | bytes 2097152 | tf_op jit(solution)/shard_map/all_to_all | solution.py:333
  130.3 23.6 %copy-start.20 = (f32[512]{0:T(512)S(1)}, f32[512]{0:T(512)}, u32[]{:S(2)}) copy-start(f32[512]{0:T(512)} %constant.59.clone) | copy-start | bytes 6148
  162.3 108.6 %all-to-all-start.3 = ((bf16[4,256,512]{2,1,0:T(8,128)(2,1)}), bf16[4,256,512]{2,1,0:T(8,128)(2,1)}, u32[]{:S(2)}, u32[]{:S(2)}) async-start(bf16[4,256,512]{2,1,0:T(8,128)(2,1)} %shard_map.302), calls=%async_computation.3 | async-start | bytes 2097152 | tf_op jit(solution)/shard_map/all_to_all | solution.py:333
  271.0 35.8 %all-to-all-start.2 = ((bf16[4,256,512]{2,1,0:T(8,128)(2,1)}), bf16[4,256,512]{2,1,0:T(8,128)(2,1)S(1)}, u32[]{:S(2)}, u32[]{:S(2)}) async-start(bf16[4,256,512]{2,1,0:T(8,128)(2,1)} %shard_map.304), calls=%async_computation.2 | async-start | bytes 2097152 | tf_op jit(solution)/shard_map/all_to_all | solution.py:333
  306.8 5.1 copy-start.3
  306.8 37.3 %all-to-all-start.4 = ((bf16[4,256,512]{2,1,0:T(8,128)(2,1)}), bf16[4,256,512]{2,1,0:T(8,128)(2,1)S(1)}, u32[]{:S(2)}, u32[]{:S(2)}) async-start(bf16[4,256,512]{2,1,0:T(8,128)(2,1)} %get-tuple-element.120), calls=%async_computation.4 | async-start | bytes 2097152 | tf_op jit(solution)/shard_map/all_to_all | solution.py:333
  344.1 16.7 %copy-start.4 = (bf16[4,256,512]{2,1,0:T(8,128)(2,1)}, bf16[4,256,512]{2,1,0:T(8,128)(2,1)S(1)}, u32[]{:S(2)}) copy-start(bf16[4,256,512]{2,1,0:T(8,128)(2,1)S(1)} %all-to-all-done.4.grad_ref) | copy-start | bytes 3145732
  344.1 29.6 %all-to-all-start.6 = ((bf16[4,256,512]{2,1,0:T(8,128)(2,1)}), bf16[4,256,512]{2,1,0:T(8,128)(2,1)S(1)}, u32[]{:S(2)}, u32[]{:S(2)}) async-start(bf16[4,256,512]{2,1,0:T(8,128)(2,1)} %get-tuple-element.126), calls=%async_computation.6 | async-start | bytes 2097152 | tf_op jit(solution)/shard_map/all_to_all | solution.py:333
  374.6 28.9 %all-to-all-start.5 = ((bf16[4,256,512]{2,1,0:T(8,128)(2,1)}), bf16[4,256,512]{2,1,0:T(8,128)(2,1)S(1)}, u32[]{:S(2)}, u32[]{:S(2)}) async-start(bf16[4,256,512]{2,1,0:T(8,128)(2,1)} %get-tuple-element.122), calls=%async_computation.5 | async-start | bytes 2097152 | tf_op jit(solution)/shard_map/all_to_all | solution.py:333
  389.8 18.1 %copy-start.11 = (f32[4,8,1024]{2,1,0:T(8,128)S(1)}, f32[4,8,1024]{2,1,0:T(8,128)}, u32[]{:S(2)}) copy-start(f32[4,8,1024]{2,1,0:T(8,128)} %get-tuple-element.139) | copy-start | bytes 393220
  389.8 18.1 %copy-start.12 = (f32[4,8,1024]{2,1,0:T(8,128)S(1)}, f32[4,8,1024]{2,1,0:T(8,128)}, u32[]{:S(2)}) copy-start(f32[4,8,1024]{2,1,0:T(8,128)} %get-tuple-element.140) | copy-start | bytes 393220
  389.8 19.4 %copy-start = (f32[4,512,128]{2,1,0:T(8,128)S(1)}, f32[4,512,128]{2,1,0:T(8,128)}, u32[]{:S(2)}) copy-start(f32[4,512,128]{2,1,0:T(8,128)} %get-tuple-element.145) | copy-start | bytes 3145732
  403.5 7.1 %copy-start.2 = (bf16[4,256,512]{2,1,0:T(8,128)(2,1)}, bf16[4,256,512]{2,1,0:T(8,128)(2,1)S(1)}, u32[]{:S(2)}) copy-start(bf16[4,256,512]{2,1,0:T(8,128)(2,1)S(1)} %all-to-all-done.5.back_ref) | copy-start | bytes 3145732
  403.5 29.5 %all-to-all-start.7 = ((bf16[4,256,512]{2,1,0:T(8,128)(2,1)}), bf16[4,256,512]{2,1,0:T(8,128)(2,1)}, u32[]{:S(2)}, u32[]{:S(2)}) async-start(bf16[4,256,512]{2,1,0:T(8,128)(2,1)} %get-tuple-element.128), calls=%async_computation.7 | async-start | bytes 2097152 | tf_op jit(solution)/shard_map/all_to_all | solution.py:333
  407.8 141.1 %reduce-scatter.4.cloned.1.call-start = ((), (), s32[]{:S(2)}) async-start(), calls=%async_computation.9 | async-start | bytes 589824
  433.1 16.9 %copy-start.14 = (f32[4,8,1024]{2,1,0:T(8,128)S(1)}, f32[4,8,1024]{2,1,0:T(8,128)}, u32[]{:S(2)}) copy-start(f32[4,8,1024]{2,1,0:T(8,128)} %get-tuple-element.135) | copy-start | bytes 393220
  433.1 17.9 %copy-start.13 = (f32[4,8,1024]{2,1,0:T(8,128)S(1)}, f32[4,8,1024]{2,1,0:T(8,128)}, u32[]{:S(2)}) copy-start(f32[4,8,1024]{2,1,0:T(8,128)} %get-tuple-element.137) | copy-start | bytes 393220
  553.9 5.8 %copy-start.16 = (f32[16,512]{1,0:T(8,128)S(1)}, f32[16,512]{1,0:T(8,128)}, u32[]{:S(2)}) copy-start(f32[16,512]{1,0:T(8,128)} %param.34) | copy-start | bytes 98308
  553.9 5.8 %copy-start.18 = (f32[16,512]{1,0:T(8,128)S(1)}, f32[16,512]{1,0:T(8,128)}, u32[]{:S(2)}) copy-start(f32[16,512]{1,0:T(8,128)} %param.35) | copy-start | bytes 98308
  553.9 5.8 %copy-start.23 = (f32[16]{0:T(128)S(1)}, f32[16]{0:T(128)}, u32[]{:S(2)}) copy-start(f32[16]{0:T(128)} %get-tuple-element.177) | copy-start | bytes 196
  553.9 7.1 %copy-start.8 = (f32[32,3072]{1,0:T(8,128)S(1)}, f32[32,3072]{1,0:T(8,128)}, u32[]{:S(2)}) copy-start(f32[32,3072]{1,0:T(8,128)} %get-tuple-element.201) | copy-start | bytes 1179652
  554.0 7.8 %copy-start.19 = (f32[32,512]{1,0:T(8,128)S(1)}, f32[32,512]{1,0:T(8,128)}, u32[]{:S(2)}) copy-start(f32[32,512]{1,0:T(8,128)} %get-tuple-element.202) | copy-start | bytes 196612
  554.0 8.5 %copy-start.10 = (f32[16,3072]{1,0:T(8,128)S(1)}, f32[16,3072]{1,0:T(8,128)}, u32[]{:S(2)}) copy-start(f32[16,3072]{1,0:T(8,128)} %get-tuple-element.207) | copy-start | bytes 589828
  554.0 9.1 %copy-start.7 = (f32[96,1024]{1,0:T(8,128)S(1)}, f32[96,1024]{1,0:T(8,128)}, u32[]{:S(2)}) copy-start(f32[96,1024]{1,0:T(8,128)} %get-tuple-element.208) | copy-start | bytes 1179652
  (2 other events, 3.8 us)
Sparse Core Ops, SparseCore 0:
  450.1 35.5 reduce-scatter.3
